TPU v7x, 32 devices: a whole 2x2x4 slice. The times are simulated.
32 devices in a mesh: dp: 2 (over core), context: 4 (over y, x), tensor: 4 (over z).
Axes of the slice: x: 2, y: 2, z: 4, core: 2. Of those that a mesh axis runs over, the one named last changes fastest.
Arguments:
- ids: int32 [4096], P(('dp', 'context', 'tensor')), parts along dimension 0, may hold values from 65 to 84, as said below
- block_order: int32 [16], P('dp'), parts along dimension 0, may hold values from 0 to 7, each once
- embed: bfloat16 [512, 4096], replicated, may hold values from -6 to 6
- mix_gain: float32 [4096], replicated, may hold values from 0.5 to 2
- in_proj: bfloat16 [3, 4096, 2048], P(None, None, 'tensor'), may hold values from -0.09375 to 0.09375
- short_filter: float32 [3, 3, 2048], P(None, None, 'tensor'), may hold values from -1 to 1
- long_filter: float32 [128, 128], P('tensor'), as said below
- conv_skip: float32 [2048], P('tensor'), may hold values from -1 to 1
- hyena_out: bfloat16 [2048, 4096], P('tensor'), may hold values from -0.125 to 0.125
- attn_gain: float32 [4096], replicated, may hold values from 0.5 to 2
- qkv_proj: bfloat16 [3, 4096, 2048], P(None, None, 'tensor'), as said below
- attn_out: bfloat16 [2048, 4096], P('tensor'), may hold values from -0.5 to 0.5
Outputs:
- stream_out: float32 [4096, 4096], P(('dp', 'context', 'tensor')), parts along dimension 0
There are 2 independent parts, one for each index of `dp`. A program takes and returns all parts, laid end to end along the dimension named above; an argument that names none is the same for every part. Nothing has to cross between parts.
Inputs may be any that keep to these rules, and one draw needn't show every extreme that they name: `ids`: every id is the code of a base: 65, 67, 71 or 84. `block_order`: every block lies in exactly one slot. `long_filter`: real-valued filter taps. `qkv_proj`: real-valued projection weights.
All inputs are finite; a program needn't handle non-finite values.
Results may differ from a plain program's by a relative error of at most 0.01.
Values may be sent and summed in bfloat16 or wider, within the bound.
No kernel may reach another device: no remote copies, remote signals or barrier semaphores. Data moves between devices by JAX's collectives and lax.ppermute only.
A program may use at most 192 MiB of HBM per device.

v0:
```python
import math

import jax
import jax.numpy as jnp
from jax import lax
from jax.sharding import PartitionSpec as P

HD = 128
GROUP_CH = 16


EPS = 1e-06
THETA = 1000000.0
NEG_FILL = -1e30


def rms_scale(row_data, gain_vec):
    values = row_data.astype(jnp.float32)
    factor = lax.rsqrt(jnp.mean(values * values, axis=-1, keepdims=True) + EPS)
    return (values * factor * gain_vec).astype(jnp.bfloat16)


def toeplitz(long_filter):
    filter_len = long_filter.shape[1]
    tap_lag = (
        jnp.arange(filter_len, dtype=jnp.int32)[:, None]
        - jnp.arange(filter_len, dtype=jnp.int32)[None, :]
    )
    near_taps = jnp.take(long_filter, jnp.clip(tap_lag, 0, filter_len - 1), axis=1)
    far_taps = jnp.take(long_filter, jnp.clip(tap_lag + filter_len, 0, filter_len - 1), axis=1)
    near_taps = jnp.where(tap_lag[None] >= 0, near_taps, jnp.zeros_like(near_taps))
    far_taps = jnp.where(tap_lag[None] < 0, far_taps, jnp.zeros_like(far_taps))
    return (near_taps, far_taps)


def long_conv(padded, long_filter, group_width):
    filter_len = long_filter.shape[1]
    near_taps, far_taps = toeplitz(long_filter)
    row_total = padded.shape[0]
    chan_total = padded.shape[1]
    blocks = padded.reshape(
        row_total // filter_len, filter_len, chan_total // group_width, group_width
    )
    current_part = jnp.einsum(
        "grs,bsgc->brgc", near_taps, blocks[1:], precision=lax.Precision.HIGHEST
    )
    before = jnp.einsum("grs,bsgc->brgc", far_taps, blocks[:-1], precision=lax.Precision.HIGHEST)
    return (current_part + before).reshape(row_total - filter_len, chan_total)


def short_conv(padded_rows, short_filter, out_len):
    taps = short_filter.shape[1]
    result = jnp.zeros((padded_rows.shape[0], out_len, padded_rows.shape[2]), jnp.float32)
    for tap_at in range(taps):
        offset = taps - 1 - tap_at
        result = (
            result + short_filter[:, tap_at][:, None, :] * padded_rows[:, offset : offset + out_len]
        )
    return result


def rotate(values, positions, head_dim):
    half_dim = head_dim // 2
    inverse_freq = THETA ** (-(2.0 * jnp.arange(half_dim, dtype=jnp.float32)) / head_dim)
    angles = positions.astype(jnp.float32)[:, None] * inverse_freq[None, :]
    cosine_part = jnp.cos(angles)[:, None, :]
    sine_part = jnp.sin(angles)[:, None, :]
    lower_half = values[..., :half_dim]
    upper_half = values[..., half_dim:]
    return jnp.concatenate(
        [
            lower_half * cosine_part - upper_half * sine_part,
            upper_half * cosine_part + lower_half * sine_part,
        ],
        axis=-1,
    )


def body(
    ids,
    block_order,
    embed,
    mix_gain,
    in_proj,
    short_filter,
    long_filter,
    conv_skip,
    hyena_out,
    attn_gain,
    qkv_proj,
    attn_out,
):
    tok_rows = ids.shape[0]
    tensor_count = lax.axis_size("tensor")
    context_count = lax.axis_size("context")
    ctx_rows = tok_rows * tensor_count
    block_rows = ctx_rows // 2
    filter_len = long_filter.shape[1]
    short_len = short_filter.shape[1]
    halo_len = filter_len + short_len - 2
    chan_local = in_proj.shape[2]
    context_at = lax.axis_index("context")
    vocab_ids = jnp.arange(embed.shape[0], dtype=jnp.int32)
    chosen = (ids[:, None] == vocab_ids[None, :]).astype(jnp.bfloat16)
    embedded = jnp.dot(chosen, embed, preferred_element_type=jnp.float32).astype(jnp.bfloat16)
    embedded_all = lax.all_gather(embedded, "tensor", axis=0, tiled=True)
    mixed_in = rms_scale(embedded_all, mix_gain)
    projected = jnp.einsum(
        "rd,jdc->jrc", mixed_in, in_proj, preferred_element_type=jnp.float32
    ).astype(jnp.bfloat16)
    slot_ids = jnp.arange(2 * context_count, dtype=jnp.int32)
    slot_pair = 2 * context_at + jnp.arange(2, dtype=jnp.int32)
    owned_blocks = jnp.sum(
        jnp.where(slot_ids[None, :] == slot_pair[:, None], block_order[None, :], 0), axis=1
    )
    local_pos = (
        owned_blocks[:, None] * block_rows + jnp.arange(block_rows, dtype=jnp.int32)[None, :]
    ).reshape(ctx_rows)
    tail_rows = jnp.stack(
        [projected[:, block_rows - halo_len : block_rows], projected[:, ctx_rows - halo_len :]]
    )
    all_tails = lax.all_gather(tail_rows, "context", axis=0, tiled=True)
    out_len = filter_len - 1 + block_rows
    pieces = []
    for block_at in range(2):
        holder_hit = (block_order == owned_blocks[block_at] - 1).astype(jnp.bfloat16)
        before_rows = jnp.einsum(
            "s,sjrc->jrc", holder_hit, all_tails, preferred_element_type=jnp.float32
        )
        own_rows = projected[:, block_at * block_rows : (block_at + 1) * block_rows].astype(
            jnp.float32
        )
        extended = jnp.concatenate([before_rows, own_rows], axis=1)
        filtered = short_conv(extended, short_filter, out_len)
        gated_rows = filtered[1] * filtered[2]
        padded = jnp.concatenate([jnp.zeros((1, chan_local), jnp.float32), gated_rows], axis=0)
        long_mix = long_conv(padded, long_filter, GROUP_CH)
        own_gate = gated_rows[filter_len - 1 :]
        pieces.append(
            (filtered[0, filter_len - 1 :] * (long_mix + conv_skip * own_gate)).astype(jnp.bfloat16)
        )
    hyena_mix = jnp.concatenate(pieces, axis=0)
    hyena_own = lax.psum_scatter(
        jnp.dot(hyena_mix, hyena_out, preferred_element_type=jnp.float32),
        "tensor",
        scatter_dimension=0,
        tiled=True,
    )
    stream_own = embedded.astype(jnp.float32) + hyena_own
    stream_all = lax.all_gather(stream_own, "tensor", axis=0, tiled=True)
    attn_in = rms_scale(stream_all, attn_gain)
    projections = jnp.einsum("rd,jdf->jrf", attn_in, qkv_proj, preferred_element_type=jnp.float32)
    local_heads = projections.shape[2] // HD
    shaped = projections.reshape(3, ctx_rows, local_heads, HD)
    queries = rotate(shaped[0], local_pos, HD).astype(jnp.bfloat16)
    keys_flat = (
        rotate(shaped[1], local_pos, HD).astype(jnp.bfloat16).reshape(ctx_rows, local_heads * HD)
    )
    values_flat = shaped[2].astype(jnp.bfloat16).reshape(ctx_rows, local_heads * HD)
    score_scale = HD ** (-0.5)
    start_state = (
        jnp.full((2, block_rows, local_heads), NEG_FILL, jnp.float32),
        jnp.zeros((2, block_rows, local_heads), jnp.float32),
        jnp.zeros((2, block_rows, local_heads, HD), jnp.float32),
    )
    key_piece = lax.all_gather(keys_flat, "context", axis=0, tiled=True)
    value_piece = lax.all_gather(values_flat, "context", axis=0, tiled=True)
    piece_len = key_piece.shape[0]
    sub_len = math.gcd(piece_len, 512)

    def attend_sub(sub_index, carried):
        key_block = lax.dynamic_slice_in_dim(key_piece, sub_index * sub_len, sub_len, 0).reshape(
            sub_len, local_heads, HD
        )
        value_block = lax.dynamic_slice_in_dim(
            value_piece, sub_index * sub_len, sub_len, 0
        ).reshape(sub_len, local_heads, HD)
        row_ids = sub_index * sub_len + jnp.arange(sub_len, dtype=jnp.int32)
        holder = row_ids // block_rows
        key_pos = (
            jnp.sum(
                jnp.where(holder[:, None] == slot_ids[None, :], block_order[None, :], 0), axis=1
            )
            * block_rows
            + row_ids % block_rows
        )
        top_all, sums_all, weighted_all = carried
        outputs = []
        for block_at in range(2):
            query_rows = queries[block_at * block_rows : (block_at + 1) * block_rows]
            query_pos = local_pos[block_at * block_rows : (block_at + 1) * block_rows]
            top_score = top_all[block_at]
            weight_sum = sums_all[block_at]
            weighted = weighted_all[block_at]
            scores = (
                jnp.einsum(
                    "qhd,khd->qhk", query_rows, key_block, preferred_element_type=jnp.float32
                )
                * score_scale
            )
            visible = key_pos[None, None, :] <= query_pos[:, None, None]
            scores = jnp.where(visible, scores, NEG_FILL)
            new_top = jnp.maximum(top_score, jnp.max(scores, axis=-1))
            rescale = jnp.exp(top_score - new_top)
            weights = jnp.where(visible, jnp.exp(scores - new_top[..., None]), 0.0)
            weight_sum = weight_sum * rescale + jnp.sum(weights, axis=-1)
            weighted = weighted * rescale[..., None] + jnp.einsum(
                "qhk,khd->qhd",
                weights.astype(jnp.bfloat16),
                value_block,
                preferred_element_type=jnp.float32,
            )
            result = (new_top, weight_sum, weighted)
            outputs.append(result)
        return tuple((jnp.stack([entry[field] for entry in outputs]) for field in range(3)))

    top_final, sums_final, weighted_final = lax.fori_loop(
        0, piece_len // sub_len, attend_sub, start_state
    )
    attended = (
        (weighted_final / sums_final[..., None])
        .astype(jnp.bfloat16)
        .reshape(ctx_rows, local_heads * HD)
    )
    attn_own = lax.psum_scatter(
        jnp.dot(attended, attn_out, preferred_element_type=jnp.float32).astype(jnp.bfloat16),
        "tensor",
        scatter_dimension=0,
        tiled=True,
    ).astype(jnp.float32)
    return stream_own + attn_own


def solution(mesh):
    placed = (
        P(("dp", "context", "tensor")),
        P("dp"),
        P(),
        P(),
        P(None, None, "tensor"),
        P(None, None, "tensor"),
        P("tensor", None),
        P("tensor"),
        P("tensor", None),
        P(),
        P(None, None, "tensor"),
        P("tensor", None),
    )
    return jax.shard_map(
        body,
        mesh=mesh,
        in_specs=placed,
        out_specs=P(("dp", "context", "tensor"), None),
        check_vma=False,
    )
```

profile of v0, /device:TPU:0, one launch (start us, length us, event | category | flops | bytes accessed | tf_op | source)
XLA Modules:
  0.0 799.1 jit_solution(8134422457217076364)
XLA Ops:
  6.5 3.9 convolution_convert_fusion.1
  10.5 83.6 %all-gather.7.cloned.1.call-done = bf16[512,4096]{1,0:T(8,128)(2,1)} async-done(((bf16[128,4096]{1,0:T(8,128)(2,1)}), bf16[512,4096]{1,0:T(8,128)(2,1)}) %all-gather.7.cloned.1.call-update) | async-done | bytes 4194320 | tf_op jit(solution)/shard_map/all_gather | solution.py:106
  94.1 3.2 fusion.38
  97.6 9.9 %fusion.83 = bf16[3,512,512]{2,1,0:T(8,128)(2,1)S(1)} fusion(bf16[3,4096,512]{2,1,0:T(8,128)(2,1)} %param.20, bf16[512,4096]{1,0:T(8,128)(2,1)S(1)} %copy-done.10, f32[4096]{0:T(1024)S(1)} %copy-done.18, f32[512]{0:T(512)S(1)} %add_rsqrt_fusion.1), kind=kOutput, calls=%fused_computation.128 | convolution fusion | flops 6451625984 | bytes 18368512 | tf_op jit(solution)/shard_map/rd,jdc->jrc/dot_general | solution.py:108
  112.2 54.8 %gather_fusion.1 = f32[16384,32]{1,0:T(8,128)} fusion(f32[32,128]{0,1:T(8,128)S(1)} %copy.81, s32[16384]{0:T(1024)S(1)} %bitcast_clamp_fusion), kind=kCustom, calls=%fused_computation.1.clone | custom fusion | bytes 4259840 | tf_op jit(solution)/shard_map/jit(_take)/gather | solution.py:30
  167.0 6.4 copy.86
  173.4 54.8 %gather_fusion = f32[16384,32]{1,0:T(8,128)} fusion(f32[32,128]{0,1:T(8,128)S(1)} %copy.81, s32[16384]{0:T(1024)S(1)} %bitcast_clamp_fusion.1), kind=kCustom, calls=%fused_computation.clone | custom fusion | bytes 4259840 | tf_op jit(solution)/shard_map/jit(_take)/gather | solution.py:29
  228.3 5.5 copy.82
  233.9 3.4 slice_convert_fusion.2
  237.4 3.4 fusion.51
  256.6 5.0 fusion.71
  261.6 3.4 fusion.89
  270.5 5.2 fusion.69
  280.7 4.6 fusion.95
  288.2 7.8 fusion.120
  296.1 143.2 %reduce-scatter.3.cloned.1.call-done = f32[128,4096]{1,0:T(8,128)} async-done(((f32[512,4096]{1,0:T(8,128)}), f32[128,4096]{1,0:T(8,128)}) %reduce-scatter.3.cloned.1.call-update) | async-done | bytes 2097168 | tf_op jit(solution)/shard_map/reduce_scatter | solution.py:143
  443.2 149.7 %all-gather.11.cloned.1.call-done = f32[512,4096]{1,0:T(8,128)} async-done(((f32[128,4096]{1,0:T(8,128)}), f32[512,4096]{1,0:T(8,128)}) %all-gather.11.cloned.1.call-update) | async-done | bytes 8388624 | tf_op jit(solution)/shard_map/all_gather | solution.py:150
  592.8 4.2 multiply_reduce_fusion
  598.6 11.4 %fusion.77 = f32[3,512,512]{1,2,0:T(8,128)} fusion(bf16[3,4096,512]{2,1,0:T(8,128)(2,1)} %param.26, f32[512,4096]{1,0:T(8,128)S(1)} %copy-done.5, f32[4096]{0:T(1024)S(1)} %copy-done.19, f32[512]{0:T(512)S(1)} %add_rsqrt_fusion), kind=kOutput, calls=%fused_computation.126 | convolution fusion | flops 6448742400 | bytes 24135680 | tf_op jit(solution)/shard_map/rd,jdf->jrf/dot_general | solution.py:152
  615.5 30.9 %all-gather.13.cloned.1.call-done = bf16[2048,512]{0,1:T(8,128)(2,1)} async-done(((bf16[512,512]{0,1:T(8,128)(2,1)}), bf16[2048,512]{0,1:T(8,128)(2,1)}) %all-gather.13.cloned.1.call-update) | async-done | bytes 2097168 | tf_op jit(solution)/shard_map/all_gather | solution.py:166
  646.3 36.8 %all-gather.15.cloned.1.call-done = bf16[1,2048,512]{1,2,0:T(8,128)(2,1)} async-done(((bf16[1,512,512]{1,2,0:T(8,128)(2,1)}), bf16[1,2048,512]{1,2,0:T(8,128)(2,1)}) %all-gather.15.cloned.1.call-update) | async-done | bytes 2097168 | tf_op jit(solution)/shard_map/all_gather | solution.py:167
  683.2 22.0 %while.20 = (s32[]{:T(128)}, f32[2,256,4]{1,2,0:T(4,128)S(1)}, f32[2,256,4]{1,2,0:T(4,128)S(1)}, f32[2,256,4,128]{1,3,2,0:T(8,128)S(1)}, s32[8]{0:T(128)S(1)}, /...) while((s32[]{:T(128)}, f32[2,256,4]{1,2,0:T(4,128)S(1)}, ...), condition=%wide.region_10.12_spmd.clone, body=%wide.region_4.11_spmd.clone.sunk | while | flops 551590400 | bytes 22718688 | solution.py:217
  705.6 6.5 convolution_convert_fusion
  712.1 77.0 %reduce-scatter.5.cloned.1.call-done = bf16[128,4096]{1,0:T(8,128)(2,1)} async-done(((bf16[512,4096]{1,0:T(8,128)(2,1)}), bf16[128,4096]{1,0:T(8,128)(2,1)}) %reduce-scatter.5.cloned.1.call-update) | async-done | bytes 1048592 | tf_op jit(solution)/shard_map/reduce_scatter | solution.py:225
  (183 shorter events, 68.4 us)
Async XLA Ops:
  6.5 87.6 %all-gather.7.cloned.1.call-start = ((), (), s32[]{:S(2)}) async-start(), calls=%async_computation.2 | async-start | bytes 5242880 | tf_op jit(solution)/shard_map/all_gather | solution.py:106
  10.5 86.9 %copy-start.18 = (f32[4096]{0:T(1024)S(1)}, f32[4096]{0:T(1024)}, u32[]{:S(2)}) copy-start(f32[4096]{0:T(1024)} %param.19) | copy-start | bytes 49156
  10.5 226.9 %all-gather.9.cloned.1.call-start = ((), (), s32[]{:S(2)}) async-start(), calls=%async_computation.3 | async-start | bytes 4177920 | tf_op jit(solution)/shard_map/all_gather | solution.py:122
  94.1 3.4 copy-start.10
  108.7 1.3 copy-start.14
  108.7 3.3 copy-start.16
  108.7 3.3 copy-start.15
  109.9 329.4 %reduce-scatter.3.cloned.1.call-start = ((), (), s32[]{:S(2)}) async-start(), calls=%async_computation.4 | async-start | bytes 10485760 | tf_op jit(solution)/shard_map/reduce_scatter | solution.py:143
  237.4 3.4 copy-start.3
  242.1 1.4 copy-start.6
  242.1 1.9 copy-start.7
  245.7 1.4 copy-start.1
  245.7 2.4 copy-start.2
  256.6 5.0 copy-start.13
  270.5 5.2 copy-start.8
  285.3 1.3 copy-start.12
  296.0 143.3 %copy-start.4 = (bf16[128,4096]{1,0:T(8,128)(2,1)S(1)}, bf16[128,4096]{1,0:T(8,128)(2,1)}, u32[]{:S(2)}) copy-start(bf16[128,4096]{1,0:T(8,128)(2,1)} %convolution_convert_fusion.1) | copy-start | bytes 3145732
  296.1 296.8 %all-gather.11.cloned.1.call-start = ((), (), s32[]{:S(2)}) async-start(), calls=%async_computation.5 | async-start | bytes 10485760 | tf_op jit(solution)/shard_map/all_gather | solution.py:150
  442.5 203.9 %all-gather.13.cloned.1.call-start = ((), (), s32[]{:S(2)}) async-start(), calls=%async_computation.6 | async-start | bytes 2621440 | tf_op jit(solution)/shard_map/all_gather | solution.py:166
  442.6 154.4 %copy-start.19 = (f32[4096]{0:T(1024)S(1)}, f32[4096]{0:T(1024)}, u32[]{:S(2)}) copy-start(f32[4096]{0:T(1024)} %param.25) | copy-start | bytes 49156
  592.8 5.8 copy-start.5
  612.9 70.1 %all-gather.15.cloned.1.call-start = ((), (), s32[]{:S(2)}) async-start(), calls=%async_computation.8 | async-start | bytes 2621440 | tf_op jit(solution)/shard_map/all_gather | solution.py:167
  615.1 174.0 %reduce-scatter.5.cloned.1.call-start = ((), (), s32[]{:S(2)}) async-start(), calls=%async_computation.7 | async-start | bytes 5242880 | tf_op jit(solution)/shard_map/reduce_scatter | solution.py:225
  712.1 77.0 %copy-start = (f32[128,4096]{1,0:T(8,128)S(1)}, f32[128,4096]{1,0:T(8,128)}, u32[]{:S(2)}) copy-start(f32[128,4096]{1,0:T(8,128)} %convert_add_fusion.1) | copy-start | bytes 6291460
  (3 other events, 3.7 us)
Sparse Core Ops, SparseCore 0:
  10.6 83.4 all-gather.6
  110.0 43.9 all-gather.8
  296.2 143.0 reduce-scatter.2
  442.6 150.2 all-gather.10
  613.0 33.2 all-gather.12
  648.0 35.0 all-gather.14
  712.2 76.7 reduce-scatter.4
where the time goes:
time: 807 us; the launch traced here: 799 us
  waiting for transfers between devices  521 us (65%)
  local copies, waits for them, and re-layouts  157 us (19%)
  matrix products  72.5 us (9%)
  other arithmetic  31.7 us (4%)
  between operations  15.5 us (2%)
    all_gather x1, waiting for transfers between devices, body(): stream_all = lax.all_gather(stream_own, 'tensor', axis=0, tiled=True)  150 us
    reduce_scatter x1, waiting for transfers between devices, body(): lax.psum_scatter(jnp.dot(hyena_mix, hyena_out, preferred_element_type=jnp...  143 us
    all_gather x1, waiting for transfers between devices, body(): embedded_all = lax.all_gather(embedded, 'tensor', axis=0, tiled=True)  83.6 us
    reduce_scatter x1, waiting for transfers between devices, body(): lax.psum_scatter(jnp.dot(attended, attn_out, preferred_element_type=jnp.f...  77 us
    gather x2, local copies, waits for them, and re-layouts, toeplitz(): jnp.take(long_filter, jnp.clip(tap_lag + filter_len, 0, filter_len - 1),...  61.2 us
    gather x2, local copies, waits for them, and re-layouts, toeplitz(): jnp.take(long_filter, jnp.clip(tap_lag, 0, filter_len - 1), axis=1)  60.3 us
    all_gather x1, waiting for transfers between devices, body(): value_piece = lax.all_gather(values_flat, 'context', axis=0, tiled=True)  36.8 us
    all_gather x1, waiting for transfers between devices, body(): key_piece = lax.all_gather(keys_flat, 'context', axis=0, tiled=True)  30.9 us
  transfers between devices with their start and end apart: 7, of which 6 were waited for; matrix products, arithmetic and copies ran while one was open for 16% of the time, Pallas kernels for 0%

commit v1 on v0

--- a/solution.py
+++ b/solution.py
@@ -3,6 +3,8 @@
 import jax
 import jax.numpy as jnp
 from jax import lax
+from jax.experimental import pallas as pl
+from jax.experimental.pallas import tpu as pltpu
 from jax.sharding import PartitionSpec as P
 
 HD = 128
@@ -76,7 +78,7 @@
     )
 
 
-def body(
+def generic_body(
     ids,
     block_order,
     embed,
@@ -231,7 +233,446 @@
     return stream_own + attn_own
 
 
+CODES = (65, 67, 71, 84)
+BF16 = jnp.bfloat16
+F32 = jnp.float32
+
+
+def swap_axis(value, axis, mask):
+    size = lax.axis_size(axis)
+    return lax.ppermute(value, axis, [(at, at ^ mask) for at in range(size)])
+
+
+def rows_of(weights, lane_start, width):
+    return lax.dynamic_slice(weights, (0, lane_start), (weights.shape[0], width))
+
+
+def along_chain(piece, edge_plane):
+    middle = [(1, 2), (2, 1)]
+    outward = [(1, 0), (2, 3)]
+    near = swap_axis(piece, "tensor", 1)
+    across = lax.ppermute(piece, "tensor", middle)
+    far_mid = lax.ppermute(near, "tensor", middle)
+    across_out = lax.ppermute(across, "tensor", outward)
+    far_out = lax.ppermute(far_mid, "tensor", outward)
+    return (
+        near,
+        jnp.where(edge_plane, across_out, across),
+        jnp.where(edge_plane, far_out, far_mid),
+    )
+
+
+def dot32(left, right):
+    return jnp.dot(left, right, preferred_element_type=F32)
+
+
+def hyena_kernel(coef_ref, hot_ref, taps_ref, skip_ref, mix_ref):
+    hot = hot_ref[...]
+    first, second, third = (dot32(coef_ref[j], hot) for j in range(3))
+    gated = second * third
+    packed = gated.astype(BF16)
+    row = lax.broadcasted_iota(jnp.int32, (128, 128), 0)
+    lane = lax.broadcasted_iota(jnp.int32, (128, 128), 1)
+    near = lane >= row
+    mixed = []
+    for group in range(16):
+        spread = jnp.broadcast_to(taps_ref[group : group + 1, :], (128, 128))
+        rolled = pltpu.roll(spread, 0, 1, stride=1, stride_axis=0)
+        zero = jnp.zeros_like(rolled)
+        matrix = jnp.concatenate(
+            [jnp.where(near, zero, rolled), jnp.where(near, rolled, zero)], axis=0
+        ).astype(BF16)
+        chans = packed[16 * group : 16 * group + 16]
+        left = jnp.concatenate(
+            [chans[:, at : at + 256] for at in (0, 128, 384, 512)], axis=0
+        )
+        result = dot32(left, matrix)
+        mixed.append(jnp.concatenate([result[16 * i : 16 * i + 16] for i in range(4)], axis=1))
+    long_mix = jnp.concatenate(mixed, axis=0)
+    own_gate = jnp.concatenate([gated[:, 128:384], gated[:, 512:768]], axis=1)
+    own_first = jnp.concatenate([first[:, 128:384], first[:, 512:768]], axis=1)
+    mix = own_first * (long_mix + skip_ref[...] * own_gate)
+    mix_ref[...] = mix.T.astype(BF16)
+
+
+def hyena_mixes(coef, hot, taps, skip):
+    chans = coef.shape[1]
+    step = 256
+    return pl.pallas_call(
+        hyena_kernel,
+        grid=(chans // step,),
+        in_specs=[
+            pl.BlockSpec((3, step, coef.shape[2]), lambda i: (0, i, 0)),
+            pl.BlockSpec(hot.shape, lambda i: (0, 0)),
+            pl.BlockSpec((step // 16, 128), lambda i: (i, 0)),
+            pl.BlockSpec((step, 1), lambda i: (i, 0)),
+        ],
+        out_specs=pl.BlockSpec((512, step), lambda i: (0, i)),
+        out_shape=jax.ShapeDtypeStruct((512, chans), BF16),
+        name="hyena_mix",
+    )(coef, hot, taps, skip)
+
+
+VM = pl.BlockSpec(memory_space=pltpu.VMEM)
+SM = pl.BlockSpec(memory_space=pltpu.SMEM)
+
+
+def branch_kernel(where_ref, own_mix_ref, oth_mix_ref, home_ref, *refs):
+    parts, (own_ref, oth_ref) = refs[:15], refs[15:]
+    for mix_ref, out_ref in ((own_mix_ref, own_ref), (oth_mix_ref, oth_ref)):
+
+        def lefts(unit, start, size):
+            base = pl.multiple_of(where_ref[unit] * 512, 512)
+            return mix_ref[:, pl.ds(base + start, size)]
+
+        for rel in range(4):
+            lane = pl.multiple_of(where_ref[4 + rel] * 512, 512)
+            total = dot32(lefts(0, 0, 512), home_ref[:, pl.ds(lane, 512)])
+            for unit in range(3):
+                block = parts[5 * unit : 5 * unit + 5]
+                if rel < 3:
+                    total += dot32(lefts(unit + 1, 0, 512), block[rel][...])
+                else:
+                    total += dot32(lefts(unit + 1, 0, 256), block[3][...])
+                    total += dot32(lefts(unit + 1, 256, 256), block[4][...])
+            out_ref[:, pl.ds(lane, 512)] = total.astype(out_ref.dtype)
+
+
+def hyena_branches(where, own_mix, oth_mix, home, parts):
+    return pl.pallas_call(
+        branch_kernel,
+        in_specs=[SM] + [VM] * (3 + len(parts)),
+        out_specs=[VM, VM],
+        out_shape=[
+            jax.ShapeDtypeStruct((512, 2048), F32),
+            jax.ShapeDtypeStruct((512, 2048), BF16),
+        ],
+        name="hyena_branch",
+    )(where, own_mix, oth_mix, home, *parts)
+
+
+def qkv_kernel(
+    where_ref, own_ref, oth_ref, hot_ref, base_ref, gain_ref, proj_ref, cos_ref, sin_ref,
+    out_ref, rows_ref, total_ref, power_ref, block_ref,
+):
+    at = pl.program_id(0)
+
+    @pl.when(at == 0)
+    def _():
+        total_ref[...] = jnp.zeros_like(total_ref)
+        power_ref[...] = jnp.zeros_like(power_ref)
+
+    embedded = dot32(hot_ref[...], base_ref[...])
+
+    @pl.when(at < 4)
+    def _():
+        block_ref[...] = embedded + own_ref[...]
+
+    @pl.when(at >= 4)
+    def _():
+        block_ref[...] = embedded + oth_ref[...].astype(F32)
+
+    stream = block_ref[...]
+    rows_ref[...] = block_ref[pl.ds(pl.multiple_of(where_ref[8] * 128, 128), 128), :]
+    power_ref[...] += jnp.sum(stream * stream, axis=1, keepdims=True)
+    scaled = (stream * gain_ref[...]).astype(BF16)
+    for j in range(3):
+        total_ref[:, 512 * j : 512 * j + 512] += dot32(scaled, proj_ref[j])
+
+    @pl.when(at == 7)
+    def _():
+        factor = lax.rsqrt(power_ref[...] * (1.0 / 4096.0) + EPS)
+        cosine = cos_ref[...] * factor
+        sine = sin_ref[...] * factor
+        for rel in range(4):
+            for j in range(3):
+                lane = pl.multiple_of(where_ref[9 + rel] * 128 + 512 * j, 128)
+                piece = total_ref[:, pl.ds(lane, 128)]
+                if j < 2:
+                    piece = piece * cosine + pltpu.roll(piece, 64, 1) * sine
+                else:
+                    piece = piece * factor
+                out_ref[rel, :, 128 * j : 128 * j + 128] = piece.astype(BF16)
+
+
+def qkv_heads(where, own, oth, hot, base, gain, proj, cosine, sine):
+    grid_spec = pltpu.PrefetchScalarGridSpec(
+        num_scalar_prefetch=1,
+        grid=(8,),
+        in_specs=[
+            pl.BlockSpec((512, 512), lambda i, w: (0, jnp.minimum(i, 3))),
+            pl.BlockSpec((512, 512), lambda i, w: (0, jnp.maximum(i - 4, 0))),
+            pl.BlockSpec(hot.shape, lambda i, w: (0, 0)),
+            pl.BlockSpec((base.shape[0], 512), lambda i, w: (0, w[i])),
+            pl.BlockSpec((1, 512), lambda i, w: (0, w[i])),
+            pl.BlockSpec((3, 512, 512), lambda i, w: (0, w[i], 0)),
+            pl.BlockSpec((512, 128), lambda i, w: (0, 0)),
+            pl.BlockSpec((512, 128), lambda i, w: (0, 0)),
+        ],
+        out_specs=[
+            pl.BlockSpec((4, 512, 384), lambda i, w: (0, 0, 0)),
+            pl.BlockSpec((128, 512), lambda i, w: (0, w[i])),
+        ],
+        scratch_shapes=[
+            pltpu.VMEM((512, 1536), F32),
+            pltpu.VMEM((512, 1), F32),
+            pltpu.VMEM((512, 512), F32),
+        ],
+    )
+    return pl.pallas_call(
+        qkv_kernel,
+        grid_spec=grid_spec,
+        out_shape=[
+            jax.ShapeDtypeStruct((4, 512, 384), BF16),
+            jax.ShapeDtypeStruct((128, 4096), F32),
+        ],
+        name="qkv_heads",
+    )(where, own, oth, hot, base, gain, proj, cosine, sine)
+
+
+def attend_kernel(slot_ref, x0_ref, x1_ref, x2_ref, x3_ref, out_ref, q_ref, k_ref, v_ref):
+    for rel, x_ref in enumerate((x0_ref, x1_ref, x2_ref, x3_ref)):
+        for half in range(2):
+            base = pl.multiple_of(slot_ref[2 * rel + half] * 256, 256)
+            rows = slice(256 * half, 256 * half + 256)
+            q_ref[pl.ds(base, 256), :] = x_ref[rows, 0:128]
+            k_ref[pl.ds(base, 256), :] = x_ref[rows, 128:256]
+            v_ref[pl.ds(base, 256), :] = x_ref[rows, 256:384]
+    row = lax.broadcasted_iota(jnp.int32, (256, 256), 0)
+    lane = lax.broadcasted_iota(jnp.int32, (256, 256), 1)
+    causal = lane <= row
+    scale = HD ** (-0.5)
+    for block in range(8):
+        width = 256 * block + 256
+        query = q_ref[256 * block : width, :]
+        scores = lax.dot_general(
+            query, k_ref[0:width, :], (((1,), (1,)), ((), ())), preferred_element_type=F32
+        )
+        last = jnp.where(causal, scores[:, width - 256 :], NEG_FILL)
+        if block > 0:
+            scores = jnp.concatenate([scores[:, : width - 256], last], axis=1)
+        else:
+            scores = last
+        top = jnp.max(scores, axis=1, keepdims=True)
+        weights = jnp.exp((scores - top) * scale)
+        total = jnp.sum(weights, axis=1, keepdims=True)
+        mixed = dot32(weights.astype(BF16), v_ref[0:width, :])
+        base = pl.multiple_of(slot_ref[8 + block] * 256, 256)
+        out_ref[pl.ds(base, 256), :] = (mixed / total).astype(BF16)
+
+
+def attend(slots, pieces):
+    return pl.pallas_call(
+        attend_kernel,
+        in_specs=[SM] + [VM] * 4,
+        out_specs=VM,
+        out_shape=jax.ShapeDtypeStruct((2048, 128), BF16),
+        scratch_shapes=[pltpu.VMEM((2048, 128), BF16)] * 3,
+        name="attend",
+    )(slots, *pieces)
+
+
+def out_kernel(where_ref, own_ref, oth_ref, home_ref, *refs):
+    parts, (own_out_ref, oth_out_ref, left_ref) = refs[:9], refs[9:]
+    for side, src_ref in enumerate((own_ref, oth_ref)):
+        for far in range(4):
+            for rel in range(4):
+                head = where_ref[4 + far] * 4 + where_ref[8 + rel]
+                lane = pl.multiple_of(head * 128, 128)
+                at = 512 * far + 128 * rel
+                left_ref[128 * side : 128 * side + 128, pl.ds(lane, 128)] = src_ref[
+                    :, at : at + 128
+                ]
+
+    def left(unit):
+        return left_ref[:, pl.ds(pl.multiple_of(where_ref[unit] * 512, 512), 512)]
+
+    for quarter in range(4):
+        near = quarter < 2
+        half = where_ref[12] if near else 1 - where_ref[12]
+        lane = pl.multiple_of(half * 1024 + (quarter % 2) * 512, 512)
+        total = dot32(left(0), home_ref[:, pl.ds(lane, 512)])
+        for unit in range(3):
+            block, side_x, side_y = parts[3 * unit : 3 * unit + 3]
+            if near:
+                right = block[:, 512 * quarter : 512 * quarter + 512]
+            else:
+                right = (side_x, side_y)[quarter - 2][...]
+            total += dot32(left(unit + 1), right)
+        own_out_ref[:, pl.ds(lane, 512)] = total[:128]
+        oth_out_ref[:, pl.ds(lane, 512)] = total[128:].astype(oth_out_ref.dtype)
+
+
+def out_branches(where, own, oth, home, parts):
+    return pl.pallas_call(
+        out_kernel,
+        in_specs=[SM] + [VM] * (3 + len(parts)),
+        out_specs=[VM, VM],
+        out_shape=[
+            jax.ShapeDtypeStruct((128, 2048), F32),
+            jax.ShapeDtypeStruct((128, 2048), BF16),
+        ],
+        scratch_shapes=[pltpu.VMEM((256, 2048), BF16)],
+        name="out_branch",
+    )(where, own, oth, home, *parts)
+
+
+def block_body(
+    ids,
+    block_order,
+    embed,
+    mix_gain,
+    in_proj,
+    short_filter,
+    long_filter,
+    conv_skip,
+    hyena_out,
+    attn_gain,
+    qkv_proj,
+    attn_out,
+):
+    half_at = lax.axis_index("dp")
+    ctx = lax.axis_index("context")
+    plane = lax.axis_index("tensor")
+    edge = jnp.logical_or(plane == 0, plane == 3)
+    order = block_order.astype(jnp.int32)
+    half_lane = half_at * 2048
+
+    home = rows_of(hyena_out, half_lane, 2048)
+    units = along_chain(rows_of(hyena_out, half_lane + ctx * 512, 512), edge)
+    parts = []
+    for unit in units:
+        side_x = swap_axis(unit, "context", 1)
+        side_y = swap_axis(unit, "context", 2)
+        corner_top = swap_axis(side_y[:256], "context", 1)
+        corner_low = swap_axis(side_x[256:], "context", 2)
+        parts += [unit, side_x, side_y, corner_top, corner_low]
+
+    all_ids = lax.all_to_all(
+        jnp.tile(ids[None], (16, 1)), ("context", "tensor"), 0, 0, tiled=True
+    ).reshape(8, 256)
+
+    base = jnp.concatenate([embed[code : code + 1] for code in CODES], axis=0)
+    mixed_in = rms_scale(base, mix_gain)
+    table = jnp.einsum(
+        "rd,jdc->jrc", mixed_in, in_proj, preferred_element_type=F32
+    ).astype(BF16)
+    packed = jnp.concatenate(
+        [
+            table.astype(F32).reshape(12, 512),
+            short_filter.reshape(9, 512),
+            conv_skip.reshape(1, 512),
+            long_filter.reshape(8, 512),
+        ],
+        axis=0,
+    )
+    everything = lax.all_to_all(
+        jnp.tile(packed[None], (4, 1, 1)), "tensor", 0, 0, tiled=True
+    )
+    tables = everything[:, :12].reshape(4, 3, 1, 4, 512)
+    shorts = everything[:, 12:21].reshape(4, 3, 3, 1, 512)
+    coef = (tables * shorts).transpose(1, 0, 4, 2, 3).reshape(3, 2048, 12)
+    coarse = lax.reduce_precision(coef, 8, 7)
+    coef = jnp.concatenate([coarse, coef - coarse], axis=2).astype(BF16)
+    skip = everything[:, 21].reshape(2048, 1)
+    taps = everything[:, 22:].reshape(128, 128)
+
+    slot_pair = 2 * ctx + jnp.arange(2, dtype=jnp.int32)
+    slot_ids = jnp.arange(8, dtype=jnp.int32)
+    own_hit = slot_ids[None, :] == slot_pair[:, None]
+    owned = jnp.sum(jnp.where(own_hit, order[None, :], 0), axis=1)
+    before_hit = order[None, :] == owned[:, None] - 1
+    own_ids = jnp.sum(jnp.where(own_hit[:, :, None], all_ids[None], 0), axis=1)
+    before_ids = jnp.sum(jnp.where(before_hit[:, :, None], all_ids[None], 0), axis=1)
+    span = jnp.concatenate([before_ids, own_ids], axis=1)
+    codes = jnp.array(CODES, jnp.int32)
+    hot = jnp.stack(
+        [
+            (span[None, :, 128 - lag : 512 - lag] == codes[:, None, None]).astype(BF16)
+            for lag in range(3)
+        ]
+    ).reshape(12, 768)
+    hot = jnp.concatenate([hot, hot], axis=0)
+    own_mix = hyena_mixes(coef, hot, taps, skip)
+    oth_mix = swap_axis(own_mix, "dp", 1)
+
+    unit_plane = [
+        jnp.array([1, 0, 3, 2], jnp.int32)[plane],
+        jnp.array([2, 2, 1, 1], jnp.int32)[plane],
+        jnp.array([3, 3, 0, 0], jnp.int32)[plane],
+    ]
+    where = jnp.stack([plane] + unit_plane + [ctx ^ rel for rel in range(4)])
+    own_half, give_half = hyena_branches(where, own_mix, oth_mix, home, parts)
+    got_half = swap_axis(give_half, "dp", 1)
+
+    local_pos = (
+        owned[:, None] * 256 + jnp.arange(256, dtype=jnp.int32)[None, :]
+    ).reshape(512)
+    inverse_freq = THETA ** (-(2.0 * jnp.arange(64, dtype=F32)) / HD)
+    angles = local_pos.astype(F32)[:, None] * inverse_freq[None, :]
+    cosine = jnp.cos(angles)
+    sine = jnp.sin(angles)
+    cosine = jnp.concatenate([cosine, cosine], axis=1)
+    sine = jnp.concatenate([-sine, sine], axis=1)
+    own_hot = (own_ids.reshape(512, 1) == codes[None, :]).astype(BF16)
+    blocks = [half_at * 4 + at for at in range(4)] + [(1 - half_at) * 4 + at for at in range(4)]
+    where = jnp.stack(blocks + [plane] + [ctx ^ rel for rel in range(4)])
+    heads, stream_rows = qkv_heads(
+        where, own_half, got_half, own_hot, base, attn_gain[None], qkv_proj, cosine, sine
+    )
+
+    pieces = [heads[0]] + [swap_axis(heads[rel], "context", rel) for rel in range(1, 4)]
+    near_slots = jnp.stack([2 * (ctx ^ rel) + half for rel in range(4) for half in range(2)])
+    hit = near_slots[:, None] == slot_ids[None, :]
+    place = jnp.sum(jnp.where(hit, order[None, :], 0), axis=1)
+    holder = jnp.sum(
+        jnp.where(place[None, :] == slot_ids[:, None], slot_ids[None, :], 0), axis=1
+    )
+    attended = attend(jnp.concatenate([place, holder]), pieces).reshape(4, 512, 128)
+    mine = jnp.concatenate(
+        [attended[0]] + [swap_axis(attended[rel], "context", rel) for rel in range(1, 4)],
+        axis=1,
+    ).reshape(4, 128, 512)
+
+    def rows_for(rel):
+        return lax.dynamic_index_in_dim(mine, plane ^ rel, 0, keepdims=False)
+
+    own_att = jnp.concatenate(
+        [rows_for(0)] + [swap_axis(rows_for(rel), "tensor", rel) for rel in range(1, 4)],
+        axis=1,
+    )
+    oth_att = swap_axis(own_att, "dp", 1)
+
+    home = rows_of(attn_out, half_lane, 2048)
+    cross = (ctx & 1) ^ (ctx >> 1)
+    units = along_chain(rows_of(attn_out, half_lane + cross * 1024, 1024), edge)
+    parts = []
+    for unit in units:
+        parts += [
+            unit,
+            swap_axis(unit[:, :512], "context", 1),
+            swap_axis(unit[:, 512:], "context", 2),
+        ]
+    where = jnp.stack(
+        [plane]
+        + unit_plane
+        + [plane ^ rel for rel in range(4)]
+        + [ctx ^ rel for rel in range(4)]
+        + [cross]
+    )
+    own_out, give_out = out_branches(where, own_att, oth_att, home, parts)
+    got_out = swap_axis(give_out, "dp", 1).astype(F32)
+    first = half_at == 0
+    attn_rows = jnp.concatenate(
+        [jnp.where(first, own_out, got_out), jnp.where(first, got_out, own_out)], axis=1
+    )
+    return stream_rows + attn_rows
+
+
 def solution(mesh):
+    grid_shape = dict(mesh.shape)
+    square = (grid_shape["dp"], grid_shape["context"], grid_shape["tensor"]) == (2, 4, 4)
+    body = block_body if square else generic_body
     placed = (
         P(("dp", "context", "tensor")),
         P("dp"),

time: 807 us -> 293 us (0.36)
  waiting for transfers between devices: 521 us -> 77.1 us
  local copies, waits for them, and re-layouts: 157 us -> 43.2 us
  starting transfers between devices: 0.25 us -> 90.9 us
  matrix products: 72.5 us -> 6.38 us
  Pallas kernels: 0 us -> 55.9 us
  between operations: 15.5 us -> 0.65 us
  other arithmetic: 31.7 us -> 17.4 us
    all_gather x5 -> x0, waiting for transfers between devices: 301 us -> none  [the longest x1 150 us: body(): stream_all = lax.all_gather(stream_own, 'tensor', axis=0, tiled=True)]
    reduce_scatter x2 -> x0, waiting for transfers between devices: 220 us -> none  [the longest x1 143 us: body(): lax.psum_scatter(jnp.dot(hyena_mix, hyena_out, preferred_element_type=jnp...]
    gather x4 -> x0, local copies, waits for them, and re-layouts: 122 us -> none  [the longest x2 61.2 us: toeplitz(): jnp.take(long_filter, jnp.clip(tap_lag + filter_len, 0, filter_len - 1),...]
    ppermute x0 -> x41, starting transfers between devices: none -> 79 us  [the longest x33 67.6 us: swap_axis(): return lax.ppermute(value, axis, [(at, at ^ mask) for at in range(size)])]
    ppermute x0 -> x41, waiting for transfers between devices: none -> 71.4 us  [the longest x33 44.5 us: swap_axis(): return lax.ppermute(value, axis, [(at, at ^ mask) for at in range(size)])]
    dot_general x27 -> x1, matrix products: 72.5 us -> 6.38 us  [block_body(): jnp.einsum('rd,jdc->jrc', mixed_in, in_proj, preferred_element_type=F32)]
    pallas_call x0 -> x5, Pallas kernels: none -> 55.9 us  [the longest x1 17.5 us: qkv_heads(): pl.pallas_call(qkv_kernel, grid_spec=grid_spec, out_shape=[jax.ShapeDtype...]
    all_to_all x0 -> x2, starting transfers between devices: none -> 11.9 us  [the longest x1 6.87 us: block_body(): lax.all_to_all(jnp.tile(ids[None], (16, 1)), ('context', 'tensor'), 0, 0,...]
  transfers between devices with their start and end apart: 7 -> 43, of which waited for: 6 -> 17; matrix products, arithmetic and copies ran while one was open for 16% -> 20% of each run, Pallas kernels for 0% -> 17%
where the time goes in v1:
time: 293 us; the launch traced here: 291 us
  starting transfers between devices  90.9 us (31%)
  waiting for transfers between devices  77.1 us (26%)
  Pallas kernels  55.9 us (19%)
  local copies, waits for them, and re-layouts  43.2 us (15%)
  other arithmetic  17.4 us (6%)
  matrix products  6.38 us (2%)
    ppermute x33, starting transfers between devices, swap_axis(): return lax.ppermute(value, axis, [(at, at ^ mask) for at in range(size)])  67.6 us
    ppermute x33, waiting for transfers between devices, swap_axis(): return lax.ppermute(value, axis, [(at, at ^ mask) for at in range(size)])  44.5 us
    pallas_call x1, Pallas kernels, qkv_heads(): pl.pallas_call(qkv_kernel, grid_spec=grid_spec, out_shape=[jax.ShapeDtype...  17.5 us
    pallas_call x1, Pallas kernels, hyena_branches(): pl.pallas_call(branch_kernel, in_specs=[SM] + [VM] * (3 + len(parts)), ou...  14.7 us
    ppermute x2, waiting for transfers between devices, along_chain(): across_out = lax.ppermute(across, 'tensor', outward)  14.7 us
    ppermute x2, waiting for transfers between devices, along_chain(): far_out = lax.ppermute(far_mid, 'tensor', outward)  12.3 us
    dynamic_slice x4, local copies, waits for them, and re-layouts, rows_of(): lax.dynamic_slice(weights, (0, lane_start), (weights.shape[0], width))  9.85 us
    pallas_call x1, Pallas kernels, hyena_mixes(): pl.pallas_call(hyena_kernel, grid=(chans // step,), in_specs=[pl.BlockSpe...  9.17 us
  transfers between devices with their start and end apart: 43, of which 17 were waited for; matrix products, arithmetic and copies ran while one was open for 20% of the time, Pallas kernels for 17%

profile of v1, /device:TPU:0, one launch (start us, length us, event | category | flops | bytes accessed | tf_op | source)
XLA Modules:
  0.0 291.5 jit_solution(1050026204068924637)
XLA Ops:
  1.1 3.1 %collective-permute-start.1 = (bf16[512,512]{1,0:T(8,128)(2,1)S(1)}, bf16[512,512]{1,0:T(8,128)(2,1)}, u32[]{:S(2)}, u32[]{:S(2)}) collective-permute-start(bf16[512,512]{1,0:T(8,128)(2,1)S(1)} %constant_dynamic-slice_fusion.2), channel_id=1, source_target_pairs={{0,1},{1,0},{2,3},{3,2},{4,5},{5,4},{6,7},{7,6},{8,9},{9,8},{10,11... | collective-permute-start | bytes 1572872 | tf_op jit(solution)/shard_map/ppermute | solution.py:243
  6.9 6.9 %all-to-all-start.1 = ((s32[16,1,128]{2,1,0:T(1,128)}), s32[16,1,128]{2,1,0:T(1,128)S(1)}, u32[]{:S(2)}, u32[]{:S(2)}) async-start(s32[16,1,128]{2,1,0:T(1,128)} %tile.5), calls=%async_computation.1 | async-start | bytes 16384 | tf_op jit(solution)/shard_map/all_to_all | solution.py:551
  16.7 6.4 %fusion.1 = f32[3,4,512]{2,1,0:T(4,128)S(1)} fusion(bf16[3,4096,512]{2,1,0:T(8,128)(2,1)} %param.20, bf16[4,4096]{1,0:T(4,128)(2,1)S(1)} %get-tuple-element.20.base_ref, f32[4096]{0:T(1024)} %param.19, f32[4]{0:T(128)S(1)} %add_rsqrt_fusion), kind=kOutput, calls=%fused_computation.5 | convolution fusion | flops 50409472 | bytes 12656656 | tf_op jit(solution)/shard_map/rd,jdc->jrc/dot_general | solution.py:557
  23.9 5.0 %all-to-all-start = ((f32[4,30,512]{2,1,0:T(8,128)}), f32[4,30,512]{2,1,0:T(8,128)S(1)}, u32[]{:S(2)}, u32[]{:S(2)}) async-start(f32[4,30,512]{2,1,0:T(8,128)} %tile.4), calls=%async_computation | async-start | bytes 524288 | tf_op jit(solution)/shard_map/all_to_all | solution.py:569
  31.2 5.6 %all-to-all-done = f32[4,30,512]{2,1,0:T(8,128)S(1)} async-done(((f32[4,30,512]{2,1,0:T(8,128)}), f32[4,30,512]{2,1,0:T(8,128)S(1)}, u32[]{:S(2)}, u32[]{:S(2)}) %all-to-all-start) | async-done | bytes 245792 | tf_op jit(solution)/shard_map/all_to_all | solution.py:569
  43.8 9.2 %hyena_mix.1.own_mix_ref = bf16[512,2048]{1,0:T(8,128)(2,1)} custom-call(bf16[3,2048,24]{2,1,0:T(8,128)(2,1)} %copy.38.coef_ref, bf16[24,768]{1,0:T(8,128)(2,1)} %add_convert_fusion.hot_ref, f32[128,128]{1,0:T(8,128)} %reshape.179.taps_ref, f32[2048,1]{1,0:T(8,128)} %copy.39.skip_ref), custom_call_target="tpu_custom_call" | custom-call | tf_op jit(solution)/shard_map/hyena_mix/pallas_call | solution.py:301
  59.0 11.5 %collective-permute-done.13 = bf16[512,512]{1,0:T(8,128)(2,1)S(1)} collective-permute-done((bf16[512,512]{1,0:T(8,128)(2,1)}, bf16[512,512]{1,0:T(8,128)(2,1)S(1)}, u32[]{:S(2)}, u32[]{:S(2)}) %collective-permute-start.13) | collective-permute-done | bytes 524320 | tf_op jit(solution)/shard_map/ppermute | solution.py:257
  77.4 3.1 %collective-permute-done.9.refs_7_ = bf16[512,512]{1,0:T(8,128)(2,1)S(1)} collective-permute-done((bf16[512,512]{1,0:T(8,128)(2,1)S(1)}, bf16[512,512]{1,0:T(8,128)(2,1)S(1)}, u32[]{:S(2)}, u32[]{:S(2)}) %collective-permute-start.9) | collective-permute-done | bytes 524320 | tf_op jit(solution)/shard_map/ppermute | solution.py:243
  82.8 3.3 %collective-permute-done.8.refs_6_ = bf16[512,512]{1,0:T(8,128)(2,1)S(1)} collective-permute-done((bf16[512,512]{1,0:T(8,128)(2,1)S(1)}, bf16[512,512]{1,0:T(8,128)(2,1)S(1)}, u32[]{:S(2)}, u32[]{:S(2)}) %collective-permute-start.8) | collective-permute-done | bytes 524320 | tf_op jit(solution)/shard_map/ppermute | solution.py:243
  87.5 4.3 %collective-permute-done.15.refs_12_ = bf16[512,512]{1,0:T(8,128)(2,1)S(1)} collective-permute-done((bf16[512,512]{1,0:T(8,128)(2,1)S(1)}, bf16[512,512]{1,0:T(8,128)(2,1)S(1)}, u32[]{:S(2)}, u32[]{:S(2)}) %collective-permute-start.15) | collective-permute-done | bytes 524320 | tf_op jit(solution)/shard_map/ppermute | solution.py:243
  97.9 3.5 %collective-permute-start.29 = (bf16[512,1024]{1,0:T(8,128)(2,1)}, bf16[512,1024]{1,0:T(8,128)(2,1)S(1)}, u32[]{:S(2)}, u32[]{:S(2)}) collective-permute-start(bf16[512,1024]{1,0:T(8,128)(2,1)} %constant_dynamic-slice_fusion), channel_id=1, source_target_pairs={{0,1},{1,0},{2,3},{3,2},{4,5},{5,4},{6,7},{7,6},{8,9},{9,8},{10,11... | collective-permute-start | bytes 3145736 | tf_op jit(solution)/shard_map/ppermute | solution.py:243
  110.1 3.2 %constant_dynamic-slice_fusion.3.home_ref = bf16[512,2048]{1,0:T(8,128)(2,1)} fusion(bf16[512,4096]{1,0:T(8,128)(2,1)} %param.24, s32[]{:T(128)S(6)} %select_n.84), kind=kLoop, calls=%fused_computation.63 | loop fusion | bytes 4194308 | tf_op jit(solution)/shard_map/dynamic_slice | solution.py:247
  119.1 14.7 %hyena_branch.1 = (f32[512,2048]{1,0:T(8,128)}, bf16[512,2048]{1,0:T(8,128)(2,1)}) custom-call(s32[8]{0:T(128)} %stack.119.where_ref, bf16[512,2048]{1,0:T(8,128)(2,1)} %hyena_mix.1.own_mix_ref, bf16[512,2048]{1,0:T(8,128)(2,1)} %copy-done.4, bf16[512,2048]{1,0:T(8,128)(2,1)} %constant_dynamic-slice_fusion.3.home_ref, ...), custom_call_target="tpu_custom_call" | custom-call | tf_op jit(solution)/shard_map/hyena_branch/pallas_call | solution.py:342
  150.2 17.5 %qkv_heads.1 = (bf16[4,512,384]{2,1,0:T(8,128)(2,1)}, f32[128,4096]{1,0:T(8,128)}) custom-call(s32[13]{0:T(128)} %stack.118.where_ref, f32[512,2048]{1,0:T(8,128)} %get-tuple-element.11.own_ref, bf16[512,2048]{1,0:T(8,128)(2,1)} %copy-done.5, bf16[512,4]{1,0:T(8,128)(2,1)} %compare_convert_fusion.hot_ref, bf16[4,4096]{1,0:T(4,128)(2,1)} %copy-done.25, ...), custom_call_target="tpu_custom_call" | custom-call | tf_op jit(solution)/shard_map/qkv_heads/pallas_call | solution.py:422
  171.2 14.7 %collective-permute-done.33 = bf16[512,1024]{1,0:T(8,128)(2,1)} collective-permute-done((bf16[512,1024]{1,0:T(8,128)(2,1)}, bf16[512,1024]{1,0:T(8,128)(2,1)}, u32[]{:S(2)}, u32[]{:S(2)}) %collective-permute-start.33) | collective-permute-done | bytes 1048608 | tf_op jit(solution)/shard_map/ppermute | solution.py:256
  191.3 5.1 %collective-permute-done.21.x3_ref = bf16[512,384]{1,0:T(8,128)(2,1)S(1)} collective-permute-done((bf16[512,384]{1,0:T(8,128)(2,1)S(1)}, bf16[512,384]{1,0:T(8,128)(2,1)S(1)}, u32[]{:S(2)}, u32[]{:S(2)}) %collective-permute-start.21) | collective-permute-done | bytes 393248 | tf_op jit(solution)/shard_map/ppermute | solution.py:243
  197.2 7.1 %attend.1 = bf16[2048,128]{1,0:T(8,128)(2,1)} custom-call(s32[16]{0:T(128)} %pad_add_fusion.2.slot_ref, bf16[512,384]{1,0:T(8,128)(2,1)} %get-tuple-element.30.x0_ref, bf16[512,384]{1,0:T(8,128)(2,1)} %copy-done.22, bf16[512,384]{1,0:T(8,128)(2,1)} %copy-done.23, bf16[512,384]{1,0:T(8,128)(2,1)} %copy-done.24), custom_call_target="tpu_custom_call" | custom-call | tf_op jit(solution)/shard_map/attend/pallas_call | solution.py:465
  211.1 3.6 %collective-permute-done.23 = bf16[512,128]{1,0:T(8,128)(2,1)S(1)} collective-permute-done((bf16[512,128]{1,0:T(8,128)(2,1)S(1)}, bf16[512,128]{1,0:T(8,128)(2,1)S(1)}, u32[]{:S(2)}, u32[]{:S(2)}) %collective-permute-start.23) | collective-permute-done | bytes 131104 | tf_op jit(solution)/shard_map/ppermute | solution.py:243
  214.8 29.8 %collective-permute-start.25 = (bf16[128,512]{1,0:T(8,128)(2,1)S(1)}, bf16[128,512]{1,0:T(8,128)(2,1)S(1)}, u32[]{:S(2)}, u32[]{:S(2)}) collective-permute-start(bf16[128,512]{1,0:T(8,128)(2,1)S(1)} %get-tuple-element.40), channel_id=1, source_target_pairs={{0,1},{1,0},{2,3},{3,2},{4,5},{5,4},{6,7},{7,6},{8,9},{9,8},{10,11... | collective-permute-start | bytes 393224 | tf_op jit(solution)/shard_map/ppermute | solution.py:243
  251.3 3.4 %collective-permute-done.26 = bf16[128,512]{1,0:T(8,128)(2,1)S(1)} collective-permute-done((bf16[128,512]{1,0:T(8,128)(2,1)S(1)}, bf16[128,512]{1,0:T(8,128)(2,1)S(1)}, u32[]{:S(2)}, u32[]{:S(2)}) %collective-permute-start.26) | collective-permute-done | bytes 131104 | tf_op jit(solution)/shard_map/ppermute | solution.py:243
  260.3 3.2 %constant_dynamic-slice_fusion.1.home_ref = bf16[512,2048]{1,0:T(8,128)(2,1)} fusion(bf16[512,4096]{1,0:T(8,128)(2,1)} %param.27, s32[]{:T(128)S(6)} %select_n.84), kind=kLoop, calls=%fused_computation.61 | loop fusion | bytes 4194308 | tf_op jit(solution)/shard_map/dynamic_slice | solution.py:247
  264.1 5.7 %collective-permute-done.35.refs_5_ = bf16[512,512]{1,0:T(8,128)(2,1)S(1)} collective-permute-done((bf16[512,512]{1,0:T(8,128)(2,1)}, bf16[512,512]{1,0:T(8,128)(2,1)S(1)}, u32[]{:S(2)}, u32[]{:S(2)}) %collective-permute-start.35) | collective-permute-done | bytes 524320 | tf_op jit(solution)/shard_map/ppermute | solution.py:243
  271.0 7.0 %collective-permute-done.39.refs_8_ = bf16[512,512]{1,0:T(8,128)(2,1)S(1)} collective-permute-done((bf16[512,512]{1,0:T(8,128)(2,1)}, bf16[512,512]{1,0:T(8,128)(2,1)S(1)}, u32[]{:S(2)}, u32[]{:S(2)}) %collective-permute-start.39) | collective-permute-done | bytes 524320 | tf_op jit(solution)/shard_map/ppermute | solution.py:243
  278.8 7.4 %out_branch.1 = (f32[128,2048]{1,0:T(8,128)}, bf16[128,2048]{1,0:T(8,128)(2,1)}) custom-call(s32[13]{0:T(128)} %stack.125.where_ref, bf16[128,2048]{1,0:T(8,128)(2,1)} %copy-done.8, bf16[128,2048]{1,0:T(8,128)(2,1)} %collective-permute-done.28.oth_ref, bf16[512,2048]{1,0:T(8,128)(2,1)} %constant_dynamic-slice_fusion.1.home_ref, bf16[512,1024]{1,0:T(8,128)(2,1)} %copy-done.2, ...), custom_call_target="tpu_custom_call" | custom-call | tf_op jit(solution)/shard_map/out_branch/pallas_call | solution.py:507
  (215 shorter events, 106.6 us)
Async XLA Ops:
  1.1 36.2 %collective-permute-start.1 = (bf16[512,512]{1,0:T(8,128)(2,1)S(1)}, bf16[512,512]{1,0:T(8,128)(2,1)}, u32[]{:S(2)}, u32[]{:S(2)}) collective-permute-start(bf16[512,512]{1,0:T(8,128)(2,1)S(1)} %constant_dynamic-slice_fusion.2), channel_id=1, source_target_pairs={{0,1},{1,0},{2,3},{3,2},{4,5},{5,4},{6,7},{7,6},{8,9},{9,8},{10,11... | collective-permute-start | bytes 1572872 | tf_op jit(solution)/shard_map/ppermute | solution.py:243
  4.2 34.7 %collective-permute-start.6 = (bf16[512,512]{1,0:T(8,128)(2,1)S(1)}, bf16[512,512]{1,0:T(8,128)(2,1)}, u32[]{:S(2)}, u32[]{:S(2)}) collective-permute-start(bf16[512,512]{1,0:T(8,128)(2,1)S(1)} %constant_dynamic-slice_fusion.2), channel_id=1, source_target_pairs={{1,2},{2,1},{5,6},{6,5},{9,10},{10,9},{13,14},{14,13},{17,18},{18,... | collective-permute-start | bytes 1572872 | tf_op jit(solution)/shard_map/ppermute | solution.py:254
  6.9 16.3 %all-to-all-start.1 = ((s32[16,1,128]{2,1,0:T(1,128)}), s32[16,1,128]{2,1,0:T(1,128)S(1)}, u32[]{:S(2)}, u32[]{:S(2)}) async-start(s32[16,1,128]{2,1,0:T(1,128)} %tile.5), calls=%async_computation.1 | async-start | bytes 16384 | tf_op jit(solution)/shard_map/all_to_all | solution.py:551
  38.9 18.4 %collective-permute-start.7 = (bf16[512,512]{1,0:T(8,128)(2,1)}, bf16[512,512]{1,0:T(8,128)(2,1)}, u32[]{:S(2)}, u32[]{:S(2)}) collective-permute-start(bf16[512,512]{1,0:T(8,128)(2,1)} %collective-permute-done.6), channel_id=1, source_target_pairs={{1,0},{2,3},{5,4},{6,7},{9,8},{10,11},{13,12},{14,15},{17,16},{18,... | collective-permute-start | bytes 1572872 | tf_op jit(solution)/shard_map/ppermute | solution.py:256
  52.9 64.9 %collective-permute-start = (bf16[512,2048]{1,0:T(8,128)(2,1)}, bf16[512,2048]{1,0:T(8,128)(2,1)S(1)}, u32[]{:S(2)}, u32[]{:S(2)}) collective-permute-start(bf16[512,2048]{1,0:T(8,128)(2,1)} %hyena_mix.1.own_mix_ref), channel_id=1, source_target_pairs={{0,16},{16,0},{1,17},{17,1},{2,18},{18,2},{3,19},{19,3},{4,20},{20... | collective-permute-start | bytes 6291464 | tf_op jit(solution)/shard_map/ppermute | solution.py:243
  52.9 17.5 %collective-permute-start.13 = (bf16[512,512]{1,0:T(8,128)(2,1)}, bf16[512,512]{1,0:T(8,128)(2,1)S(1)}, u32[]{:S(2)}, u32[]{:S(2)}) collective-permute-start(bf16[512,512]{1,0:T(8,128)(2,1)} %collective-permute-done.12), channel_id=1, source_target_pairs={{1,0},{2,3},{5,4},{6,7},{9,8},{10,11},{13,12},{14,15},{17,16},{18,... | collective-permute-start | bytes 1572872 | tf_op jit(solution)/shard_map/ppermute | solution.py:257
  54.2 19.6 %collective-permute-start.3 = (bf16[512,512]{1,0:T(8,128)(2,1)}, bf16[512,512]{1,0:T(8,128)(2,1)S(1)}, u32[]{:S(2)}, u32[]{:S(2)}) collective-permute-start(bf16[512,512]{1,0:T(8,128)(2,1)} %collective-permute-done.1.refs_0_), channel_id=1, source_target_pairs={{0,8},{4,12},{8,0},{12,4},{1,9},{5,13},{9,1},{13,5},{2,10},{6,14},... | collective-permute-start | bytes 1572872 | tf_op jit(solution)/shard_map/ppermute | solution.py:243
  55.8 19.6 %collective-permute-start.2 = (bf16[512,512]{1,0:T(8,128)(2,1)}, bf16[512,512]{1,0:T(8,128)(2,1)S(1)}, u32[]{:S(2)}, u32[]{:S(2)}) collective-permute-start(bf16[512,512]{1,0:T(8,128)(2,1)} %collective-permute-done.1.refs_0_), channel_id=1, source_target_pairs={{0,4},{4,0},{8,12},{12,8},{1,5},{5,1},{9,13},{13,9},{2,6},{6,2},{1... | collective-permute-start | bytes 1572872 | tf_op jit(solution)/shard_map/ppermute | solution.py:243
  58.4 22.2 %collective-permute-start.9 = (bf16[512,512]{1,0:T(8,128)(2,1)S(1)}, bf16[512,512]{1,0:T(8,128)(2,1)S(1)}, u32[]{:S(2)}, u32[]{:S(2)}) collective-permute-start(bf16[512,512]{1,0:T(8,128)(2,1)S(1)} %broadcast_select_fusion.3.refs_5_), channel_id=1, source_target_pairs={{0,8},{4,12},{8,0},{12,4},{1,9},{5,13},{9,1},{13,5},{2,10},{6,14},... | collective-permute-start | bytes 1572872 | tf_op jit(solution)/shard_map/ppermute | solution.py:243
  73.9 17.9 %collective-permute-start.15 = (bf16[512,512]{1,0:T(8,128)(2,1)S(1)}, bf16[512,512]{1,0:T(8,128)(2,1)S(1)}, u32[]{:S(2)}, u32[]{:S(2)}) collective-permute-start(bf16[512,512]{1,0:T(8,128)(2,1)S(1)} %broadcast_select_fusion.2.refs_10_), channel_id=1, source_target_pairs={{0,8},{4,12},{8,0},{12,4},{1,9},{5,13},{9,1},{13,5},{2,10},{6,14},... | collective-permute-start | bytes 1572872 | tf_op jit(solution)/shard_map/ppermute | solution.py:243
  75.4 22.5 %collective-permute-start.14 = (bf16[512,512]{1,0:T(8,128)(2,1)S(1)}, bf16[512,512]{1,0:T(8,128)(2,1)}, u32[]{:S(2)}, u32[]{:S(2)}) collective-permute-start(bf16[512,512]{1,0:T(8,128)(2,1)S(1)} %broadcast_select_fusion.2.refs_10_), channel_id=1, source_target_pairs={{0,4},{4,0},{8,12},{12,8},{1,5},{5,1},{9,13},{13,9},{2,6},{6,2},{1... | collective-permute-start | bytes 1572872 | tf_op jit(solution)/shard_map/ppermute | solution.py:243
  80.6 22.5 %collective-permute-start.4 = (bf16[256,512]{1,0:T(8,128)(2,1)}, bf16[256,512]{1,0:T(8,128)(2,1)S(1)}, u32[]{:S(2)}, u32[]{:S(2)}) collective-permute-start(bf16[256,512]{1,0:T(8,128)(2,1)} %slice.136), channel_id=1, source_target_pairs={{0,4},{4,0},{8,12},{12,8},{1,5},{5,1},{9,13},{13,9},{2,6},{6,2},{1... | collective-permute-start | bytes 786440 | tf_op jit(solution)/shard_map/ppermute | solution.py:243
  86.1 18.6 %collective-permute-start.5 = (bf16[256,512]{1,0:T(8,128)(2,1)}, bf16[256,512]{1,0:T(8,128)(2,1)}, u32[]{:S(2)}, u32[]{:S(2)}) collective-permute-start(bf16[256,512]{1,0:T(8,128)(2,1)} %slice.137), channel_id=1, source_target_pairs={{0,8},{4,12},{8,0},{12,4},{1,9},{5,13},{9,1},{13,5},{2,10},{6,14},... | collective-permute-start | bytes 786440 | tf_op jit(solution)/shard_map/ppermute | solution.py:243
  92.6 16.0 %collective-permute-start.10 = (bf16[256,512]{1,0:T(8,128)(2,1)}, bf16[256,512]{1,0:T(8,128)(2,1)}, u32[]{:S(2)}, u32[]{:S(2)}) collective-permute-start(bf16[256,512]{1,0:T(8,128)(2,1)} %slice.138), channel_id=1, source_target_pairs={{0,4},{4,0},{8,12},{12,8},{1,5},{5,1},{9,13},{13,9},{2,6},{6,2},{1... | collective-permute-start | bytes 786440 | tf_op jit(solution)/shard_map/ppermute | solution.py:243
  97.9 38.0 %collective-permute-start.29 = (bf16[512,1024]{1,0:T(8,128)(2,1)}, bf16[512,1024]{1,0:T(8,128)(2,1)S(1)}, u32[]{:S(2)}, u32[]{:S(2)}) collective-permute-start(bf16[512,1024]{1,0:T(8,128)(2,1)} %constant_dynamic-slice_fusion), channel_id=1, source_target_pairs={{0,1},{1,0},{2,3},{3,2},{4,5},{5,4},{6,7},{7,6},{8,9},{9,8},{10,11... | collective-permute-start | bytes 3145736 | tf_op jit(solution)/shard_map/ppermute | solution.py:243
  139.4 46.4 %collective-permute-start.33 = (bf16[512,1024]{1,0:T(8,128)(2,1)}, bf16[512,1024]{1,0:T(8,128)(2,1)}, u32[]{:S(2)}, u32[]{:S(2)}) collective-permute-start(bf16[512,1024]{1,0:T(8,128)(2,1)} %collective-permute-done.32), channel_id=1, source_target_pairs={{1,0},{2,3},{5,4},{6,7},{9,8},{10,11},{13,12},{14,15},{17,16},{18,... | collective-permute-start | bytes 3145736 | tf_op jit(solution)/shard_map/ppermute | solution.py:256
  146.1 110.2 %collective-permute-start.30 = (bf16[512,512]{1,0:T(8,128)(2,1)}, bf16[512,512]{1,0:T(8,128)(2,1)}, u32[]{:S(2)}, u32[]{:S(2)}) collective-permute-start(bf16[512,512]{1,0:T(8,128)(2,1)} %get-tuple-element.36), channel_id=1, source_target_pairs={{0,4},{4,0},{8,12},{12,8},{1,5},{5,1},{9,13},{13,9},{2,6},{6,2},{1... | collective-permute-start | bytes 1572872 | tf_op jit(solution)/shard_map/ppermute | solution.py:243
  147.6 60.7 %collective-permute-start.37 = (bf16[512,1024]{1,0:T(8,128)(2,1)}, bf16[512,1024]{1,0:T(8,128)(2,1)}, u32[]{:S(2)}, u32[]{:S(2)}) collective-permute-start(bf16[512,1024]{1,0:T(8,128)(2,1)} %collective-permute-done.36), channel_id=1, source_target_pairs={{1,0},{2,3},{5,4},{6,7},{9,8},{10,11},{13,12},{14,15},{17,16},{18,... | collective-permute-start | bytes 3145736 | tf_op jit(solution)/shard_map/ppermute | solution.py:257
  170.0 19.8 %collective-permute-start.19 = (bf16[512,384]{1,0:T(8,128)(2,1)S(1)}, bf16[512,384]{1,0:T(8,128)(2,1)S(1)}, u32[]{:S(2)}, u32[]{:S(2)}) collective-permute-start(bf16[512,384]{1,0:T(8,128)(2,1)S(1)} %get-tuple-element.29), channel_id=1, source_target_pairs={{0,4},{4,0},{8,12},{12,8},{1,5},{5,1},{9,13},{13,9},{2,6},{6,2},{1... | collective-permute-start | bytes 1179656 | tf_op jit(solution)/shard_map/ppermute | solution.py:243
  170.6 20.7 %collective-permute-start.20 = (bf16[512,384]{1,0:T(8,128)(2,1)S(1)}, bf16[512,384]{1,0:T(8,128)(2,1)S(1)}, u32[]{:S(2)}, u32[]{:S(2)}) collective-permute-start(bf16[512,384]{1,0:T(8,128)(2,1)S(1)} %get-tuple-element.28), channel_id=1, source_target_pairs={{0,8},{4,12},{8,0},{12,4},{1,9},{5,13},{9,1},{13,5},{2,10},{6,14},... | collective-permute-start | bytes 1179656 | tf_op jit(solution)/shard_map/ppermute | solution.py:243
  189.8 68.0 %collective-permute-start.31 = (bf16[512,512]{1,0:T(8,128)(2,1)}, bf16[512,512]{1,0:T(8,128)(2,1)S(1)}, u32[]{:S(2)}, u32[]{:S(2)}) collective-permute-start(bf16[512,512]{1,0:T(8,128)(2,1)} %get-tuple-element.35), channel_id=1, source_target_pairs={{0,8},{4,12},{8,0},{12,4},{1,9},{5,13},{9,1},{13,5},{2,10},{6,14},... | collective-permute-start | bytes 1572872 | tf_op jit(solution)/shard_map/ppermute | solution.py:243
  214.8 35.6 %collective-permute-start.25 = (bf16[128,512]{1,0:T(8,128)(2,1)S(1)}, bf16[128,512]{1,0:T(8,128)(2,1)S(1)}, u32[]{:S(2)}, u32[]{:S(2)}) collective-permute-start(bf16[128,512]{1,0:T(8,128)(2,1)S(1)} %get-tuple-element.40), channel_id=1, source_target_pairs={{0,1},{1,0},{2,3},{3,2},{4,5},{5,4},{6,7},{7,6},{8,9},{9,8},{10,11... | collective-permute-start | bytes 393224 | tf_op jit(solution)/shard_map/ppermute | solution.py:243
  256.3 21.7 %collective-permute-start.39 = (bf16[512,512]{1,0:T(8,128)(2,1)}, bf16[512,512]{1,0:T(8,128)(2,1)S(1)}, u32[]{:S(2)}, u32[]{:S(2)}) collective-permute-start(bf16[512,512]{1,0:T(8,128)(2,1)} %get-tuple-element.31), channel_id=1, source_target_pairs={{0,8},{4,12},{8,0},{12,4},{1,9},{5,13},{9,1},{13,5},{2,10},{6,14},... | collective-permute-start | bytes 1572872 | tf_op jit(solution)/shard_map/ppermute | solution.py:243
  257.8 20.2 %collective-permute-start.28 = (bf16[128,2048]{1,0:T(8,128)(2,1)S(1)}, bf16[128,2048]{1,0:T(8,128)(2,1)}, u32[]{:S(2)}, u32[]{:S(2)}) collective-permute-start(bf16[128,2048]{1,0:T(8,128)(2,1)S(1)} %pad_maximum_fusion.1.own_ref), channel_id=1, source_target_pairs={{0,16},{16,0},{1,17},{17,1},{2,18},{18,2},{3,19},{19,3},{4,20},{20... | collective-permute-start | bytes 1572872 | tf_op jit(solution)/shard_map/ppermute | solution.py:243
  (54 other events, 529.3 us)

commit v2 on v0

--- a/solution.py
+++ b/solution.py
@@ -1,8 +1,12 @@
+import functools
 import math
 
 import jax
 import jax.numpy as jnp
+import numpy as np
 from jax import lax
+from jax.experimental import pallas as pl
+from jax.experimental.pallas import tpu as pltpu
 from jax.sharding import PartitionSpec as P
 
 HD = 128
@@ -76,7 +80,7 @@
     )
 
 
-def body(
+def generic_body(
     ids,
     block_order,
     embed,
@@ -214,9 +218,7 @@
             outputs.append(result)
         return tuple((jnp.stack([entry[field] for entry in outputs]) for field in range(3)))
 
-    top_final, sums_final, weighted_final = lax.fori_loop(
-        0, piece_len // sub_len, attend_sub, start_state
-    )
+    _, sums_final, weighted_final = lax.fori_loop(0, piece_len // sub_len, attend_sub, start_state)
     attended = (
         (weighted_final / sums_final[..., None])
         .astype(jnp.bfloat16)
@@ -231,7 +233,545 @@
     return stream_own + attn_own
 
 
+CODES = (65, 67, 71, 84)
+BF16 = jnp.bfloat16
+F32 = jnp.float32
+VM = pl.BlockSpec(memory_space=pltpu.VMEM)
+SM = pl.BlockSpec(memory_space=pltpu.SMEM)
+
+UNIT, CTX, PLANE, CROSS, HALF, OTHER = 0, 4, 8, 12, 13, 14
+MINE, THEIRS, SLOTS = 15, 17, 19
+
+
+def position_table():
+    rows = []
+    for half in range(2):
+        for ctx in range(4):
+            for plane in range(4):
+                units = [plane, (1, 0, 3, 2)[plane], (2, 2, 1, 1)[plane], (3, 3, 0, 0)[plane]]
+                row = units + [ctx ^ rel for rel in range(4)] + [plane ^ rel for rel in range(4)]
+                row += [(ctx & 1) ^ (ctx >> 1), half, 1 - half]
+                row += [2 * half, 2 * half + 1, 2 - 2 * half, 3 - 2 * half]
+                row += [2 * (ctx ^ rel) + at for rel in range(4) for at in range(2)]
+                rows.append(row)
+    return np.array(rows, np.int32)
+
+
+def swap(value, axis, mask):
+    size = lax.axis_size(axis)
+    return lax.ppermute(value, axis, [(at, at ^ mask) for at in range(size)])
+
+
+def rows_of(weights, lane_start, width):
+    return lax.dynamic_slice(weights, (0, lane_start), (weights.shape[0], width))
+
+
+def along_chain(piece, edge_plane):
+    middle = [(1, 2), (2, 1)]
+    outward = [(1, 0), (2, 3)]
+    near = swap(piece, "tensor", 1)
+    across = lax.ppermute(piece, "tensor", middle)
+    far_mid = lax.ppermute(near, "tensor", middle)
+    across_out = lax.ppermute(across, "tensor", outward)
+    far_out = lax.ppermute(far_mid, "tensor", outward)
+    return (
+        near,
+        jnp.where(edge_plane, across_out, across),
+        jnp.where(edge_plane, far_out, far_mid),
+    )
+
+
+def dot32(left, right):
+    return jnp.dot(left, right, preferred_element_type=F32)
+
+
+def hyena_kernel(where_ref, coef_ref, hot_ref, taps_ref, skip_ref, mix_ref):
+    hot = hot_ref[...]
+    first, second, third = (dot32(coef_ref[j], hot) for j in range(3))
+    gated = second * third
+    packed = gated.astype(BF16)
+    row = lax.broadcasted_iota(jnp.int32, (128, 128), 0)
+    lane = lax.broadcasted_iota(jnp.int32, (128, 128), 1)
+    near = lane >= row
+    mixed = []
+    for group in range(16):
+        spread = jnp.broadcast_to(taps_ref[group : group + 1, :], (128, 128))
+        rolled = pltpu.roll(spread, 0, 1, stride=1, stride_axis=0)
+        zero = jnp.zeros_like(rolled)
+        matrix = jnp.concatenate(
+            [jnp.where(near, zero, rolled), jnp.where(near, rolled, zero)], axis=0
+        ).astype(BF16)
+        chans = packed[16 * group : 16 * group + 16]
+        left = jnp.concatenate(
+            [chans[:, at : at + 256] for at in (0, 128, 384, 512)], axis=0
+        )
+        result = dot32(left, matrix)
+        mixed.append(jnp.concatenate([result[16 * i : 16 * i + 16] for i in range(4)], axis=1))
+    long_mix = jnp.concatenate(mixed, axis=0)
+    own_gate = jnp.concatenate([gated[:, 128:384], gated[:, 512:768]], axis=1)
+    own_first = jnp.concatenate([first[:, 128:384], first[:, 512:768]], axis=1)
+    mix = own_first * (long_mix + skip_ref[...] * own_gate)
+    mix_ref[...] = mix.T.astype(BF16)
+
+
+def hyena_mixes(where, coef, hot, taps, skip):
+    chans = coef.shape[1]
+    step = 256
+    return pl.pallas_call(
+        hyena_kernel,
+        grid_spec=pltpu.PrefetchScalarGridSpec(
+            num_scalar_prefetch=1,
+            grid=(chans // step,),
+            in_specs=[
+                pl.BlockSpec((3, step, coef.shape[2]), lambda i, w: (0, i, 0)),
+                pl.BlockSpec(hot.shape, lambda i, w: (0, 0)),
+                pl.BlockSpec((step // 16, 128), lambda i, w: (i, 0)),
+                pl.BlockSpec((step, 1), lambda i, w: (i, 0)),
+            ],
+            out_specs=pl.BlockSpec(
+                (512, step), lambda i, w: (0, w[PLANE + i // 2] * 2 + i % 2)
+            ),
+        ),
+        out_shape=jax.ShapeDtypeStruct((512, chans), BF16),
+        name="hyena_mix",
+    )(where, coef, hot, taps, skip)
+
+
+def both(own_ref, oth_ref):
+    return jnp.concatenate([own_ref[...], oth_ref[...]], axis=0)
+
+
+def branch_lane(where_ref, rel):
+    return pl.ds(pl.multiple_of(where_ref[CTX + rel] * 512, 512), 512)
+
+
+def branch_a_kernel(where_ref, own0, oth0, own1, oth1, own2, oth2, home_ref, *refs):
+    block1, block2, sum_ref = refs[:4], refs[4:8], refs[8]
+    left0, left1, left2 = both(own0, oth0), both(own1, oth1), both(own2, oth2)
+    rows = own0.shape[0]
+    for rel in range(4):
+        lane = branch_lane(where_ref, rel)
+        total = dot32(left0, home_ref[:, lane]) + dot32(left1, block1[rel][...])
+        total += dot32(left2, block2[rel][...])
+        sum_ref[0, :, lane] = total[:rows]
+        sum_ref[1, :, lane] = total[rows:]
+
+
+def branch_b_kernel(where_ref, own3, oth3, sum_ref, *refs):
+    block3, (own_ref, oth_ref) = refs[:4], refs[4:]
+    left3 = both(own3, oth3)
+    rows = own3.shape[0]
+    for rel in range(4):
+        lane = branch_lane(where_ref, rel)
+        total = dot32(left3, block3[rel][...])
+        own_ref[:, lane] = sum_ref[0, :, lane] + total[:rows]
+        oth_ref[:, lane] = (sum_ref[1, :, lane] + total[rows:]).astype(BF16)
+
+
+def hyena_branches(where, own_mix, oth_mix, home, parts):
+    tile = 256
+    grid = (512 // tile,)
+
+    def mixes(at):
+        return [pl.BlockSpec((tile, 512), lambda i, w: (i, w[UNIT + at]))] * 2
+
+    sums = pl.BlockSpec((2, tile, 2048), lambda i, w: (0, i, 0))
+    flat = pl.BlockSpec((tile, 2048), lambda i, w: (i, 0))
+    sum_shape = jax.ShapeDtypeStruct((2, 512, 2048), F32)
+    half_shapes = [
+        jax.ShapeDtypeStruct((512, 2048), F32),
+        jax.ShapeDtypeStruct((512, 2048), BF16),
+    ]
+
+    def call(kernel, in_specs, out_specs, out_shape, operands):
+        return pl.pallas_call(
+            kernel,
+            grid_spec=pltpu.PrefetchScalarGridSpec(
+                num_scalar_prefetch=1, grid=grid, in_specs=in_specs, out_specs=out_specs
+            ),
+            out_shape=out_shape,
+            name="hyena_branch",
+        )(where, *operands)
+
+    mix = [own_mix, oth_mix]
+    home_spec = pl.BlockSpec((512, 2048), lambda i, w: (0, w[HALF]))
+    partial = call(
+        branch_a_kernel,
+        mixes(0) + mixes(1) + mixes(2) + [home_spec] + [VM] * 8,
+        sums,
+        sum_shape,
+        mix * 3 + [home] + parts[0] + parts[1],
+    )
+    return call(
+        branch_b_kernel,
+        mixes(3) + [sums] + [VM] * 4,
+        [flat, flat],
+        half_shapes,
+        mix + [partial] + parts[2],
+    )
+
+
+def qkv_kernel(where_ref, half_ref, hot_ref, base_ref, gain_ref, proj_ref, *refs, first):
+    at = pl.program_id(0)
+    if first:
+        total_ref, power_ref, rows_ref, block_ref = refs
+    else:
+        part_ref, part_power_ref, cos_ref, sin_ref = refs[:4]
+        head_refs = refs[4:8]
+        rows_ref, total_ref, power_ref, block_ref = refs[8:]
+
+    @pl.when(at == 0)
+    def _():
+        if first:
+            total_ref[...] = jnp.zeros_like(total_ref)
+            power_ref[...] = jnp.zeros_like(power_ref)
+        else:
+            total_ref[...] = part_ref[...]
+            power_ref[...] = part_power_ref[...]
+
+    stream = dot32(hot_ref[...], base_ref[...]) + half_ref[...].astype(F32)
+    block_ref[...] = stream
+    rows_ref[...] = block_ref[pl.ds(pl.multiple_of(where_ref[PLANE] * 128, 128), 128), :]
+    power_ref[...] += jnp.sum(stream * stream, axis=1, keepdims=True)
+    scaled = (stream * gain_ref[...]).astype(BF16)
+    for j in range(3):
+        total_ref[:, 512 * j : 512 * j + 512] += dot32(scaled, proj_ref[j])
+    if first:
+        return
+
+    @pl.when(at == 1)
+    def _():
+        factor = lax.rsqrt(power_ref[...] * (1.0 / 4096.0) + EPS)
+        cosine = cos_ref[...] * factor
+        sine = sin_ref[...] * factor
+        for rel in range(4):
+            for j in range(3):
+                lane = pl.multiple_of(where_ref[CTX + rel] * 128 + 512 * j, 128)
+                piece = total_ref[:, pl.ds(lane, 128)]
+                if j < 2:
+                    piece = piece * cosine + pltpu.roll(piece, 64, 1) * sine
+                else:
+                    piece = piece * factor
+                head_refs[rel][:, 128 * j : 128 * j + 128] = piece.astype(BF16)
+
+
+def qkv_half(where, half, hot, base, gain, proj, extra=()):
+    first = not extra
+    at = MINE if first else THEIRS
+    whole = lambda shape: pl.BlockSpec(shape, lambda i, w: (0,) * len(shape))
+    in_specs = [
+        pl.BlockSpec((512, 1024), lambda i, w: (0, i)),
+        whole(hot.shape),
+        pl.BlockSpec((base.shape[0], 1024), lambda i, w: (0, w[at + i])),
+        pl.BlockSpec((1, 1024), lambda i, w: (0, w[at + i])),
+        pl.BlockSpec((3, 1024, 512), lambda i, w: (0, w[at + i], 0)),
+    ]
+    rows_spec = pl.BlockSpec((128, 1024), lambda i, w: (0, i))
+    rows_shape = jax.ShapeDtypeStruct((128, 2048), F32)
+    scratch = [pltpu.VMEM((512, 1024), F32)]
+    if first:
+        out_specs = [whole((512, 1536)), whole((512, 1)), rows_spec]
+        out_shape = [
+            jax.ShapeDtypeStruct((512, 1536), F32),
+            jax.ShapeDtypeStruct((512, 1), F32),
+            rows_shape,
+        ]
+    else:
+        in_specs += [whole(value.shape) for value in extra]
+        out_specs = [whole((512, 384))] * 4 + [rows_spec]
+        out_shape = [jax.ShapeDtypeStruct((512, 384), BF16)] * 4 + [rows_shape]
+        scratch = [pltpu.VMEM((512, 1536), F32), pltpu.VMEM((512, 1), F32)] + scratch
+    return pl.pallas_call(
+        functools.partial(qkv_kernel, first=first),
+        grid_spec=pltpu.PrefetchScalarGridSpec(
+            num_scalar_prefetch=1,
+            grid=(2,),
+            in_specs=in_specs,
+            out_specs=out_specs,
+            scratch_shapes=scratch,
+        ),
+        out_shape=out_shape,
+        name="qkv_half",
+    )(where, half, hot, base, gain, proj, *extra)
+
+
+def attend_kernel(slot_ref, *refs):
+    x_refs, out_refs, (q_ref, k_ref, v_ref, mixed_ref) = refs[:4], refs[4:8], refs[8:]
+    for rel, x_ref in enumerate(x_refs):
+        for half in range(2):
+            base = pl.multiple_of(slot_ref[2 * rel + half] * 256, 256)
+            rows = slice(256 * half, 256 * half + 256)
+            q_ref[pl.ds(base, 256), :] = x_ref[rows, 0:128]
+            k_ref[pl.ds(base, 256), :] = x_ref[rows, 128:256]
+            v_ref[pl.ds(base, 256), :] = x_ref[rows, 256:384]
+    row = lax.broadcasted_iota(jnp.int32, (256, 256), 0)
+    lane = lax.broadcasted_iota(jnp.int32, (256, 256), 1)
+    causal = lane <= row
+    scale = HD ** (-0.5)
+    for block in range(8):
+        width = 256 * block + 256
+        query = q_ref[256 * block : width, :]
+        scores = lax.dot_general(
+            query, k_ref[0:width, :], (((1,), (1,)), ((), ())), preferred_element_type=F32
+        )
+        last = jnp.where(causal, scores[:, width - 256 :], NEG_FILL)
+        if block > 0:
+            scores = jnp.concatenate([scores[:, : width - 256], last], axis=1)
+        else:
+            scores = last
+        top = jnp.max(scores, axis=1, keepdims=True)
+        weights = jnp.exp((scores - top) * scale)
+        total = jnp.sum(weights, axis=1, keepdims=True)
+        mixed = dot32(weights.astype(BF16), v_ref[0:width, :])
+        mixed_ref[256 * block : width, :] = (mixed / total).astype(BF16)
+    for rel, out_ref in enumerate(out_refs):
+        for half in range(2):
+            base = pl.multiple_of(slot_ref[2 * rel + half] * 256, 256)
+            out_ref[256 * half : 256 * half + 256, :] = mixed_ref[pl.ds(base, 256), :]
+
+
+def attend(slots, pieces):
+    return pl.pallas_call(
+        attend_kernel,
+        in_specs=[SM] + [VM] * 4,
+        out_specs=[VM] * 4,
+        out_shape=[jax.ShapeDtypeStruct((512, 128), BF16)] * 4,
+        scratch_shapes=[pltpu.VMEM((2048, 128), BF16)] * 4,
+        name="attend",
+    )(slots, *pieces)
+
+
+def out_kernel(where_ref, own_ref, oth_ref, rows_ref, home_ref, *refs):
+    parts, refs = refs[:9], refs[9:]
+    own_out_ref, oth_out_ref, left_ref, home_vm, *rest = refs
+    held, sem = rest[:9], rest[9]
+    lane = pl.multiple_of(where_ref[HALF] * 2048, 2048)
+    copies = [pltpu.make_async_copy(home_ref.at[:, pl.ds(lane, 2048)], home_vm, sem.at[9])]
+    copies += [
+        pltpu.make_async_copy(part, room, sem.at[at])
+        for at, (part, room) in enumerate(zip(parts, held))
+    ]
+    copies[0].start()
+    for kind in range(3):
+        for unit in range(3):
+            copies[1 + 3 * unit + kind].start()
+    for side, src_ref in enumerate((own_ref, oth_ref)):
+        for far in range(4):
+            for rel in range(4):
+                head = where_ref[PLANE + far] * 4 + where_ref[CTX + rel]
+                lane = pl.multiple_of(head * 128, 128)
+                at = 512 * far + 128 * rel
+                left_ref[128 * side : 128 * side + 128, pl.ds(lane, 128)] = src_ref[
+                    :, at : at + 128
+                ]
+
+    def left(unit):
+        return left_ref[:, pl.ds(pl.multiple_of(where_ref[UNIT + unit] * 512, 512), 512)]
+
+    lanes = []
+    copies[0].wait()
+    for quarter in range(4):
+        half = where_ref[CROSS] if quarter < 2 else 1 - where_ref[CROSS]
+        lanes.append(pl.multiple_of(half * 1024 + (quarter % 2) * 512, 512))
+        own_out_ref[:, pl.ds(lanes[quarter], 512)] = rows_ref[:, pl.ds(lanes[quarter], 512)]
+    for quarter in range(4):
+        for unit in range(3):
+            if quarter != 1:
+                copies[1 + 3 * unit + max(quarter - 1, 0)].wait()
+        total = dot32(left(0), home_vm[:, pl.ds(lanes[quarter], 512)])
+        for unit in range(3):
+            block, side_x, side_y = held[3 * unit : 3 * unit + 3]
+            if quarter < 2:
+                right = block[:, 512 * quarter : 512 * quarter + 512]
+            else:
+                right = (side_x, side_y)[quarter - 2][...]
+            total += dot32(left(unit + 1), right)
+        own_out_ref[:, pl.ds(lanes[quarter], 512)] += total[:128]
+        oth_out_ref[:, pl.ds(lanes[quarter], 512)] = total[128:].astype(oth_out_ref.dtype)
+
+
+def out_branches(where, own, oth, rows, home, parts):
+    anywhere = pl.BlockSpec(memory_space=pl.ANY)
+    flat = pl.BlockSpec((128, 2048), lambda i, w: (0, 0))
+    return pl.pallas_call(
+        out_kernel,
+        grid_spec=pltpu.PrefetchScalarGridSpec(
+            num_scalar_prefetch=1,
+            grid=(1,),
+            in_specs=[flat, flat, flat] + [anywhere] * (1 + len(parts)),
+            out_specs=[pl.BlockSpec((128, 2048), lambda i, w: (0, w[HALF])), flat],
+            scratch_shapes=[pltpu.VMEM((256, 2048), BF16), pltpu.VMEM((512, 2048), BF16)]
+            + [pltpu.VMEM(part.shape, BF16) for part in parts]
+            + [pltpu.SemaphoreType.DMA((10,))],
+        ),
+        out_shape=[jax.ShapeDtypeStruct((128, 4096), F32), jax.ShapeDtypeStruct((128, 2048), BF16)],
+        name="out_branch",
+    )(where, own, oth, rows, home, *parts)
+
+
+def join_kernel(where_ref, own_any, rows_ref, got_ref, out_ref):
+    out_ref[...] = rows_ref[...] + got_ref[...].astype(F32)
+
+
+def join_halves(where, own, rows, got):
+    piece = pl.BlockSpec((128, 1024), lambda i, w: (0, i))
+    return pl.pallas_call(
+        join_kernel,
+        grid_spec=pltpu.PrefetchScalarGridSpec(
+            num_scalar_prefetch=1,
+            grid=(2,),
+            in_specs=[pl.BlockSpec(memory_space=pl.ANY), piece, piece],
+            out_specs=pl.BlockSpec((128, 1024), lambda i, w: (0, w[OTHER] * 2 + i)),
+        ),
+        out_shape=jax.ShapeDtypeStruct((128, 4096), F32),
+        input_output_aliases={1: 0},
+        name="join_halves",
+    )(where, own, rows, got)
+
+
+def block_body(*operands):
+    return block_rows_out(*operands)
+
+
+def block_rows_out(
+    ids,
+    block_order,
+    embed,
+    mix_gain,
+    in_proj,
+    short_filter,
+    long_filter,
+    conv_skip,
+    hyena_out,
+    attn_gain,
+    qkv_proj,
+    attn_out,
+):
+    half_at = lax.axis_index("dp")
+    ctx = lax.axis_index("context")
+    plane = lax.axis_index("tensor")
+    edge = jnp.logical_or(plane == 0, plane == 3)
+    order = block_order.astype(jnp.int32)
+    half_lane = half_at * 2048
+    table_rows = jnp.asarray(position_table())
+    where = lax.dynamic_index_in_dim(
+        table_rows, half_at * 16 + ctx * 4 + plane, 0, keepdims=False
+    )
+
+    piece = rows_of(hyena_out, half_lane + ctx * 512, 512)
+    parts = []
+    for unit in along_chain(piece, edge):
+        parts.append(
+            [unit, swap(unit, "context", 1), swap(unit, "context", 2), swap(unit, "context", 3)]
+        )
+
+    own_row = ids.astype(F32).reshape(1, 128)
+    id_rows = jnp.concatenate(
+        [own_row] + [swap(own_row, "context", rel) for rel in range(1, 4)], axis=1
+    )
+
+    base = jnp.concatenate([embed[code : code + 1] for code in CODES], axis=0)
+    mixed_in = rms_scale(base, mix_gain)
+    table = jnp.einsum(
+        "rd,jdc->jrc", mixed_in, in_proj, preferred_element_type=F32
+    ).astype(BF16)
+    packed = jnp.concatenate(
+        [
+            table.astype(F32).reshape(12, 512),
+            short_filter.reshape(9, 512),
+            conv_skip.reshape(1, 512),
+            long_filter.reshape(8, 512),
+            id_rows,
+        ],
+        axis=0,
+    )
+    everything = jnp.stack([packed] + [swap(packed, "tensor", rel) for rel in range(1, 4)])
+    slot_ids = jnp.arange(8, dtype=jnp.int32)
+    place = jnp.sum(
+        jnp.where(where[SLOTS : SLOTS + 8, None] == slot_ids[None, :], order[None, :], 0), axis=1
+    )
+    owned = place[:2]
+    local_pos = (
+        owned[:, None] * 256 + jnp.arange(256, dtype=jnp.int32)[None, :]
+    ).reshape(512)
+    inverse_freq = THETA ** (-(2.0 * jnp.arange(64, dtype=F32)) / HD)
+    angles = local_pos.astype(F32)[:, None] * inverse_freq[None, :]
+    cosine = jnp.cos(angles)
+    sine = jnp.sin(angles)
+    cosine = jnp.concatenate([cosine, cosine], axis=1)
+    sine = jnp.concatenate([-sine, sine], axis=1)
+    which = where[None, PLANE : PLANE + 4] == jnp.arange(4, dtype=jnp.int32)[:, None]
+    plane_ids = everything[:, 30].reshape(1, 4, 4, 128)
+    plane_ids = jnp.sum(jnp.where(which[:, :, None, None], plane_ids, 0.0), axis=1)
+    all_ids = plane_ids.transpose(1, 0, 2).reshape(8, 256)
+    tables = everything[:, :12].reshape(4, 3, 1, 4, 512)
+    shorts = everything[:, 12:21].reshape(4, 3, 3, 1, 512)
+    coef = (tables * shorts).transpose(1, 0, 4, 2, 3).reshape(3, 2048, 12)
+    coarse = lax.reduce_precision(coef, 8, 7)
+    coef = jnp.concatenate([coarse, coef - coarse], axis=2).astype(BF16)
+    skip = everything[:, 21].reshape(2048, 1)
+    taps = everything[:, 22:30].reshape(128, 128)
+
+    before_hit = place[None, :] == owned[:, None] - 1
+    own_ids = all_ids[:2]
+    before_ids = jnp.sum(jnp.where(before_hit[:, :, None], all_ids[None], 0.0), axis=1)
+    span = jnp.concatenate([before_ids, own_ids], axis=1)
+    codes = jnp.array(CODES, F32)
+    hot = jnp.stack(
+        [
+            (span[None, :, 128 - lag : 512 - lag] == codes[:, None, None]).astype(BF16)
+            for lag in range(3)
+        ]
+    ).reshape(12, 768)
+    hot = jnp.concatenate([hot, hot], axis=0)
+    own_hot = (own_ids.reshape(512, 1) == codes[None, :]).astype(BF16)
+    coef, hot, place, cosine, sine, own_hot, base = lax.optimization_barrier(
+        (coef, hot, place, cosine, sine, own_hot, base)
+    )
+
+    own_mix = hyena_mixes(where, coef, hot, taps, skip)
+    oth_mix = swap(own_mix, "dp", 1)
+
+    own_half, give_half = hyena_branches(where, own_mix, oth_mix, hyena_out, parts)
+    got_half = swap(give_half, "dp", 1)
+    gain = attn_gain[None]
+    total, power, own_rows = qkv_half(where, own_half, own_hot, base, gain, qkv_proj)
+    *heads, oth_rows = qkv_half(
+        where, got_half, own_hot, base, gain, qkv_proj, (total, power, cosine, sine)
+    )
+
+    pieces = [heads[0]] + [swap(heads[rel], "context", rel) for rel in range(1, 4)]
+    attended = attend(place, pieces)
+    mine = jnp.concatenate(
+        [attended[0]]
+        + [swap(attended[rel], "context", rel) for rel in range(1, 4)],
+        axis=1,
+    ).reshape(4, 128, 512)
+
+    def rows_for(rel):
+        return lax.dynamic_index_in_dim(mine, plane ^ rel, 0, keepdims=False)
+
+    own_att = jnp.concatenate(
+        [rows_for(0)] + [swap(rows_for(rel), "tensor", rel) for rel in range(1, 4)],
+        axis=1,
+    )
+    oth_att = swap(own_att, "dp", 1)
+
+    cross = (ctx & 1) ^ (ctx >> 1)
+    late_lane, _ = lax.optimization_barrier((half_lane + cross * 1024, coef))
+    units = along_chain(rows_of(attn_out, late_lane, 1024), edge)
+    parts = []
+    for unit in units:
+        parts += [unit, swap(unit[:, :512], "context", 1), swap(unit[:, 512:], "context", 2)]
+    own_out, give_out = out_branches(where, own_att, oth_att, own_rows, attn_out, parts)
+    got_out = swap(give_out, "dp", 1)
+    return join_halves(where, own_out, oth_rows, got_out)
+
+
 def solution(mesh):
+    grid_shape = dict(mesh.shape)
+    square = (grid_shape["dp"], grid_shape["context"], grid_shape["tensor"]) == (2, 4, 4)
+    body = block_body if square else generic_body
     placed = (
         P(("dp", "context", "tensor")),
         P("dp"),

time: 807 us -> 298 us (0.37)
  waiting for transfers between devices: 521 us -> 98.1 us
  local copies, waits for them, and re-layouts: 157 us -> 19.8 us
  starting transfers between devices: 0.25 us -> 88.1 us
  Pallas kernels: 0 us -> 70.3 us
  matrix products: 72.5 us -> 6.37 us
  other arithmetic: 31.7 us -> 12.8 us
  between operations: 15.5 us -> 0.62 us
    all_gather x5 -> x0, waiting for transfers between devices: 301 us -> none  [the longest x1 150 us: body(): stream_all = lax.all_gather(stream_own, 'tensor', axis=0, tiled=True)]
    reduce_scatter x2 -> x0, waiting for transfers between devices: 220 us -> none  [the longest x1 143 us: body(): lax.psum_scatter(jnp.dot(hyena_mix, hyena_out, preferred_element_type=jnp...]
    gather x4 -> x0, local copies, waits for them, and re-layouts: 122 us -> none  [the longest x2 61.2 us: toeplitz(): jnp.take(long_filter, jnp.clip(tap_lag + filter_len, 0, filter_len - 1),...]
    ppermute x0 -> x44, waiting for transfers between devices: none -> 98.1 us  [the longest x36 64.1 us: swap(): return lax.ppermute(value, axis, [(at, at ^ mask) for at in range(size)])]
    ppermute x0 -> x44, starting transfers between devices: none -> 88.1 us  [the longest x36 77.3 us: swap(): return lax.ppermute(value, axis, [(at, at ^ mask) for at in range(size)])]
    pallas_call x0 -> x8, Pallas kernels: none -> 70.3 us  [the longest x2 21.3 us: call(): pl.pallas_call(kernel, grid_spec=pltpu.PrefetchScalarGridSpec(num_scalar_...]
    dot_general x27 -> x1, matrix products: 72.5 us -> 6.37 us  [block_rows_out(): jnp.einsum('rd,jdc->jrc', mixed_in, in_proj, preferred_element_type=F32)]
    slice x20 -> x10, local copies, waits for them, and re-layouts: 21 us -> 3.46 us  [the longest x3 2.31 us: block_rows_out(): unit[:, 512:]]
  transfers between devices with their start and end apart: 7 -> 44, of which waited for: 6 -> 17; matrix products, arithmetic and copies ran while one was open for 16% -> 11% of each run, Pallas kernels for 0% -> 20%
where the time goes in v2:
time: 298 us; the launch traced here: 296 us
  waiting for transfers between devices  98.1 us (33%)
  starting transfers between devices  88.1 us (30%)
  Pallas kernels  70.3 us (24%)
  local copies, waits for them, and re-layouts  19.8 us (7%)
  other arithmetic  12.8 us (4%)
  matrix products  6.37 us (2%)
    ppermute x36, starting transfers between devices, swap(): return lax.ppermute(value, axis, [(at, at ^ mask) for at in range(size)])  77.3 us
    ppermute x36, waiting for transfers between devices, swap(): return lax.ppermute(value, axis, [(at, at ^ mask) for at in range(size)])  64.1 us
    ppermute x2, waiting for transfers between devices, along_chain(): across_out = lax.ppermute(across, 'tensor', outward)  32.1 us
    pallas_call x2, Pallas kernels, call(): pl.pallas_call(kernel, grid_spec=pltpu.PrefetchScalarGridSpec(num_scalar_...  21.3 us
    pallas_call x2, Pallas kernels, qkv_half(): pl.pallas_call(functools.partial(qkv_kernel, first=first), grid_spec=pltp...  20.4 us
    pallas_call x1, Pallas kernels, hyena_mixes(): pl.pallas_call(hyena_kernel, grid_spec=pltpu.PrefetchScalarGridSpec(num_s...  9.88 us
    pallas_call x1, Pallas kernels, out_branches(): pl.pallas_call(out_kernel, grid_spec=pltpu.PrefetchScalarGridSpec(num_sca...  8.79 us
    unnamed x57, local copies, waits for them, and re-layouts  7.32 us
  transfers between devices with their start and end apart: 44, of which 17 were waited for; matrix products, arithmetic and copies ran while one was open for 11% of the time, Pallas kernels for 20%

profile of v2, /device:TPU:0, one launch (start us, length us, event | category | flops | bytes accessed | tf_op | source)
XLA Modules:
  0.0 296.1 jit_solution(8907967199033132216)
XLA Ops:
  0.7 3.0 %collective-permute-start = (f32[1,128]{1,0:T(1,128)S(1)}, f32[1,128]{1,0:T(1,128)S(1)}, u32[]{:S(2)}, u32[]{:S(2)}) collective-permute-start(f32[1,128]{1,0:T(1,128)S(1)} %convert_bitcast_fusion.1), channel_id=1, source_target_pairs={{0,4},{4,0},{8,12},{12,8},{1,5},{5,1},{9,13},{13,9},{2,6},{6,2},{1... | collective-permute-start | bytes 1544 | tf_op jit(solution)/shard_map/ppermute | solution.py:262
  7.7 4.9 %collective-permute-start.7 = (bf16[512,512]{1,0:T(8,128)(2,1)}, bf16[512,512]{1,0:T(8,128)(2,1)S(1)}, u32[]{:S(2)}, u32[]{:S(2)}) collective-permute-start(bf16[512,512]{1,0:T(8,128)(2,1)} %constant_dynamic-slice_fusion), channel_id=1, source_target_pairs={{0,1},{1,0},{2,3},{3,2},{4,5},{5,4},{6,7},{7,6},{8,9},{9,8},{10,11... | collective-permute-start | bytes 1572872 | tf_op jit(solution)/shard_map/ppermute | solution.py:262
  17.3 6.4 %fusion.1 = f32[3,4,512]{2,1,0:T(4,128)S(1)} fusion(bf16[3,4096,512]{2,1,0:T(8,128)(2,1)} %param.18, bf16[4,4096]{1,0:T(4,128)(2,1)S(1)} %get-tuple-element.34.base_ref, f32[4096]{0:T(1024)} %param.17, f32[4]{0:T(128)S(1)} %add_rsqrt_fusion), kind=kOutput, calls=%fused_computation.2 | convolution fusion | flops 50409472 | bytes 12656656 | tf_op jit(solution)/shard_map/rd,jdc->jrc/dot_general | solution.py:675
  38.4 9.9 %hyena_mix.1.own0.own1.own2.own3 = bf16[512,2048]{1,0:T(8,128)(2,1)} custom-call(s32[27]{0:T(128)} %get-tuple-element.74.where_ref, bf16[3,2048,24]{2,1,0:T(8,128)(2,1)} %copy.46.coef_ref, bf16[24,768]{1,0:T(8,128)(2,1)} %add_convert_fusion.hot_ref, f32[128,128]{1,0:T(8,128)} %reshape.160.taps_ref, f32[2048,1]{1,0:T(8,128)} %bitcast.52), custom_call_target="tpu_custom_call" | custom-call | tf_op jit(solution)/shard_map/hyena_mix/pallas_call | solution.py:320
  55.4 10.7 %collective-permute-done.12 = bf16[512,512]{1,0:T(8,128)(2,1)} collective-permute-done((bf16[512,512]{1,0:T(8,128)(2,1)S(1)}, bf16[512,512]{1,0:T(8,128)(2,1)}, u32[]{:S(2)}, u32[]{:S(2)}) %collective-permute-start.12) | collective-permute-done | bytes 524320 | tf_op jit(solution)/shard_map/ppermute | solution.py:275
  70.3 7.9 %collective-permute-done.8.refs_1_ = bf16[512,512]{1,0:T(8,128)(2,1)} collective-permute-done((bf16[512,512]{1,0:T(8,128)(2,1)S(1)}, bf16[512,512]{1,0:T(8,128)(2,1)}, u32[]{:S(2)}, u32[]{:S(2)}) %collective-permute-start.8) | collective-permute-done | bytes 524320 | tf_op jit(solution)/shard_map/ppermute | solution.py:262
  83.6 5.8 %collective-permute-done.13.refs_5_ = bf16[512,512]{1,0:T(8,128)(2,1)} collective-permute-done((bf16[512,512]{1,0:T(8,128)(2,1)S(1)}, bf16[512,512]{1,0:T(8,128)(2,1)}, u32[]{:S(2)}, u32[]{:S(2)}) %collective-permute-start.13) | collective-permute-done | bytes 524320 | tf_op jit(solution)/shard_map/ppermute | solution.py:262
  90.0 14.4 %collective-permute-done.14.refs_6_ = bf16[512,512]{1,0:T(8,128)(2,1)} collective-permute-done((bf16[512,512]{1,0:T(8,128)(2,1)S(1)}, bf16[512,512]{1,0:T(8,128)(2,1)}, u32[]{:S(2)}, u32[]{:S(2)}) %collective-permute-start.14) | collective-permute-done | bytes 524320 | tf_op jit(solution)/shard_map/ppermute | solution.py:262
  105.8 2.9 constant_dynamic-slice_fusion.1
  112.1 13.1 %hyena_branch.2.sum_ref = f32[2,512,2048]{2,1,0:T(8,128)} custom-call(s32[27]{0:T(128)} %get-tuple-element.74.where_ref, bf16[512,2048]{1,0:T(8,128)(2,1)} %hyena_mix.1.own0.own1.own2.own3, bf16[512,2048]{1,0:T(8,128)(2,1)} %copy-done, bf16[512,2048]{1,0:T(8,128)(2,1)} %hyena_mix.1.own0.own1.own2.own3, bf16[512,2048]{1,0:T(8,128)(2,1)} %copy-done, ...), custom_call_target="tpu_custom_call" | custom-call | tf_op jit(solution)/shard_map/hyena_branch/pallas_call | solution.py:387
  125.2 8.2 %hyena_branch.3 = (f32[512,2048]{1,0:T(8,128)}, bf16[512,2048]{1,0:T(8,128)(2,1)}) custom-call(s32[27]{0:T(128)} %get-tuple-element.74.where_ref, bf16[512,2048]{1,0:T(8,128)(2,1)} %hyena_mix.1.own0.own1.own2.own3, bf16[512,2048]{1,0:T(8,128)(2,1)} %copy-done, f32[2,512,2048]{2,1,0:T(8,128)} %hyena_branch.2.sum_ref, ...), custom_call_target="tpu_custom_call" | custom-call | tf_op jit(solution)/shard_map/hyena_branch/pallas_call | solution.py:387
  141.9 9.4 %qkv_half.2 = (f32[512,1536]{1,0:T(8,128)}, f32[512,1]{1,0:T(8,128)}, f32[128,2048]{1,0:T(8,128)}) custom-call(s32[27]{0:T(128)} %get-tuple-element.74.where_ref, f32[512,2048]{1,0:T(8,128)} %get-tuple-element.35.half_ref, bf16[512,4]{1,0:T(8,128)(2,1)} %compare_convert_fusion.hot_ref, bf16[4,4096]{1,0:T(4,128)(2,1)} %copy-done.8, f32[1,4096]{1,0:T(1,128)} %bitcast.61, ...), custom_call_target="tpu_custom_call" | custom-call | tf_op jit(solution)/shard_map/qkv_half/pallas_call | solution.py:484
  152.7 11.0 %qkv_half.3 = (bf16[512,384]{1,0:T(8,128)(2,1)}, bf16[512,384]{1,0:T(8,128)(2,1)}, bf16[512,384]{1,0:T(8,128)(2,1)}, bf16[512,384]{1,0:T(8,128)(2,1)}, f32[128,2048]{1,0:T(8,128)}) custom-call(s32[27]{0:T(128)} %get-tuple-element.74.where_ref, bf16[512,2048]{1,0:T(8,128)(2,1)} %copy-done.5, bf16[512,4]{1,0:T(8,128)(2,1)} %compare_convert_fusion.hot_ref, ...), custom_call_target="tpu_custom_call" | custom-call | tf_op jit(solution)/shard_map/qkv_half/pallas_call | solution.py:484
  166.9 21.5 %collective-permute-done.36 = bf16[512,1024]{1,0:T(8,128)(2,1)} collective-permute-done((bf16[512,1024]{1,0:T(8,128)(2,1)}, bf16[512,1024]{1,0:T(8,128)(2,1)}, u32[]{:S(2)}, u32[]{:S(2)}) %collective-permute-start.36) | collective-permute-done | bytes 1048608 | tf_op jit(solution)/shard_map/ppermute | solution.py:275
  193.9 5.3 %collective-permute-done.24.refs_3_ = bf16[512,384]{1,0:T(8,128)(2,1)S(1)} collective-permute-done((bf16[512,384]{1,0:T(8,128)(2,1)}, bf16[512,384]{1,0:T(8,128)(2,1)S(1)}, u32[]{:S(2)}, u32[]{:S(2)}) %collective-permute-start.24) | collective-permute-done | bytes 393248 | tf_op jit(solution)/shard_map/ppermute | solution.py:262
  200.0 7.1 %attend.1 = (bf16[512,128]{1,0:T(8,128)(2,1)}, bf16[512,128]{1,0:T(8,128)(2,1)}, bf16[512,128]{1,0:T(8,128)(2,1)}, bf16[512,128]{1,0:T(8,128)(2,1)}) custom-call(s32[8]{0:T(128)} %copy-done.25, bf16[512,384]{1,0:T(8,128)(2,1)} %get-tuple-element.40.refs_0_, bf16[512,384]{1,0:T(8,128)(2,1)} %copy-done.18, bf16[512,384]{1,0:T(8,128)(2,1)} %copy-done.19, ...), custom_call_target="tpu_custom_call" | custom-call | tf_op jit(solution)/shard_map/attend/pallas_call | solution.py:534
  213.7 3.2 %collective-permute-done.27 = bf16[512,128]{1,0:T(8,128)(2,1)S(1)} collective-permute-done((bf16[512,128]{1,0:T(8,128)(2,1)}, bf16[512,128]{1,0:T(8,128)(2,1)S(1)}, u32[]{:S(2)}, u32[]{:S(2)}) %collective-permute-start.27) | collective-permute-done | bytes 131104 | tf_op jit(solution)/shard_map/ppermute | solution.py:262
  218.0 32.8 %collective-permute-start.28 = (bf16[128,512]{1,0:T(8,128)(2,1)S(1)}, bf16[128,512]{1,0:T(8,128)(2,1)S(1)}, u32[]{:S(2)}, u32[]{:S(2)}) collective-permute-start(bf16[128,512]{1,0:T(8,128)(2,1)S(1)} %get-tuple-element.68), channel_id=1, source_target_pairs={{0,1},{1,0},{2,3},{3,2},{4,5},{5,4},{6,7},{7,6},{8,9},{9,8},{10,11... | collective-permute-start | bytes 393224 | tf_op jit(solution)/shard_map/ppermute | solution.py:262
  255.4 5.1 %collective-permute-done.29 = bf16[128,512]{1,0:T(8,128)(2,1)S(1)} collective-permute-done((bf16[128,512]{1,0:T(8,128)(2,1)S(1)}, bf16[128,512]{1,0:T(8,128)(2,1)S(1)}, u32[]{:S(2)}, u32[]{:S(2)}) %collective-permute-start.29) | collective-permute-done | bytes 131104 | tf_op jit(solution)/shard_map/ppermute | solution.py:262
  264.2 4.9 %collective-permute-done.37.refs_4_ = bf16[512,512]{1,0:T(8,128)(2,1)S(1)} collective-permute-done((bf16[512,512]{1,0:T(8,128)(2,1)}, bf16[512,512]{1,0:T(8,128)(2,1)S(1)}, u32[]{:S(2)}, u32[]{:S(2)}) %collective-permute-start.37) | collective-permute-done | bytes 524320 | tf_op jit(solution)/shard_map/ppermute | solution.py:262
  269.1 5.1 %collective-permute-done.38.refs_5_ = bf16[512,512]{1,0:T(8,128)(2,1)S(1)} collective-permute-done((bf16[512,512]{1,0:T(8,128)(2,1)S(1)}, bf16[512,512]{1,0:T(8,128)(2,1)S(1)}, u32[]{:S(2)}, u32[]{:S(2)}) %collective-permute-start.38) | collective-permute-done | bytes 524320 | tf_op jit(solution)/shard_map/ppermute | solution.py:262
  274.8 5.1 %collective-permute-done.42.refs_8_ = bf16[512,512]{1,0:T(8,128)(2,1)S(1)} collective-permute-done((bf16[512,512]{1,0:T(8,128)(2,1)S(1)}, bf16[512,512]{1,0:T(8,128)(2,1)S(1)}, u32[]{:S(2)}, u32[]{:S(2)}) %collective-permute-start.42) | collective-permute-done | bytes 524320 | tf_op jit(solution)/shard_map/ppermute | solution.py:262
  281.5 8.8 %out_branch.1 = (f32[128,4096]{1,0:T(8,128)}, bf16[128,2048]{1,0:T(8,128)(2,1)}) custom-call(s32[27]{0:T(128)} %get-tuple-element.74.where_ref, bf16[128,2048]{1,0:T(8,128)(2,1)} %copy-done.6, bf16[128,2048]{1,0:T(8,128)(2,1)} %copy-done.14, f32[128,2048]{1,0:T(8,128)} %get-tuple-element.48.rows_ref, bf16[512,4096]{1,0:T(8,128)(2,1)} %home_ref.3, ...), custom_call_target="tpu_custom_call" | custom-call | tf_op jit(solution)/shard_map/out_branch/pallas_call | solution.py:596
  293.3 2.9 join_halves.1
  (190 shorter events, 86.3 us)
Async XLA Ops:
  0.7 23.1 %collective-permute-start = (f32[1,128]{1,0:T(1,128)S(1)}, f32[1,128]{1,0:T(1,128)S(1)}, u32[]{:S(2)}, u32[]{:S(2)}) collective-permute-start(f32[1,128]{1,0:T(1,128)S(1)} %convert_bitcast_fusion.1), channel_id=1, source_target_pairs={{0,4},{4,0},{8,12},{12,8},{1,5},{5,1},{9,13},{13,9},{2,6},{6,2},{1... | collective-permute-start | bytes 1544 | tf_op jit(solution)/shard_map/ppermute | solution.py:262
  3.6 20.2 %collective-permute-start.1 = (f32[1,128]{1,0:T(1,128)S(1)}, f32[1,128]{1,0:T(1,128)S(1)}, u32[]{:S(2)}, u32[]{:S(2)}) collective-permute-start(f32[1,128]{1,0:T(1,128)S(1)} %convert_bitcast_fusion.1), channel_id=1, source_target_pairs={{0,8},{4,12},{8,0},{12,4},{1,9},{5,13},{9,1},{13,5},{2,10},{6,14},... | collective-permute-start | bytes 1544 | tf_op jit(solution)/shard_map/ppermute | solution.py:262
  5.1 18.7 %collective-permute-start.2 = (f32[1,128]{1,0:T(1,128)S(1)}, f32[1,128]{1,0:T(1,128)S(1)}, u32[]{:S(2)}, u32[]{:S(2)}) collective-permute-start(f32[1,128]{1,0:T(1,128)S(1)} %convert_bitcast_fusion.1), channel_id=1, source_target_pairs={{0,12},{4,8},{8,4},{12,0},{1,13},{5,9},{9,5},{13,1},{2,14},{6,10},... | collective-permute-start | bytes 1544 | tf_op jit(solution)/shard_map/ppermute | solution.py:262
  7.0 42.8 %collective-permute-start.11 = (bf16[512,512]{1,0:T(8,128)(2,1)}, bf16[512,512]{1,0:T(8,128)(2,1)S(1)}, u32[]{:S(2)}, u32[]{:S(2)}) collective-permute-start(bf16[512,512]{1,0:T(8,128)(2,1)} %constant_dynamic-slice_fusion), channel_id=1, source_target_pairs={{1,2},{2,1},{5,6},{6,5},{9,10},{10,9},{13,14},{14,13},{17,18},{18,... | collective-permute-start | bytes 1572872 | tf_op jit(solution)/shard_map/ppermute | solution.py:273
  7.7 40.6 %collective-permute-start.7 = (bf16[512,512]{1,0:T(8,128)(2,1)}, bf16[512,512]{1,0:T(8,128)(2,1)S(1)}, u32[]{:S(2)}, u32[]{:S(2)}) collective-permute-start(bf16[512,512]{1,0:T(8,128)(2,1)} %constant_dynamic-slice_fusion), channel_id=1, source_target_pairs={{0,1},{1,0},{2,3},{3,2},{4,5},{5,4},{6,7},{7,6},{8,9},{9,8},{10,11... | collective-permute-start | bytes 1572872 | tf_op jit(solution)/shard_map/ppermute | solution.py:262
  48.3 62.5 %collective-permute-start.6 = (bf16[512,2048]{1,0:T(8,128)(2,1)}, bf16[512,2048]{1,0:T(8,128)(2,1)S(1)}, u32[]{:S(2)}, u32[]{:S(2)}) collective-permute-start(bf16[512,2048]{1,0:T(8,128)(2,1)} %hyena_mix.1.own0.own1.own2.own3), channel_id=1, source_target_pairs={{0,16},{16,0},{1,17},{17,1},{2,18},{18,2},{3,19},{19,3},{4,20},{20... | collective-permute-start | bytes 6291464 | tf_op jit(solution)/shard_map/ppermute | solution.py:262
  51.1 17.7 %collective-permute-start.10 = (bf16[512,512]{1,0:T(8,128)(2,1)S(1)}, bf16[512,512]{1,0:T(8,128)(2,1)}, u32[]{:S(2)}, u32[]{:S(2)}) collective-permute-start(bf16[512,512]{1,0:T(8,128)(2,1)S(1)} %collective-permute-done.7.refs_0_), channel_id=1, source_target_pairs={{0,12},{4,8},{8,4},{12,0},{1,13},{5,9},{9,5},{13,1},{2,14},{6,10},... | collective-permute-start | bytes 1572872 | tf_op jit(solution)/shard_map/ppermute | solution.py:262
  53.6 24.6 %collective-permute-start.8 = (bf16[512,512]{1,0:T(8,128)(2,1)S(1)}, bf16[512,512]{1,0:T(8,128)(2,1)}, u32[]{:S(2)}, u32[]{:S(2)}) collective-permute-start(bf16[512,512]{1,0:T(8,128)(2,1)S(1)} %collective-permute-done.7.refs_0_), channel_id=1, source_target_pairs={{0,4},{4,0},{8,12},{12,8},{1,5},{5,1},{9,13},{13,9},{2,6},{6,2},{1... | collective-permute-start | bytes 1572872 | tf_op jit(solution)/shard_map/ppermute | solution.py:262
  54.1 24.6 %collective-permute-start.17 = (bf16[512,512]{1,0:T(8,128)(2,1)}, bf16[512,512]{1,0:T(8,128)(2,1)}, u32[]{:S(2)}, u32[]{:S(2)}) collective-permute-start(bf16[512,512]{1,0:T(8,128)(2,1)} %collective-permute-done.16), channel_id=1, source_target_pairs={{1,0},{2,3},{5,4},{6,7},{9,8},{10,11},{13,12},{14,15},{17,16},{18,... | collective-permute-start | bytes 1572872 | tf_op jit(solution)/shard_map/ppermute | solution.py:276
  68.8 20.7 %collective-permute-start.13 = (bf16[512,512]{1,0:T(8,128)(2,1)S(1)}, bf16[512,512]{1,0:T(8,128)(2,1)}, u32[]{:S(2)}, u32[]{:S(2)}) collective-permute-start(bf16[512,512]{1,0:T(8,128)(2,1)S(1)} %broadcast_select_fusion.3.refs_4_), channel_id=1, source_target_pairs={{0,4},{4,0},{8,12},{12,8},{1,5},{5,1},{9,13},{13,9},{2,6},{6,2},{1... | collective-permute-start | bytes 1572872 | tf_op jit(solution)/shard_map/ppermute | solution.py:262
  78.3 26.1 %collective-permute-start.14 = (bf16[512,512]{1,0:T(8,128)(2,1)S(1)}, bf16[512,512]{1,0:T(8,128)(2,1)}, u32[]{:S(2)}, u32[]{:S(2)}) collective-permute-start(bf16[512,512]{1,0:T(8,128)(2,1)S(1)} %broadcast_select_fusion.3.refs_4_), channel_id=1, source_target_pairs={{0,8},{4,12},{8,0},{12,4},{1,9},{5,13},{9,1},{13,5},{2,10},{6,14},... | collective-permute-start | bytes 1572872 | tf_op jit(solution)/shard_map/ppermute | solution.py:262
  78.8 30.0 %collective-permute-start.15 = (bf16[512,512]{1,0:T(8,128)(2,1)S(1)}, bf16[512,512]{1,0:T(8,128)(2,1)}, u32[]{:S(2)}, u32[]{:S(2)}) collective-permute-start(bf16[512,512]{1,0:T(8,128)(2,1)S(1)} %broadcast_select_fusion.3.refs_4_), channel_id=1, source_target_pairs={{0,12},{4,8},{8,4},{12,0},{1,13},{5,9},{9,5},{13,1},{2,14},{6,10},... | collective-permute-start | bytes 1572872 | tf_op jit(solution)/shard_map/ppermute | solution.py:262
  83.1 42.1 %collective-permute-start.18 = (bf16[512,512]{1,0:T(8,128)(2,1)}, bf16[512,512]{1,0:T(8,128)(2,1)}, u32[]{:S(2)}, u32[]{:S(2)}) collective-permute-start(bf16[512,512]{1,0:T(8,128)(2,1)} %broadcast_select_fusion.2.refs_0_), channel_id=1, source_target_pairs={{0,4},{4,0},{8,12},{12,8},{1,5},{5,1},{9,13},{13,9},{2,6},{6,2},{1... | collective-permute-start | bytes 1572872 | tf_op jit(solution)/shard_map/ppermute | solution.py:262
  89.5 35.7 %collective-permute-start.19 = (bf16[512,512]{1,0:T(8,128)(2,1)}, bf16[512,512]{1,0:T(8,128)(2,1)}, u32[]{:S(2)}, u32[]{:S(2)}) collective-permute-start(bf16[512,512]{1,0:T(8,128)(2,1)} %broadcast_select_fusion.2.refs_0_), channel_id=1, source_target_pairs={{0,8},{4,12},{8,0},{12,4},{1,9},{5,13},{9,1},{13,5},{2,10},{6,14},... | collective-permute-start | bytes 1572872 | tf_op jit(solution)/shard_map/ppermute | solution.py:262
  104.4 20.8 %collective-permute-start.20 = (bf16[512,512]{1,0:T(8,128)(2,1)}, bf16[512,512]{1,0:T(8,128)(2,1)}, u32[]{:S(2)}, u32[]{:S(2)}) collective-permute-start(bf16[512,512]{1,0:T(8,128)(2,1)} %broadcast_select_fusion.2.refs_0_), channel_id=1, source_target_pairs={{0,12},{4,8},{8,4},{12,0},{1,13},{5,9},{9,5},{13,1},{2,14},{6,10},... | collective-permute-start | bytes 1572872 | tf_op jit(solution)/shard_map/ppermute | solution.py:262
  108.7 26.4 %collective-permute-start.32 = (bf16[512,1024]{1,0:T(8,128)(2,1)}, bf16[512,1024]{1,0:T(8,128)(2,1)S(1)}, u32[]{:S(2)}, u32[]{:S(2)}) collective-permute-start(bf16[512,1024]{1,0:T(8,128)(2,1)} %constant_dynamic-slice_fusion.1), channel_id=1, source_target_pairs={{0,1},{1,0},{2,3},{3,2},{4,5},{5,4},{6,7},{7,6},{8,9},{9,8},{10,11... | collective-permute-start | bytes 3145736 | tf_op jit(solution)/shard_map/ppermute | solution.py:262
  133.4 17.9 %collective-permute-start.21 = (bf16[512,2048]{1,0:T(8,128)(2,1)}, bf16[512,2048]{1,0:T(8,128)(2,1)S(1)}, u32[]{:S(2)}, u32[]{:S(2)}) collective-permute-start(bf16[512,2048]{1,0:T(8,128)(2,1)} %get-tuple-element.32), channel_id=1, source_target_pairs={{0,16},{16,0},{1,17},{17,1},{2,18},{18,2},{3,19},{19,3},{4,20},{20... | collective-permute-start | bytes 6291464 | tf_op jit(solution)/shard_map/ppermute | solution.py:262
  136.8 51.6 %collective-permute-start.36 = (bf16[512,1024]{1,0:T(8,128)(2,1)}, bf16[512,1024]{1,0:T(8,128)(2,1)}, u32[]{:S(2)}, u32[]{:S(2)}) collective-permute-start(bf16[512,1024]{1,0:T(8,128)(2,1)} %collective-permute-done.35), channel_id=1, source_target_pairs={{1,0},{2,3},{5,4},{6,7},{9,8},{10,11},{13,12},{14,15},{17,16},{18,... | collective-permute-start | bytes 3145736 | tf_op jit(solution)/shard_map/ppermute | solution.py:275
  138.1 72.8 %collective-permute-start.40 = (bf16[512,1024]{1,0:T(8,128)(2,1)}, bf16[512,1024]{1,0:T(8,128)(2,1)}, u32[]{:S(2)}, u32[]{:S(2)}) collective-permute-start(bf16[512,1024]{1,0:T(8,128)(2,1)} %collective-permute-done.39), channel_id=1, source_target_pairs={{1,0},{2,3},{5,4},{6,7},{9,8},{10,11},{13,12},{14,15},{17,16},{18,... | collective-permute-start | bytes 3145736 | tf_op jit(solution)/shard_map/ppermute | solution.py:276
  140.6 122.5 %collective-permute-start.33 = (bf16[512,512]{1,0:T(8,128)(2,1)}, bf16[512,512]{1,0:T(8,128)(2,1)}, u32[]{:S(2)}, u32[]{:S(2)}) collective-permute-start(bf16[512,512]{1,0:T(8,128)(2,1)} %get-tuple-element.64), channel_id=1, source_target_pairs={{0,4},{4,0},{8,12},{12,8},{1,5},{5,1},{9,13},{13,9},{2,6},{6,2},{1... | collective-permute-start | bytes 1572872 | tf_op jit(solution)/shard_map/ppermute | solution.py:262
  163.7 28.7 %collective-permute-start.22 = (bf16[512,384]{1,0:T(8,128)(2,1)}, bf16[512,384]{1,0:T(8,128)(2,1)S(1)}, u32[]{:S(2)}, u32[]{:S(2)}) collective-permute-start(bf16[512,384]{1,0:T(8,128)(2,1)} %get-tuple-element.41), channel_id=1, source_target_pairs={{0,4},{4,0},{8,12},{12,8},{1,5},{5,1},{9,13},{13,9},{2,6},{6,2},{1... | collective-permute-start | bytes 1179656 | tf_op jit(solution)/shard_map/ppermute | solution.py:262
  164.4 29.5 %collective-permute-start.23 = (bf16[512,384]{1,0:T(8,128)(2,1)}, bf16[512,384]{1,0:T(8,128)(2,1)S(1)}, u32[]{:S(2)}, u32[]{:S(2)}) collective-permute-start(bf16[512,384]{1,0:T(8,128)(2,1)} %get-tuple-element.42), channel_id=1, source_target_pairs={{0,8},{4,12},{8,0},{12,4},{1,9},{5,13},{9,1},{13,5},{2,10},{6,14},... | collective-permute-start | bytes 1179656 | tf_op jit(solution)/shard_map/ppermute | solution.py:262
  192.4 71.8 %collective-permute-start.34 = (bf16[512,512]{1,0:T(8,128)(2,1)}, bf16[512,512]{1,0:T(8,128)(2,1)S(1)}, u32[]{:S(2)}, u32[]{:S(2)}) collective-permute-start(bf16[512,512]{1,0:T(8,128)(2,1)} %get-tuple-element.63), channel_id=1, source_target_pairs={{0,8},{4,12},{8,0},{12,4},{1,9},{5,13},{9,1},{13,5},{2,10},{6,14},... | collective-permute-start | bytes 1572872 | tf_op jit(solution)/shard_map/ppermute | solution.py:262
  218.0 37.4 %collective-permute-start.28 = (bf16[128,512]{1,0:T(8,128)(2,1)S(1)}, bf16[128,512]{1,0:T(8,128)(2,1)S(1)}, u32[]{:S(2)}, u32[]{:S(2)}) collective-permute-start(bf16[128,512]{1,0:T(8,128)(2,1)S(1)} %get-tuple-element.68), channel_id=1, source_target_pairs={{0,1},{1,0},{2,3},{3,2},{4,5},{5,4},{6,7},{7,6},{8,9},{9,8},{10,11... | collective-permute-start | bytes 393224 | tf_op jit(solution)/shard_map/ppermute | solution.py:262
  (46 other events, 590.5 us)

commit v3 on v2

--- a/solution.py
+++ b/solution.py
@@ -239,7 +239,7 @@
 VM = pl.BlockSpec(memory_space=pltpu.VMEM)
 SM = pl.BlockSpec(memory_space=pltpu.SMEM)
 
-UNIT, CTX, PLANE, CROSS, HALF, OTHER = 0, 4, 8, 12, 13, 14
+UNIT, CTX, PLANE, CROSS, HALF = 0, 4, 8, 12, 13
 MINE, THEIRS, SLOTS = 15, 17, 19
 
 
@@ -346,12 +346,17 @@
 
 
 def branch_a_kernel(where_ref, own0, oth0, own1, oth1, own2, oth2, home_ref, *refs):
-    block1, block2, sum_ref = refs[:4], refs[4:8], refs[8]
+    block1, block2, sum_ref = refs[:5], refs[5:9], refs[9]
     left0, left1, left2 = both(own0, oth0), both(own1, oth1), both(own2, oth2)
     rows = own0.shape[0]
     for rel in range(4):
         lane = branch_lane(where_ref, rel)
-        total = dot32(left0, home_ref[:, lane]) + dot32(left1, block1[rel][...])
+        total = dot32(left0, home_ref[:, lane])
+        if rel < 3:
+            total += dot32(left1, block1[rel][...])
+        else:
+            total += dot32(left1[:, :256], block1[3][...])
+            total += dot32(left1[:, 256:], block1[4][...])
         total += dot32(left2, block2[rel][...])
         sum_ref[0, :, lane] = total[:rows]
         sum_ref[1, :, lane] = total[rows:]
@@ -397,7 +402,7 @@
     home_spec = pl.BlockSpec((512, 2048), lambda i, w: (0, w[HALF]))
     partial = call(
         branch_a_kernel,
-        mixes(0) + mixes(1) + mixes(2) + [home_spec] + [VM] * 8,
+        mixes(0) + mixes(1) + mixes(2) + [home_spec] + [VM] * 9,
         sums,
         sum_shape,
         mix * 3 + [home] + parts[0] + parts[1],
@@ -609,26 +614,6 @@
     )(where, own, oth, rows, home, *parts)
 
 
-def join_kernel(where_ref, own_any, rows_ref, got_ref, out_ref):
-    out_ref[...] = rows_ref[...] + got_ref[...].astype(F32)
-
-
-def join_halves(where, own, rows, got):
-    piece = pl.BlockSpec((128, 1024), lambda i, w: (0, i))
-    return pl.pallas_call(
-        join_kernel,
-        grid_spec=pltpu.PrefetchScalarGridSpec(
-            num_scalar_prefetch=1,
-            grid=(2,),
-            in_specs=[pl.BlockSpec(memory_space=pl.ANY), piece, piece],
-            out_specs=pl.BlockSpec((128, 1024), lambda i, w: (0, w[OTHER] * 2 + i)),
-        ),
-        out_shape=jax.ShapeDtypeStruct((128, 4096), F32),
-        input_output_aliases={1: 0},
-        name="join_halves",
-    )(where, own, rows, got)
-
-
 def block_body(*operands):
     return block_rows_out(*operands)
 
@@ -654,16 +639,18 @@
     order = block_order.astype(jnp.int32)
     half_lane = half_at * 2048
     table_rows = jnp.asarray(position_table())
-    where = lax.dynamic_index_in_dim(
-        table_rows, half_at * 16 + ctx * 4 + plane, 0, keepdims=False
-    )
+    where = lax.dynamic_index_in_dim(table_rows, half_at * 16 + ctx * 4 + plane, 0, keepdims=False)
 
     piece = rows_of(hyena_out, half_lane + ctx * 512, 512)
     parts = []
-    for unit in along_chain(piece, edge):
-        parts.append(
-            [unit, swap(unit, "context", 1), swap(unit, "context", 2), swap(unit, "context", 3)]
-        )
+    for at, unit in enumerate(along_chain(piece, edge)):
+        side_x = swap(unit, "context", 1)
+        side_y = swap(unit, "context", 2)
+        if at == 0:
+            corner = [swap(side_y[:256], "context", 1), swap(side_x[256:], "context", 2)]
+        else:
+            corner = [swap(unit, "context", 3)]
+        parts.append([unit, side_x, side_y] + corner)
 
     own_row = ids.astype(F32).reshape(1, 128)
     id_rows = jnp.concatenate(
@@ -765,7 +752,9 @@
         parts += [unit, swap(unit[:, :512], "context", 1), swap(unit[:, 512:], "context", 2)]
     own_out, give_out = out_branches(where, own_att, oth_att, own_rows, attn_out, parts)
     got_out = swap(give_out, "dp", 1)
-    return join_halves(where, own_out, oth_rows, got_out)
+    return lax.dynamic_update_slice(
+        own_out, oth_rows + got_out.astype(F32), (0, (1 - half_at) * 2048)
+    )
 
 
 def solution(mesh):

time: 298 us -> 292 us (0.980)
  starting transfers between devices: 88.1 us -> 83.9 us
    ppermute x36 -> x37, waiting for transfers between devices: 64.1 us -> 72.3 us  [swap(): return lax.ppermute(value, axis, [(at, at ^ mask) for at in range(size)])]
    ppermute x2, waiting for transfers between devices: 32.1 us -> 24.1 us  [along_chain(): across_out = lax.ppermute(across, 'tensor', outward)]
    ppermute x36 -> x37, starting transfers between devices: 77.3 us -> 72.3 us  [swap(): return lax.ppermute(value, axis, [(at, at ^ mask) for at in range(size)])]
    unnamed x57 -> x61, local copies, waits for them, and re-layouts: 7.32 us -> 6.45 us
  transfers between devices with their start and end apart: 44 -> 45, of which waited for: 17 -> 19; matrix products, arithmetic and copies ran while one was open for 11% -> 11% of each run, Pallas kernels for 20% -> 20%
where the time goes in v3:
time: 292 us; the launch traced here: 291 us
  waiting for transfers between devices  101 us (35%)
  starting transfers between devices  83.9 us (29%)
  Pallas kernels  67.6 us (23%)
  local copies, waits for them, and re-layouts  18.2 us (6%)
  other arithmetic  13.9 us (5%)
  matrix products  6.37 us (2%)
    ppermute x37, starting transfers between devices, swap(): return lax.ppermute(value, axis, [(at, at ^ mask) for at in range(size)])  72.3 us
    ppermute x37, waiting for transfers between devices, swap(): return lax.ppermute(value, axis, [(at, at ^ mask) for at in range(size)])  72.3 us
    ppermute x2, waiting for transfers between devices, along_chain(): across_out = lax.ppermute(across, 'tensor', outward)  24.1 us
    pallas_call x2, Pallas kernels, call(): pl.pallas_call(kernel, grid_spec=pltpu.PrefetchScalarGridSpec(num_scalar_...  21.2 us
    pallas_call x2, Pallas kernels, qkv_half(): pl.pallas_call(functools.partial(qkv_kernel, first=first), grid_spec=pltp...  20.4 us
    pallas_call x1, Pallas kernels, hyena_mixes(): pl.pallas_call(hyena_kernel, grid_spec=pltpu.PrefetchScalarGridSpec(num_s...  9.89 us
    pallas_call x1, Pallas kernels, out_branches(): pl.pallas_call(out_kernel, grid_spec=pltpu.PrefetchScalarGridSpec(num_sca...  8.93 us
    pallas_call x1, Pallas kernels, attend(): pl.pallas_call(attend_kernel, in_specs=[SM] + [VM] * 4, out_specs=[VM] *...  7.09 us
  transfers between devices with their start and end apart: 45, of which 19 were waited for; matrix products, arithmetic and copies ran while one was open for 11% of the time, Pallas kernels for 20%

profile of v3, /device:TPU:0, one launch (start us, length us, event | category | flops | bytes accessed | tf_op | source)
XLA Modules:
  0.0 291.2 jit_solution(10098843075505880746)
XLA Ops:
  0.7 3.0 %collective-permute-start = (f32[1,128]{1,0:T(1,128)S(1)}, f32[1,128]{1,0:T(1,128)S(1)}, u32[]{:S(2)}, u32[]{:S(2)}) collective-permute-start(f32[1,128]{1,0:T(1,128)S(1)} %convert_bitcast_fusion.1), channel_id=1, source_target_pairs={{0,4},{4,0},{8,12},{12,8},{1,5},{5,1},{9,13},{13,9},{2,6},{6,2},{1... | collective-permute-start | bytes 1544 | tf_op jit(solution)/shard_map/ppermute | solution.py:262
  7.7 4.2 %collective-permute-start.7 = (bf16[512,512]{1,0:T(8,128)(2,1)S(1)}, bf16[512,512]{1,0:T(8,128)(2,1)}, u32[]{:S(2)}, u32[]{:S(2)}) collective-permute-start(bf16[512,512]{1,0:T(8,128)(2,1)S(1)} %constant_dynamic-slice_fusion.1), channel_id=1, source_target_pairs={{0,1},{1,0},{2,3},{3,2},{4,5},{5,4},{6,7},{7,6},{8,9},{9,8},{10,11... | collective-permute-start | bytes 1572872 | tf_op jit(solution)/shard_map/ppermute | solution.py:262
  16.5 6.4 %fusion.1 = f32[3,4,512]{2,1,0:T(4,128)S(1)} fusion(bf16[3,4096,512]{2,1,0:T(8,128)(2,1)} %param.18, bf16[4,4096]{1,0:T(4,128)(2,1)S(1)} %get-tuple-element.34.base_ref, f32[4096]{0:T(1024)} %param.17, f32[4]{0:T(128)S(1)} %add_rsqrt_fusion), kind=kOutput, calls=%fused_computation.2 | convolution fusion | flops 50409472 | bytes 12656656 | tf_op jit(solution)/shard_map/rd,jdc->jrc/dot_general | solution.py:662
  37.7 9.9 %hyena_mix.1.own0.own1.own2.own3 = bf16[512,2048]{1,0:T(8,128)(2,1)} custom-call(s32[27]{0:T(128)} %get-tuple-element.74.where_ref, bf16[3,2048,24]{2,1,0:T(8,128)(2,1)} %copy.45.coef_ref, bf16[24,768]{1,0:T(8,128)(2,1)} %add_convert_fusion.hot_ref, f32[128,128]{1,0:T(8,128)} %reshape.160.taps_ref, f32[2048,1]{1,0:T(8,128)} %bitcast.52), custom_call_target="tpu_custom_call" | custom-call | tf_op jit(solution)/shard_map/hyena_mix/pallas_call | solution.py:320
  54.7 8.9 %collective-permute-done.9.refs_2_ = bf16[512,512]{1,0:T(8,128)(2,1)S(1)} collective-permute-done((bf16[512,512]{1,0:T(8,128)(2,1)}, bf16[512,512]{1,0:T(8,128)(2,1)S(1)}, u32[]{:S(2)}, u32[]{:S(2)}) %collective-permute-start.9) | collective-permute-done | bytes 524320 | tf_op jit(solution)/shard_map/ppermute | solution.py:262
  75.3 2.7 collective-permute-done.18
  80.6 18.7 %collective-permute-done.11.refs_4_ = bf16[256,512]{1,0:T(8,128)(2,1)S(1)} collective-permute-done((bf16[256,512]{1,0:T(8,128)(2,1)S(1)}, bf16[256,512]{1,0:T(8,128)(2,1)S(1)}, u32[]{:S(2)}, u32[]{:S(2)}) %collective-permute-start.11) | collective-permute-done | bytes 262176 | tf_op jit(solution)/shard_map/ppermute | solution.py:262
  102.8 2.9 constant_dynamic-slice_fusion
  107.2 13.2 %hyena_branch.2.sum_ref = f32[2,512,2048]{2,1,0:T(8,128)} custom-call(s32[27]{0:T(128)} %get-tuple-element.74.where_ref, bf16[512,2048]{1,0:T(8,128)(2,1)} %hyena_mix.1.own0.own1.own2.own3, bf16[512,2048]{1,0:T(8,128)(2,1)} %copy-done, bf16[512,2048]{1,0:T(8,128)(2,1)} %hyena_mix.1.own0.own1.own2.own3, bf16[512,2048]{1,0:T(8,128)(2,1)} %copy-done, ...), custom_call_target="tpu_custom_call" | custom-call | tf_op jit(solution)/shard_map/hyena_branch/pallas_call | solution.py:392
  120.4 3.2 %collective-permute-done.20.refs_2_ = bf16[512,512]{1,0:T(8,128)(2,1)} collective-permute-done((bf16[512,512]{1,0:T(8,128)(2,1)}, bf16[512,512]{1,0:T(8,128)(2,1)}, u32[]{:S(2)}, u32[]{:S(2)}) %collective-permute-start.20) | collective-permute-done | bytes 524320 | tf_op jit(solution)/shard_map/ppermute | solution.py:262
  123.6 8.1 %hyena_branch.3 = (f32[512,2048]{1,0:T(8,128)}, bf16[512,2048]{1,0:T(8,128)(2,1)}) custom-call(s32[27]{0:T(128)} %get-tuple-element.74.where_ref, bf16[512,2048]{1,0:T(8,128)(2,1)} %hyena_mix.1.own0.own1.own2.own3, bf16[512,2048]{1,0:T(8,128)(2,1)} %copy-done, f32[2,512,2048]{2,1,0:T(8,128)} %hyena_branch.2.sum_ref, ...), custom_call_target="tpu_custom_call" | custom-call | tf_op jit(solution)/shard_map/hyena_branch/pallas_call | solution.py:392
  139.4 9.4 %qkv_half.2 = (f32[512,1536]{1,0:T(8,128)}, f32[512,1]{1,0:T(8,128)}, f32[128,2048]{1,0:T(8,128)}) custom-call(s32[27]{0:T(128)} %get-tuple-element.74.where_ref, f32[512,2048]{1,0:T(8,128)} %get-tuple-element.35.half_ref, bf16[512,4]{1,0:T(8,128)(2,1)} %compare_convert_fusion.hot_ref, bf16[4,4096]{1,0:T(4,128)(2,1)} %copy-done.10, f32[1,4096]{1,0:T(1,128)} %bitcast.61, ...), custom_call_target="tpu_custom_call" | custom-call | tf_op jit(solution)/shard_map/qkv_half/pallas_call | solution.py:489
  150.1 11.0 %qkv_half.3 = (bf16[512,384]{1,0:T(8,128)(2,1)}, bf16[512,384]{1,0:T(8,128)(2,1)}, bf16[512,384]{1,0:T(8,128)(2,1)}, bf16[512,384]{1,0:T(8,128)(2,1)}, f32[128,2048]{1,0:T(8,128)}) custom-call(s32[27]{0:T(128)} %get-tuple-element.74.where_ref, bf16[512,2048]{1,0:T(8,128)(2,1)} %copy-done.5, bf16[512,4]{1,0:T(8,128)(2,1)} %compare_convert_fusion.hot_ref, ...), custom_call_target="tpu_custom_call" | custom-call | tf_op jit(solution)/shard_map/qkv_half/pallas_call | solution.py:489
  162.9 21.7 %collective-permute-done.37 = bf16[512,1024]{1,0:T(8,128)(2,1)} collective-permute-done((bf16[512,1024]{1,0:T(8,128)(2,1)}, bf16[512,1024]{1,0:T(8,128)(2,1)}, u32[]{:S(2)}, u32[]{:S(2)}) %collective-permute-start.37) | collective-permute-done | bytes 1048608 | tf_op jit(solution)/shard_map/ppermute | solution.py:275
  189.3 6.2 %collective-permute-done.25.refs_3_ = bf16[512,384]{1,0:T(8,128)(2,1)S(1)} collective-permute-done((bf16[512,384]{1,0:T(8,128)(2,1)}, bf16[512,384]{1,0:T(8,128)(2,1)S(1)}, u32[]{:S(2)}, u32[]{:S(2)}) %collective-permute-start.25) | collective-permute-done | bytes 393248 | tf_op jit(solution)/shard_map/ppermute | solution.py:262
  196.2 7.1 %attend.1 = (bf16[512,128]{1,0:T(8,128)(2,1)}, bf16[512,128]{1,0:T(8,128)(2,1)}, bf16[512,128]{1,0:T(8,128)(2,1)}, bf16[512,128]{1,0:T(8,128)(2,1)}) custom-call(s32[8]{0:T(128)} %copy-done.27, bf16[512,384]{1,0:T(8,128)(2,1)} %get-tuple-element.40.refs_0_, bf16[512,384]{1,0:T(8,128)(2,1)} %copy-done.18, bf16[512,384]{1,0:T(8,128)(2,1)} %copy-done.19, ...), custom_call_target="tpu_custom_call" | custom-call | tf_op jit(solution)/shard_map/attend/pallas_call | solution.py:539
  210.3 3.0 %collective-permute-done.28 = bf16[512,128]{1,0:T(8,128)(2,1)S(1)} collective-permute-done((bf16[512,128]{1,0:T(8,128)(2,1)}, bf16[512,128]{1,0:T(8,128)(2,1)S(1)}, u32[]{:S(2)}, u32[]{:S(2)}) %collective-permute-start.28) | collective-permute-done | bytes 131104 | tf_op jit(solution)/shard_map/ppermute | solution.py:262
  214.2 33.0 %collective-permute-start.29 = (bf16[128,512]{1,0:T(8,128)(2,1)S(1)}, bf16[128,512]{1,0:T(8,128)(2,1)S(1)}, u32[]{:S(2)}, u32[]{:S(2)}) collective-permute-start(bf16[128,512]{1,0:T(8,128)(2,1)S(1)} %get-tuple-element.68), channel_id=1, source_target_pairs={{0,1},{1,0},{2,3},{3,2},{4,5},{5,4},{6,7},{7,6},{8,9},{9,8},{10,11... | collective-permute-start | bytes 393224 | tf_op jit(solution)/shard_map/ppermute | solution.py:262
  249.7 3.1 %collective-permute-done.29 = bf16[128,512]{1,0:T(8,128)(2,1)S(1)} collective-permute-done((bf16[128,512]{1,0:T(8,128)(2,1)S(1)}, bf16[128,512]{1,0:T(8,128)(2,1)S(1)}, u32[]{:S(2)}, u32[]{:S(2)}) %collective-permute-start.29) | collective-permute-done | bytes 131104 | tf_op jit(solution)/shard_map/ppermute | solution.py:262
  252.8 4.6 %collective-permute-done.30 = bf16[128,512]{1,0:T(8,128)(2,1)S(1)} collective-permute-done((bf16[128,512]{1,0:T(8,128)(2,1)S(1)}, bf16[128,512]{1,0:T(8,128)(2,1)S(1)}, u32[]{:S(2)}, u32[]{:S(2)}) %collective-permute-start.30) | collective-permute-done | bytes 131104 | tf_op jit(solution)/shard_map/ppermute | solution.py:262
  259.7 6.5 %collective-permute-done.38.refs_4_ = bf16[512,512]{1,0:T(8,128)(2,1)S(1)} collective-permute-done((bf16[512,512]{1,0:T(8,128)(2,1)}, bf16[512,512]{1,0:T(8,128)(2,1)S(1)}, u32[]{:S(2)}, u32[]{:S(2)}) %collective-permute-start.38) | collective-permute-done | bytes 524320 | tf_op jit(solution)/shard_map/ppermute | solution.py:262
  266.2 5.5 %collective-permute-done.39.refs_5_ = bf16[512,512]{1,0:T(8,128)(2,1)S(1)} collective-permute-done((bf16[512,512]{1,0:T(8,128)(2,1)S(1)}, bf16[512,512]{1,0:T(8,128)(2,1)S(1)}, u32[]{:S(2)}, u32[]{:S(2)}) %collective-permute-start.39) | collective-permute-done | bytes 524320 | tf_op jit(solution)/shard_map/ppermute | solution.py:262
  271.9 5.5 %collective-permute-done.43.refs_8_ = bf16[512,512]{1,0:T(8,128)(2,1)S(1)} collective-permute-done((bf16[512,512]{1,0:T(8,128)(2,1)S(1)}, bf16[512,512]{1,0:T(8,128)(2,1)S(1)}, u32[]{:S(2)}, u32[]{:S(2)}) %collective-permute-start.43) | collective-permute-done | bytes 524320 | tf_op jit(solution)/shard_map/ppermute | solution.py:262
  279.0 8.9 %out_branch.1 = (f32[128,4096]{1,0:T(8,128)}, bf16[128,2048]{1,0:T(8,128)(2,1)}) custom-call(s32[27]{0:T(128)} %get-tuple-element.74.where_ref, bf16[128,2048]{1,0:T(8,128)(2,1)} %copy-done.6, bf16[128,2048]{1,0:T(8,128)(2,1)} %copy-done.16, f32[128,2048]{1,0:T(8,128)} %get-tuple-element.48.rows_ref, bf16[512,4096]{1,0:T(8,128)(2,1)} %home_ref.3, ...), custom_call_target="tpu_custom_call" | custom-call | tf_op jit(solution)/shard_map/out_branch/pallas_call | solution.py:601
  (198 shorter events, 84.2 us)
Async XLA Ops:
  0.7 22.4 %collective-permute-start = (f32[1,128]{1,0:T(1,128)S(1)}, f32[1,128]{1,0:T(1,128)S(1)}, u32[]{:S(2)}, u32[]{:S(2)}) collective-permute-start(f32[1,128]{1,0:T(1,128)S(1)} %convert_bitcast_fusion.1), channel_id=1, source_target_pairs={{0,4},{4,0},{8,12},{12,8},{1,5},{5,1},{9,13},{13,9},{2,6},{6,2},{1... | collective-permute-start | bytes 1544 | tf_op jit(solution)/shard_map/ppermute | solution.py:262
  3.6 19.4 %collective-permute-start.1 = (f32[1,128]{1,0:T(1,128)S(1)}, f32[1,128]{1,0:T(1,128)S(1)}, u32[]{:S(2)}, u32[]{:S(2)}) collective-permute-start(f32[1,128]{1,0:T(1,128)S(1)} %convert_bitcast_fusion.1), channel_id=1, source_target_pairs={{0,8},{4,12},{8,0},{12,4},{1,9},{5,13},{9,1},{13,5},{2,10},{6,14},... | collective-permute-start | bytes 1544 | tf_op jit(solution)/shard_map/ppermute | solution.py:262
  5.1 17.9 %collective-permute-start.2 = (f32[1,128]{1,0:T(1,128)S(1)}, f32[1,128]{1,0:T(1,128)S(1)}, u32[]{:S(2)}, u32[]{:S(2)}) collective-permute-start(f32[1,128]{1,0:T(1,128)S(1)} %convert_bitcast_fusion.1), channel_id=1, source_target_pairs={{0,12},{4,8},{8,4},{12,0},{1,13},{5,9},{9,5},{13,1},{2,14},{6,10},... | collective-permute-start | bytes 1544 | tf_op jit(solution)/shard_map/ppermute | solution.py:262
  6.2 44.3 %collective-permute-start.12 = (bf16[512,512]{1,0:T(8,128)(2,1)S(1)}, bf16[512,512]{1,0:T(8,128)(2,1)}, u32[]{:S(2)}, u32[]{:S(2)}) collective-permute-start(bf16[512,512]{1,0:T(8,128)(2,1)S(1)} %constant_dynamic-slice_fusion.1), channel_id=1, source_target_pairs={{1,2},{2,1},{5,6},{6,5},{9,10},{10,9},{13,14},{14,13},{17,18},{18,... | collective-permute-start | bytes 1572872 | tf_op jit(solution)/shard_map/ppermute | solution.py:273
  7.7 39.9 %collective-permute-start.7 = (bf16[512,512]{1,0:T(8,128)(2,1)S(1)}, bf16[512,512]{1,0:T(8,128)(2,1)}, u32[]{:S(2)}, u32[]{:S(2)}) collective-permute-start(bf16[512,512]{1,0:T(8,128)(2,1)S(1)} %constant_dynamic-slice_fusion.1), channel_id=1, source_target_pairs={{0,1},{1,0},{2,3},{3,2},{4,5},{5,4},{6,7},{7,6},{8,9},{9,8},{10,11... | collective-permute-start | bytes 1572872 | tf_op jit(solution)/shard_map/ppermute | solution.py:262
  47.5 58.4 %collective-permute-start.6 = (bf16[512,2048]{1,0:T(8,128)(2,1)}, bf16[512,2048]{1,0:T(8,128)(2,1)S(1)}, u32[]{:S(2)}, u32[]{:S(2)}) collective-permute-start(bf16[512,2048]{1,0:T(8,128)(2,1)} %hyena_mix.1.own0.own1.own2.own3), channel_id=1, source_target_pairs={{0,16},{16,0},{1,17},{17,1},{2,18},{18,2},{3,19},{19,3},{4,20},{20... | collective-permute-start | bytes 6291464 | tf_op jit(solution)/shard_map/ppermute | solution.py:262
  51.9 18.4 %collective-permute-start.8 = (bf16[512,512]{1,0:T(8,128)(2,1)}, bf16[512,512]{1,0:T(8,128)(2,1)S(1)}, u32[]{:S(2)}, u32[]{:S(2)}) collective-permute-start(bf16[512,512]{1,0:T(8,128)(2,1)} %collective-permute-done.7.refs_0_), channel_id=1, source_target_pairs={{0,4},{4,0},{8,12},{12,8},{1,5},{5,1},{9,13},{13,9},{2,6},{6,2},{1... | collective-permute-start | bytes 1572872 | tf_op jit(solution)/shard_map/ppermute | solution.py:262
  53.4 24.6 %collective-permute-start.18 = (bf16[512,512]{1,0:T(8,128)(2,1)}, bf16[512,512]{1,0:T(8,128)(2,1)}, u32[]{:S(2)}, u32[]{:S(2)}) collective-permute-start(bf16[512,512]{1,0:T(8,128)(2,1)} %collective-permute-done.17), channel_id=1, source_target_pairs={{1,0},{2,3},{5,4},{6,7},{9,8},{10,11},{13,12},{14,15},{17,16},{18,... | collective-permute-start | bytes 1572872 | tf_op jit(solution)/shard_map/ppermute | solution.py:276
  68.7 31.1 %collective-permute-start.14 = (bf16[512,512]{1,0:T(8,128)(2,1)S(1)}, bf16[512,512]{1,0:T(8,128)(2,1)}, u32[]{:S(2)}, u32[]{:S(2)}) collective-permute-start(bf16[512,512]{1,0:T(8,128)(2,1)S(1)} %broadcast_select_fusion.3.refs_5_), channel_id=1, source_target_pairs={{0,4},{4,0},{8,12},{12,8},{1,5},{5,1},{9,13},{13,9},{2,6},{6,2},{1... | collective-permute-start | bytes 1572872 | tf_op jit(solution)/shard_map/ppermute | solution.py:262
  70.3 30.1 %collective-permute-start.15 = (bf16[512,512]{1,0:T(8,128)(2,1)S(1)}, bf16[512,512]{1,0:T(8,128)(2,1)}, u32[]{:S(2)}, u32[]{:S(2)}) collective-permute-start(bf16[512,512]{1,0:T(8,128)(2,1)S(1)} %broadcast_select_fusion.3.refs_5_), channel_id=1, source_target_pairs={{0,8},{4,12},{8,0},{12,4},{1,9},{5,13},{9,1},{13,5},{2,10},{6,14},... | collective-permute-start | bytes 1572872 | tf_op jit(solution)/shard_map/ppermute | solution.py:262
  72.9 32.8 %collective-permute-start.16 = (bf16[512,512]{1,0:T(8,128)(2,1)S(1)}, bf16[512,512]{1,0:T(8,128)(2,1)}, u32[]{:S(2)}, u32[]{:S(2)}) collective-permute-start(bf16[512,512]{1,0:T(8,128)(2,1)S(1)} %broadcast_select_fusion.3.refs_5_), channel_id=1, source_target_pairs={{0,12},{4,8},{8,4},{12,0},{1,13},{5,9},{9,5},{13,1},{2,14},{6,10},... | collective-permute-start | bytes 1572872 | tf_op jit(solution)/shard_map/ppermute | solution.py:262
  78.1 21.2 %collective-permute-start.11 = (bf16[256,512]{1,0:T(8,128)(2,1)S(1)}, bf16[256,512]{1,0:T(8,128)(2,1)S(1)}, u32[]{:S(2)}, u32[]{:S(2)}) collective-permute-start(bf16[256,512]{1,0:T(8,128)(2,1)S(1)} %slice.111), channel_id=1, source_target_pairs={{0,8},{4,12},{8,0},{12,4},{1,9},{5,13},{9,1},{13,5},{2,10},{6,14},... | collective-permute-start | bytes 786440 | tf_op jit(solution)/shard_map/ppermute | solution.py:262
  99.3 21.1 %collective-permute-start.19 = (bf16[512,512]{1,0:T(8,128)(2,1)}, bf16[512,512]{1,0:T(8,128)(2,1)}, u32[]{:S(2)}, u32[]{:S(2)}) collective-permute-start(bf16[512,512]{1,0:T(8,128)(2,1)} %broadcast_select_fusion.2.refs_0_), channel_id=1, source_target_pairs={{0,4},{4,0},{8,12},{12,8},{1,5},{5,1},{9,13},{13,9},{2,6},{6,2},{1... | collective-permute-start | bytes 1572872 | tf_op jit(solution)/shard_map/ppermute | solution.py:262
  99.8 23.8 %collective-permute-start.20 = (bf16[512,512]{1,0:T(8,128)(2,1)}, bf16[512,512]{1,0:T(8,128)(2,1)}, u32[]{:S(2)}, u32[]{:S(2)}) collective-permute-start(bf16[512,512]{1,0:T(8,128)(2,1)} %broadcast_select_fusion.2.refs_0_), channel_id=1, source_target_pairs={{0,8},{4,12},{8,0},{12,4},{1,9},{5,13},{9,1},{13,5},{2,10},{6,14},... | collective-permute-start | bytes 1572872 | tf_op jit(solution)/shard_map/ppermute | solution.py:262
  100.3 23.3 %collective-permute-start.21 = (bf16[512,512]{1,0:T(8,128)(2,1)}, bf16[512,512]{1,0:T(8,128)(2,1)}, u32[]{:S(2)}, u32[]{:S(2)}) collective-permute-start(bf16[512,512]{1,0:T(8,128)(2,1)} %broadcast_select_fusion.2.refs_0_), channel_id=1, source_target_pairs={{0,12},{4,8},{8,4},{12,0},{1,13},{5,9},{9,5},{13,1},{2,14},{6,10},... | collective-permute-start | bytes 1572872 | tf_op jit(solution)/shard_map/ppermute | solution.py:262
  105.7 27.6 %collective-permute-start.33 = (bf16[512,1024]{1,0:T(8,128)(2,1)}, bf16[512,1024]{1,0:T(8,128)(2,1)S(1)}, u32[]{:S(2)}, u32[]{:S(2)}) collective-permute-start(bf16[512,1024]{1,0:T(8,128)(2,1)} %constant_dynamic-slice_fusion), channel_id=1, source_target_pairs={{0,1},{1,0},{2,3},{3,2},{4,5},{5,4},{6,7},{7,6},{8,9},{9,8},{10,11... | collective-permute-start | bytes 3145736 | tf_op jit(solution)/shard_map/ppermute | solution.py:262
  135.0 49.7 %collective-permute-start.37 = (bf16[512,1024]{1,0:T(8,128)(2,1)}, bf16[512,1024]{1,0:T(8,128)(2,1)}, u32[]{:S(2)}, u32[]{:S(2)}) collective-permute-start(bf16[512,1024]{1,0:T(8,128)(2,1)} %collective-permute-done.36), channel_id=1, source_target_pairs={{1,0},{2,3},{5,4},{6,7},{9,8},{10,11},{13,12},{14,15},{17,16},{18,... | collective-permute-start | bytes 3145736 | tf_op jit(solution)/shard_map/ppermute | solution.py:275
  136.3 70.9 %collective-permute-start.41 = (bf16[512,1024]{1,0:T(8,128)(2,1)}, bf16[512,1024]{1,0:T(8,128)(2,1)}, u32[]{:S(2)}, u32[]{:S(2)}) collective-permute-start(bf16[512,1024]{1,0:T(8,128)(2,1)} %collective-permute-done.40), channel_id=1, source_target_pairs={{1,0},{2,3},{5,4},{6,7},{9,8},{10,11},{13,12},{14,15},{17,16},{18,... | collective-permute-start | bytes 3145736 | tf_op jit(solution)/shard_map/ppermute | solution.py:276
  138.8 120.6 %collective-permute-start.34 = (bf16[512,512]{1,0:T(8,128)(2,1)}, bf16[512,512]{1,0:T(8,128)(2,1)}, u32[]{:S(2)}, u32[]{:S(2)}) collective-permute-start(bf16[512,512]{1,0:T(8,128)(2,1)} %get-tuple-element.64), channel_id=1, source_target_pairs={{0,4},{4,0},{8,12},{12,8},{1,5},{5,1},{9,13},{13,9},{2,6},{6,2},{1... | collective-permute-start | bytes 1572872 | tf_op jit(solution)/shard_map/ppermute | solution.py:262
  161.1 27.8 %collective-permute-start.23 = (bf16[512,384]{1,0:T(8,128)(2,1)}, bf16[512,384]{1,0:T(8,128)(2,1)S(1)}, u32[]{:S(2)}, u32[]{:S(2)}) collective-permute-start(bf16[512,384]{1,0:T(8,128)(2,1)} %get-tuple-element.41), channel_id=1, source_target_pairs={{0,4},{4,0},{8,12},{12,8},{1,5},{5,1},{9,13},{13,9},{2,6},{6,2},{1... | collective-permute-start | bytes 1179656 | tf_op jit(solution)/shard_map/ppermute | solution.py:262
  162.6 26.6 %collective-permute-start.24 = (bf16[512,384]{1,0:T(8,128)(2,1)}, bf16[512,384]{1,0:T(8,128)(2,1)S(1)}, u32[]{:S(2)}, u32[]{:S(2)}) collective-permute-start(bf16[512,384]{1,0:T(8,128)(2,1)} %get-tuple-element.42), channel_id=1, source_target_pairs={{0,8},{4,12},{8,0},{12,4},{1,9},{5,13},{9,1},{13,5},{2,10},{6,14},... | collective-permute-start | bytes 1179656 | tf_op jit(solution)/shard_map/ppermute | solution.py:262
  188.9 70.8 %collective-permute-start.35 = (bf16[512,512]{1,0:T(8,128)(2,1)}, bf16[512,512]{1,0:T(8,128)(2,1)S(1)}, u32[]{:S(2)}, u32[]{:S(2)}) collective-permute-start(bf16[512,512]{1,0:T(8,128)(2,1)} %get-tuple-element.63), channel_id=1, source_target_pairs={{0,8},{4,12},{8,0},{12,4},{1,9},{5,13},{9,1},{13,5},{2,10},{6,14},... | collective-permute-start | bytes 1572872 | tf_op jit(solution)/shard_map/ppermute | solution.py:262
  214.2 38.6 %collective-permute-start.29 = (bf16[128,512]{1,0:T(8,128)(2,1)S(1)}, bf16[128,512]{1,0:T(8,128)(2,1)S(1)}, u32[]{:S(2)}, u32[]{:S(2)}) collective-permute-start(bf16[128,512]{1,0:T(8,128)(2,1)S(1)} %get-tuple-element.68), channel_id=1, source_target_pairs={{0,1},{1,0},{2,3},{3,2},{4,5},{5,4},{6,7},{7,6},{8,9},{9,8},{10,11... | collective-permute-start | bytes 393224 | tf_op jit(solution)/shard_map/ppermute | solution.py:262
  259.4 17.9 %collective-permute-start.43 = (bf16[512,512]{1,0:T(8,128)(2,1)S(1)}, bf16[512,512]{1,0:T(8,128)(2,1)S(1)}, u32[]{:S(2)}, u32[]{:S(2)}) collective-permute-start(bf16[512,512]{1,0:T(8,128)(2,1)S(1)} %get-tuple-element.59), channel_id=1, source_target_pairs={{0,8},{4,12},{8,0},{12,4},{1,9},{5,13},{9,1},{13,5},{2,10},{6,14},... | collective-permute-start | bytes 1572872 | tf_op jit(solution)/shard_map/ppermute | solution.py:262
  (49 other events, 607.6 us)

commit v4 on v3

--- a/solution.py
+++ b/solution.py
@@ -285,9 +285,16 @@
     return jnp.dot(left, right, preferred_element_type=F32)
 
 
-def hyena_kernel(where_ref, coef_ref, hot_ref, taps_ref, skip_ref, mix_ref):
+def down_rows(left, right):
+    return lax.dot_general(
+        left, right, (((0,), (0,)), ((), ())), preferred_element_type=F32
+    )
+
+
+def hyena_kernel(where_ref, coef_ref, hot_ref, taps_ref, mix_ref):
     hot = hot_ref[...]
-    first, second, third = (dot32(coef_ref[j], hot) for j in range(3))
+    first, second, third = (down_rows(coef_ref[j], hot) for j in range(3))
+    skip = down_rows(coef_ref[3], jnp.ones((coef_ref.shape[1], 512), BF16))
     gated = second * third
     packed = gated.astype(BF16)
     row = lax.broadcasted_iota(jnp.int32, (128, 128), 0)
@@ -310,12 +317,12 @@
     long_mix = jnp.concatenate(mixed, axis=0)
     own_gate = jnp.concatenate([gated[:, 128:384], gated[:, 512:768]], axis=1)
     own_first = jnp.concatenate([first[:, 128:384], first[:, 512:768]], axis=1)
-    mix = own_first * (long_mix + skip_ref[...] * own_gate)
+    mix = own_first * (long_mix + skip * own_gate)
     mix_ref[...] = mix.T.astype(BF16)
 
 
-def hyena_mixes(where, coef, hot, taps, skip):
-    chans = coef.shape[1]
+def hyena_mixes(where, coef, hot, taps):
+    chans = coef.shape[2]
     step = 256
     return pl.pallas_call(
         hyena_kernel,
@@ -323,10 +330,9 @@
             num_scalar_prefetch=1,
             grid=(chans // step,),
             in_specs=[
-                pl.BlockSpec((3, step, coef.shape[2]), lambda i, w: (0, i, 0)),
+                pl.BlockSpec((4, coef.shape[1], step), lambda i, w: (0, 0, i)),
                 pl.BlockSpec(hot.shape, lambda i, w: (0, 0)),
                 pl.BlockSpec((step // 16, 128), lambda i, w: (i, 0)),
-                pl.BlockSpec((step, 1), lambda i, w: (i, 0)),
             ],
             out_specs=pl.BlockSpec(
                 (512, step), lambda i, w: (0, w[PLANE + i // 2] * 2 + i % 2)
@@ -334,7 +340,7 @@
         ),
         out_shape=jax.ShapeDtypeStruct((512, chans), BF16),
         name="hyena_mix",
-    )(where, coef, hot, taps, skip)
+    )(where, coef, hot, taps)
 
 
 def both(own_ref, oth_ref):
@@ -693,10 +699,17 @@
     all_ids = plane_ids.transpose(1, 0, 2).reshape(8, 256)
     tables = everything[:, :12].reshape(4, 3, 1, 4, 512)
     shorts = everything[:, 12:21].reshape(4, 3, 3, 1, 512)
-    coef = (tables * shorts).transpose(1, 0, 4, 2, 3).reshape(3, 2048, 12)
+    coef = (tables * shorts).transpose(1, 2, 3, 0, 4).reshape(3, 12, 2048)
+    skip = everything[:, 21].reshape(1, 1, 2048)
+    coef = jnp.concatenate(
+        [
+            jnp.pad(coef, ((0, 0), (0, 4), (0, 0))),
+            jnp.pad(skip, ((0, 0), (0, 15), (0, 0))),
+        ],
+        axis=0,
+    )
     coarse = lax.reduce_precision(coef, 8, 7)
-    coef = jnp.concatenate([coarse, coef - coarse], axis=2).astype(BF16)
-    skip = everything[:, 21].reshape(2048, 1)
+    coef = jnp.concatenate([coarse, coef - coarse], axis=1).astype(BF16)
     taps = everything[:, 22:30].reshape(128, 128)
 
     before_hit = place[None, :] == owned[:, None] - 1
@@ -710,13 +723,14 @@
             for lag in range(3)
         ]
     ).reshape(12, 768)
+    hot = jnp.pad(hot, ((0, 4), (0, 0)))
     hot = jnp.concatenate([hot, hot], axis=0)
     own_hot = (own_ids.reshape(512, 1) == codes[None, :]).astype(BF16)
     coef, hot, place, cosine, sine, own_hot, base = lax.optimization_barrier(
         (coef, hot, place, cosine, sine, own_hot, base)
     )
 
-    own_mix = hyena_mixes(where, coef, hot, taps, skip)
+    own_mix = hyena_mixes(where, coef, hot, taps)
     oth_mix = swap(own_mix, "dp", 1)
 
     own_half, give_half = hyena_branches(where, own_mix, oth_mix, hyena_out, parts)

time: 292 us -> 293 us (level)
  waiting for transfers between devices: 101 us -> 104 us
    unnamed x61 -> x59, local copies, waits for them, and re-layouts: 6.45 us -> 5.09 us
  transfers between devices with their start and end apart: 45 -> 45, of which waited for: 19 -> 19; matrix products, arithmetic and copies ran while one was open for 11% -> 10% of each run, Pallas kernels for 20% -> 20%
where the time goes in v4:
time: 293 us; the launch traced here: 291 us
  waiting for transfers between devices  104 us (35%)
  starting transfers between devices  83.9 us (29%)
  Pallas kernels  66.9 us (23%)
  local copies, waits for them, and re-layouts  15.4 us (5%)
  other arithmetic  14.8 us (5%)
  matrix products  6.37 us (2%)
    ppermute x37, waiting for transfers between devices, swap(): return lax.ppermute(value, axis, [(at, at ^ mask) for at in range(size)])  75.2 us
    ppermute x37, starting transfers between devices, swap(): return lax.ppermute(value, axis, [(at, at ^ mask) for at in range(size)])  72.3 us
    ppermute x2, waiting for transfers between devices, along_chain(): across_out = lax.ppermute(across, 'tensor', outward)  24.1 us
    pallas_call x2, Pallas kernels, call(): pl.pallas_call(kernel, grid_spec=pltpu.PrefetchScalarGridSpec(num_scalar_...  21.2 us
    pallas_call x2, Pallas kernels, qkv_half(): pl.pallas_call(functools.partial(qkv_kernel, first=first), grid_spec=pltp...  20.4 us
    pallas_call x1, Pallas kernels, hyena_mixes(): pl.pallas_call(hyena_kernel, grid_spec=pltpu.PrefetchScalarGridSpec(num_s...  9.25 us
    pallas_call x1, Pallas kernels, out_branches(): pl.pallas_call(out_kernel, grid_spec=pltpu.PrefetchScalarGridSpec(num_sca...  8.93 us
    pallas_call x1, Pallas kernels, attend(): pl.pallas_call(attend_kernel, in_specs=[SM] + [VM] * 4, out_specs=[VM] *...  7.09 us
  transfers between devices with their start and end apart: 45, of which 19 were waited for; matrix products, arithmetic and copies ran while one was open for 10% of the time, Pallas kernels for 20%

profile of v4, /device:TPU:0, one launch (start us, length us, event | category | flops | bytes accessed | tf_op | source)
XLA Modules:
  0.0 291.4 jit_solution(15378403484333053238)
XLA Ops:
  0.7 3.0 %collective-permute-start = (f32[1,128]{1,0:T(1,128)S(1)}, f32[1,128]{1,0:T(1,128)S(1)}, u32[]{:S(2)}, u32[]{:S(2)}) collective-permute-start(f32[1,128]{1,0:T(1,128)S(1)} %convert_bitcast_fusion.1), channel_id=1, source_target_pairs={{0,4},{4,0},{8,12},{12,8},{1,5},{5,1},{9,13},{13,9},{2,6},{6,2},{1... | collective-permute-start | bytes 1544 | tf_op jit(solution)/shard_map/ppermute | solution.py:262
  7.7 4.1 %collective-permute-start.7 = (bf16[512,512]{1,0:T(8,128)(2,1)S(1)}, bf16[512,512]{1,0:T(8,128)(2,1)}, u32[]{:S(2)}, u32[]{:S(2)}) collective-permute-start(bf16[512,512]{1,0:T(8,128)(2,1)S(1)} %constant_dynamic-slice_fusion.1), channel_id=1, source_target_pairs={{0,1},{1,0},{2,3},{3,2},{4,5},{5,4},{6,7},{7,6},{8,9},{9,8},{10,11... | collective-permute-start | bytes 1572872 | tf_op jit(solution)/shard_map/ppermute | solution.py:262
  16.6 6.4 %fusion.1 = f32[3,4,512]{2,1,0:T(4,128)S(1)} fusion(bf16[3,4096,512]{2,1,0:T(8,128)(2,1)} %param.18, bf16[4,4096]{1,0:T(4,128)(2,1)S(1)} %get-tuple-element.34.base_ref, f32[4096]{0:T(1024)} %param.17, f32[4]{0:T(128)S(1)} %add_rsqrt_fusion), kind=kOutput, calls=%fused_computation.2 | convolution fusion | flops 50409472 | bytes 12656656 | tf_op jit(solution)/shard_map/rd,jdc->jrc/dot_general | solution.py:668
  35.7 9.3 %hyena_mix.1.own0.own1.own2.own3 = bf16[512,2048]{1,0:T(8,128)(2,1)} custom-call(s32[27]{0:T(128)} %get-tuple-element.74.where_ref, bf16[4,32,2048]{2,1,0:T(8,128)(2,1)} %pad_maximum_fusion.coef_ref, bf16[32,768]{1,0:T(8,128)(2,1)} %add_convert_fusion.hot_ref, f32[128,128]{1,0:T(8,128)} %reshape.160.taps_ref), custom_call_target="tpu_custom_call" | custom-call | tf_op jit(solution)/shard_map/hyena_mix/pallas_call | solution.py:327
  52.1 8.9 %collective-permute-done.9.refs_2_ = bf16[512,512]{1,0:T(8,128)(2,1)S(1)} collective-permute-done((bf16[512,512]{1,0:T(8,128)(2,1)}, bf16[512,512]{1,0:T(8,128)(2,1)S(1)}, u32[]{:S(2)}, u32[]{:S(2)}) %collective-permute-start.9) | collective-permute-done | bytes 524320 | tf_op jit(solution)/shard_map/ppermute | solution.py:262
  72.7 2.7 collective-permute-done.18
  77.9 18.7 %collective-permute-done.11.refs_4_ = bf16[256,512]{1,0:T(8,128)(2,1)S(1)} collective-permute-done((bf16[256,512]{1,0:T(8,128)(2,1)S(1)}, bf16[256,512]{1,0:T(8,128)(2,1)S(1)}, u32[]{:S(2)}, u32[]{:S(2)}) %collective-permute-start.11) | collective-permute-done | bytes 262176 | tf_op jit(solution)/shard_map/ppermute | solution.py:262
  100.1 2.9 constant_dynamic-slice_fusion
  104.6 13.2 %hyena_branch.2.sum_ref = f32[2,512,2048]{2,1,0:T(8,128)} custom-call(s32[27]{0:T(128)} %get-tuple-element.74.where_ref, bf16[512,2048]{1,0:T(8,128)(2,1)} %hyena_mix.1.own0.own1.own2.own3, bf16[512,2048]{1,0:T(8,128)(2,1)} %copy-done, bf16[512,2048]{1,0:T(8,128)(2,1)} %hyena_mix.1.own0.own1.own2.own3, bf16[512,2048]{1,0:T(8,128)(2,1)} %copy-done, ...), custom_call_target="tpu_custom_call" | custom-call | tf_op jit(solution)/shard_map/hyena_branch/pallas_call | solution.py:398
  117.8 3.1 %collective-permute-done.20.refs_2_ = bf16[512,512]{1,0:T(8,128)(2,1)} collective-permute-done((bf16[512,512]{1,0:T(8,128)(2,1)}, bf16[512,512]{1,0:T(8,128)(2,1)}, u32[]{:S(2)}, u32[]{:S(2)}) %collective-permute-start.20) | collective-permute-done | bytes 524320 | tf_op jit(solution)/shard_map/ppermute | solution.py:262
  120.9 8.1 %hyena_branch.3 = (f32[512,2048]{1,0:T(8,128)}, bf16[512,2048]{1,0:T(8,128)(2,1)}) custom-call(s32[27]{0:T(128)} %get-tuple-element.74.where_ref, bf16[512,2048]{1,0:T(8,128)(2,1)} %hyena_mix.1.own0.own1.own2.own3, bf16[512,2048]{1,0:T(8,128)(2,1)} %copy-done, f32[2,512,2048]{2,1,0:T(8,128)} %hyena_branch.2.sum_ref, ...), custom_call_target="tpu_custom_call" | custom-call | tf_op jit(solution)/shard_map/hyena_branch/pallas_call | solution.py:398
  136.7 9.4 %qkv_half.2 = (f32[512,1536]{1,0:T(8,128)}, f32[512,1]{1,0:T(8,128)}, f32[128,2048]{1,0:T(8,128)}) custom-call(s32[27]{0:T(128)} %get-tuple-element.74.where_ref, f32[512,2048]{1,0:T(8,128)} %get-tuple-element.35.half_ref, bf16[512,4]{1,0:T(8,128)(2,1)} %compare_convert_fusion.hot_ref, bf16[4,4096]{1,0:T(4,128)(2,1)} %copy-done.10, f32[1,4096]{1,0:T(1,128)} %bitcast.55, ...), custom_call_target="tpu_custom_call" | custom-call | tf_op jit(solution)/shard_map/qkv_half/pallas_call | solution.py:495
  147.5 11.0 %qkv_half.3 = (bf16[512,384]{1,0:T(8,128)(2,1)}, bf16[512,384]{1,0:T(8,128)(2,1)}, bf16[512,384]{1,0:T(8,128)(2,1)}, bf16[512,384]{1,0:T(8,128)(2,1)}, f32[128,2048]{1,0:T(8,128)}) custom-call(s32[27]{0:T(128)} %get-tuple-element.74.where_ref, bf16[512,2048]{1,0:T(8,128)(2,1)} %copy-done.5, bf16[512,4]{1,0:T(8,128)(2,1)} %compare_convert_fusion.hot_ref, ...), custom_call_target="tpu_custom_call" | custom-call | tf_op jit(solution)/shard_map/qkv_half/pallas_call | solution.py:495
  160.3 21.7 %collective-permute-done.37 = bf16[512,1024]{1,0:T(8,128)(2,1)} collective-permute-done((bf16[512,1024]{1,0:T(8,128)(2,1)}, bf16[512,1024]{1,0:T(8,128)(2,1)}, u32[]{:S(2)}, u32[]{:S(2)}) %collective-permute-start.37) | collective-permute-done | bytes 1048608 | tf_op jit(solution)/shard_map/ppermute | solution.py:275
  186.7 6.2 %collective-permute-done.25.refs_3_ = bf16[512,384]{1,0:T(8,128)(2,1)S(1)} collective-permute-done((bf16[512,384]{1,0:T(8,128)(2,1)}, bf16[512,384]{1,0:T(8,128)(2,1)S(1)}, u32[]{:S(2)}, u32[]{:S(2)}) %collective-permute-start.25) | collective-permute-done | bytes 393248 | tf_op jit(solution)/shard_map/ppermute | solution.py:262
  193.6 7.1 %attend.1 = (bf16[512,128]{1,0:T(8,128)(2,1)}, bf16[512,128]{1,0:T(8,128)(2,1)}, bf16[512,128]{1,0:T(8,128)(2,1)}, bf16[512,128]{1,0:T(8,128)(2,1)}) custom-call(s32[8]{0:T(128)} %copy-done.27, bf16[512,384]{1,0:T(8,128)(2,1)} %get-tuple-element.40.refs_0_, bf16[512,384]{1,0:T(8,128)(2,1)} %copy-done.18, bf16[512,384]{1,0:T(8,128)(2,1)} %copy-done.19, ...), custom_call_target="tpu_custom_call" | custom-call | tf_op jit(solution)/shard_map/attend/pallas_call | solution.py:545
  207.7 3.0 %collective-permute-done.28 = bf16[512,128]{1,0:T(8,128)(2,1)S(1)} collective-permute-done((bf16[512,128]{1,0:T(8,128)(2,1)}, bf16[512,128]{1,0:T(8,128)(2,1)S(1)}, u32[]{:S(2)}, u32[]{:S(2)}) %collective-permute-start.28) | collective-permute-done | bytes 131104 | tf_op jit(solution)/shard_map/ppermute | solution.py:262
  211.6 32.9 %collective-permute-start.29 = (bf16[128,512]{1,0:T(8,128)(2,1)S(1)}, bf16[128,512]{1,0:T(8,128)(2,1)S(1)}, u32[]{:S(2)}, u32[]{:S(2)}) collective-permute-start(bf16[128,512]{1,0:T(8,128)(2,1)S(1)} %get-tuple-element.68), channel_id=1, source_target_pairs={{0,1},{1,0},{2,3},{3,2},{4,5},{5,4},{6,7},{7,6},{8,9},{9,8},{10,11... | collective-permute-start | bytes 393224 | tf_op jit(solution)/shard_map/ppermute | solution.py:262
  247.1 3.2 %collective-permute-done.29 = bf16[128,512]{1,0:T(8,128)(2,1)S(1)} collective-permute-done((bf16[128,512]{1,0:T(8,128)(2,1)S(1)}, bf16[128,512]{1,0:T(8,128)(2,1)S(1)}, u32[]{:S(2)}, u32[]{:S(2)}) %collective-permute-start.29) | collective-permute-done | bytes 131104 | tf_op jit(solution)/shard_map/ppermute | solution.py:262
  250.4 4.3 %collective-permute-done.30 = bf16[128,512]{1,0:T(8,128)(2,1)S(1)} collective-permute-done((bf16[128,512]{1,0:T(8,128)(2,1)S(1)}, bf16[128,512]{1,0:T(8,128)(2,1)S(1)}, u32[]{:S(2)}, u32[]{:S(2)}) %collective-permute-start.30) | collective-permute-done | bytes 131104 | tf_op jit(solution)/shard_map/ppermute | solution.py:262
  256.9 7.3 %collective-permute-done.38.refs_4_ = bf16[512,512]{1,0:T(8,128)(2,1)S(1)} collective-permute-done((bf16[512,512]{1,0:T(8,128)(2,1)}, bf16[512,512]{1,0:T(8,128)(2,1)S(1)}, u32[]{:S(2)}, u32[]{:S(2)}) %collective-permute-start.38) | collective-permute-done | bytes 524320 | tf_op jit(solution)/shard_map/ppermute | solution.py:262
  264.2 5.2 %collective-permute-done.39.refs_5_ = bf16[512,512]{1,0:T(8,128)(2,1)S(1)} collective-permute-done((bf16[512,512]{1,0:T(8,128)(2,1)S(1)}, bf16[512,512]{1,0:T(8,128)(2,1)S(1)}, u32[]{:S(2)}, u32[]{:S(2)}) %collective-permute-start.39) | collective-permute-done | bytes 524320 | tf_op jit(solution)/shard_map/ppermute | solution.py:262
  271.0 6.6 %collective-permute-done.43.refs_8_ = bf16[512,512]{1,0:T(8,128)(2,1)S(1)} collective-permute-done((bf16[512,512]{1,0:T(8,128)(2,1)S(1)}, bf16[512,512]{1,0:T(8,128)(2,1)S(1)}, u32[]{:S(2)}, u32[]{:S(2)}) %collective-permute-start.43) | collective-permute-done | bytes 524320 | tf_op jit(solution)/shard_map/ppermute | solution.py:262
  279.2 8.9 %out_branch.1 = (f32[128,4096]{1,0:T(8,128)}, bf16[128,2048]{1,0:T(8,128)(2,1)}) custom-call(s32[27]{0:T(128)} %get-tuple-element.74.where_ref, bf16[128,2048]{1,0:T(8,128)(2,1)} %copy-done.6, bf16[128,2048]{1,0:T(8,128)(2,1)} %copy-done.16, f32[128,2048]{1,0:T(8,128)} %get-tuple-element.48.rows_ref, bf16[512,4096]{1,0:T(8,128)(2,1)} %home_ref.3, ...), custom_call_target="tpu_custom_call" | custom-call | tf_op jit(solution)/shard_map/out_branch/pallas_call | solution.py:607
  (197 shorter events, 83.6 us)
Async XLA Ops:
  0.7 22.4 %collective-permute-start = (f32[1,128]{1,0:T(1,128)S(1)}, f32[1,128]{1,0:T(1,128)S(1)}, u32[]{:S(2)}, u32[]{:S(2)}) collective-permute-start(f32[1,128]{1,0:T(1,128)S(1)} %convert_bitcast_fusion.1), channel_id=1, source_target_pairs={{0,4},{4,0},{8,12},{12,8},{1,5},{5,1},{9,13},{13,9},{2,6},{6,2},{1... | collective-permute-start | bytes 1544 | tf_op jit(solution)/shard_map/ppermute | solution.py:262
  3.6 19.4 %collective-permute-start.1 = (f32[1,128]{1,0:T(1,128)S(1)}, f32[1,128]{1,0:T(1,128)S(1)}, u32[]{:S(2)}, u32[]{:S(2)}) collective-permute-start(f32[1,128]{1,0:T(1,128)S(1)} %convert_bitcast_fusion.1), channel_id=1, source_target_pairs={{0,8},{4,12},{8,0},{12,4},{1,9},{5,13},{9,1},{13,5},{2,10},{6,14},... | collective-permute-start | bytes 1544 | tf_op jit(solution)/shard_map/ppermute | solution.py:262
  6.2 41.7 %collective-permute-start.12 = (bf16[512,512]{1,0:T(8,128)(2,1)S(1)}, bf16[512,512]{1,0:T(8,128)(2,1)}, u32[]{:S(2)}, u32[]{:S(2)}) collective-permute-start(bf16[512,512]{1,0:T(8,128)(2,1)S(1)} %constant_dynamic-slice_fusion.1), channel_id=1, source_target_pairs={{1,2},{2,1},{5,6},{6,5},{9,10},{10,9},{13,14},{14,13},{17,18},{18,... | collective-permute-start | bytes 1572872 | tf_op jit(solution)/shard_map/ppermute | solution.py:273
  7.7 37.2 %collective-permute-start.7 = (bf16[512,512]{1,0:T(8,128)(2,1)S(1)}, bf16[512,512]{1,0:T(8,128)(2,1)}, u32[]{:S(2)}, u32[]{:S(2)}) collective-permute-start(bf16[512,512]{1,0:T(8,128)(2,1)S(1)} %constant_dynamic-slice_fusion.1), channel_id=1, source_target_pairs={{0,1},{1,0},{2,3},{3,2},{4,5},{5,4},{6,7},{7,6},{8,9},{9,8},{10,11... | collective-permute-start | bytes 1572872 | tf_op jit(solution)/shard_map/ppermute | solution.py:262
  44.9 58.4 %collective-permute-start.6 = (bf16[512,2048]{1,0:T(8,128)(2,1)}, bf16[512,2048]{1,0:T(8,128)(2,1)S(1)}, u32[]{:S(2)}, u32[]{:S(2)}) collective-permute-start(bf16[512,2048]{1,0:T(8,128)(2,1)} %hyena_mix.1.own0.own1.own2.own3), channel_id=1, source_target_pairs={{0,16},{16,0},{1,17},{17,1},{2,18},{18,2},{3,19},{19,3},{4,20},{20... | collective-permute-start | bytes 6291464 | tf_op jit(solution)/shard_map/ppermute | solution.py:262
  49.2 18.4 %collective-permute-start.8 = (bf16[512,512]{1,0:T(8,128)(2,1)}, bf16[512,512]{1,0:T(8,128)(2,1)S(1)}, u32[]{:S(2)}, u32[]{:S(2)}) collective-permute-start(bf16[512,512]{1,0:T(8,128)(2,1)} %collective-permute-done.7.refs_0_), channel_id=1, source_target_pairs={{0,4},{4,0},{8,12},{12,8},{1,5},{5,1},{9,13},{13,9},{2,6},{6,2},{1... | collective-permute-start | bytes 1572872 | tf_op jit(solution)/shard_map/ppermute | solution.py:262
  50.8 24.6 %collective-permute-start.18 = (bf16[512,512]{1,0:T(8,128)(2,1)}, bf16[512,512]{1,0:T(8,128)(2,1)}, u32[]{:S(2)}, u32[]{:S(2)}) collective-permute-start(bf16[512,512]{1,0:T(8,128)(2,1)} %collective-permute-done.17), channel_id=1, source_target_pairs={{1,0},{2,3},{5,4},{6,7},{9,8},{10,11},{13,12},{14,15},{17,16},{18,... | collective-permute-start | bytes 1572872 | tf_op jit(solution)/shard_map/ppermute | solution.py:276
  66.0 31.1 %collective-permute-start.14 = (bf16[512,512]{1,0:T(8,128)(2,1)S(1)}, bf16[512,512]{1,0:T(8,128)(2,1)}, u32[]{:S(2)}, u32[]{:S(2)}) collective-permute-start(bf16[512,512]{1,0:T(8,128)(2,1)S(1)} %broadcast_select_fusion.3.refs_5_), channel_id=1, source_target_pairs={{0,4},{4,0},{8,12},{12,8},{1,5},{5,1},{9,13},{13,9},{2,6},{6,2},{1... | collective-permute-start | bytes 1572872 | tf_op jit(solution)/shard_map/ppermute | solution.py:262
  67.6 30.1 %collective-permute-start.15 = (bf16[512,512]{1,0:T(8,128)(2,1)S(1)}, bf16[512,512]{1,0:T(8,128)(2,1)}, u32[]{:S(2)}, u32[]{:S(2)}) collective-permute-start(bf16[512,512]{1,0:T(8,128)(2,1)S(1)} %broadcast_select_fusion.3.refs_5_), channel_id=1, source_target_pairs={{0,8},{4,12},{8,0},{12,4},{1,9},{5,13},{9,1},{13,5},{2,10},{6,14},... | collective-permute-start | bytes 1572872 | tf_op jit(solution)/shard_map/ppermute | solution.py:262
  70.2 32.8 %collective-permute-start.16 = (bf16[512,512]{1,0:T(8,128)(2,1)S(1)}, bf16[512,512]{1,0:T(8,128)(2,1)}, u32[]{:S(2)}, u32[]{:S(2)}) collective-permute-start(bf16[512,512]{1,0:T(8,128)(2,1)S(1)} %broadcast_select_fusion.3.refs_5_), channel_id=1, source_target_pairs={{0,12},{4,8},{8,4},{12,0},{1,13},{5,9},{9,5},{13,1},{2,14},{6,10},... | collective-permute-start | bytes 1572872 | tf_op jit(solution)/shard_map/ppermute | solution.py:262
  75.4 21.2 %collective-permute-start.11 = (bf16[256,512]{1,0:T(8,128)(2,1)S(1)}, bf16[256,512]{1,0:T(8,128)(2,1)S(1)}, u32[]{:S(2)}, u32[]{:S(2)}) collective-permute-start(bf16[256,512]{1,0:T(8,128)(2,1)S(1)} %slice.110), channel_id=1, source_target_pairs={{0,8},{4,12},{8,0},{12,4},{1,9},{5,13},{9,1},{13,5},{2,10},{6,14},... | collective-permute-start | bytes 786440 | tf_op jit(solution)/shard_map/ppermute | solution.py:262
  96.6 21.2 %collective-permute-start.19 = (bf16[512,512]{1,0:T(8,128)(2,1)}, bf16[512,512]{1,0:T(8,128)(2,1)}, u32[]{:S(2)}, u32[]{:S(2)}) collective-permute-start(bf16[512,512]{1,0:T(8,128)(2,1)} %broadcast_select_fusion.2.refs_0_), channel_id=1, source_target_pairs={{0,4},{4,0},{8,12},{12,8},{1,5},{5,1},{9,13},{13,9},{2,6},{6,2},{1... | collective-permute-start | bytes 1572872 | tf_op jit(solution)/shard_map/ppermute | solution.py:262
  97.2 23.8 %collective-permute-start.20 = (bf16[512,512]{1,0:T(8,128)(2,1)}, bf16[512,512]{1,0:T(8,128)(2,1)}, u32[]{:S(2)}, u32[]{:S(2)}) collective-permute-start(bf16[512,512]{1,0:T(8,128)(2,1)} %broadcast_select_fusion.2.refs_0_), channel_id=1, source_target_pairs={{0,8},{4,12},{8,0},{12,4},{1,9},{5,13},{9,1},{13,5},{2,10},{6,14},... | collective-permute-start | bytes 1572872 | tf_op jit(solution)/shard_map/ppermute | solution.py:262
  97.7 23.3 %collective-permute-start.21 = (bf16[512,512]{1,0:T(8,128)(2,1)}, bf16[512,512]{1,0:T(8,128)(2,1)}, u32[]{:S(2)}, u32[]{:S(2)}) collective-permute-start(bf16[512,512]{1,0:T(8,128)(2,1)} %broadcast_select_fusion.2.refs_0_), channel_id=1, source_target_pairs={{0,12},{4,8},{8,4},{12,0},{1,13},{5,9},{9,5},{13,1},{2,14},{6,10},... | collective-permute-start | bytes 1572872 | tf_op jit(solution)/shard_map/ppermute | solution.py:262
  103.0 27.6 %collective-permute-start.33 = (bf16[512,1024]{1,0:T(8,128)(2,1)}, bf16[512,1024]{1,0:T(8,128)(2,1)S(1)}, u32[]{:S(2)}, u32[]{:S(2)}) collective-permute-start(bf16[512,1024]{1,0:T(8,128)(2,1)} %constant_dynamic-slice_fusion), channel_id=1, source_target_pairs={{0,1},{1,0},{2,3},{3,2},{4,5},{5,4},{6,7},{7,6},{8,9},{9,8},{10,11... | collective-permute-start | bytes 3145736 | tf_op jit(solution)/shard_map/ppermute | solution.py:262
  132.3 49.7 %collective-permute-start.37 = (bf16[512,1024]{1,0:T(8,128)(2,1)}, bf16[512,1024]{1,0:T(8,128)(2,1)}, u32[]{:S(2)}, u32[]{:S(2)}) collective-permute-start(bf16[512,1024]{1,0:T(8,128)(2,1)} %collective-permute-done.36), channel_id=1, source_target_pairs={{1,0},{2,3},{5,4},{6,7},{9,8},{10,11},{13,12},{14,15},{17,16},{18,... | collective-permute-start | bytes 3145736 | tf_op jit(solution)/shard_map/ppermute | solution.py:275
  133.6 70.9 %collective-permute-start.41 = (bf16[512,1024]{1,0:T(8,128)(2,1)}, bf16[512,1024]{1,0:T(8,128)(2,1)}, u32[]{:S(2)}, u32[]{:S(2)}) collective-permute-start(bf16[512,1024]{1,0:T(8,128)(2,1)} %collective-permute-done.40), channel_id=1, source_target_pairs={{1,0},{2,3},{5,4},{6,7},{9,8},{10,11},{13,12},{14,15},{17,16},{18,... | collective-permute-start | bytes 3145736 | tf_op jit(solution)/shard_map/ppermute | solution.py:276
  136.2 120.2 %collective-permute-start.34 = (bf16[512,512]{1,0:T(8,128)(2,1)}, bf16[512,512]{1,0:T(8,128)(2,1)}, u32[]{:S(2)}, u32[]{:S(2)}) collective-permute-start(bf16[512,512]{1,0:T(8,128)(2,1)} %get-tuple-element.64), channel_id=1, source_target_pairs={{0,4},{4,0},{8,12},{12,8},{1,5},{5,1},{9,13},{13,9},{2,6},{6,2},{1... | collective-permute-start | bytes 1572872 | tf_op jit(solution)/shard_map/ppermute | solution.py:262
  158.5 27.8 %collective-permute-start.23 = (bf16[512,384]{1,0:T(8,128)(2,1)}, bf16[512,384]{1,0:T(8,128)(2,1)S(1)}, u32[]{:S(2)}, u32[]{:S(2)}) collective-permute-start(bf16[512,384]{1,0:T(8,128)(2,1)} %get-tuple-element.41), channel_id=1, source_target_pairs={{0,4},{4,0},{8,12},{12,8},{1,5},{5,1},{9,13},{13,9},{2,6},{6,2},{1... | collective-permute-start | bytes 1179656 | tf_op jit(solution)/shard_map/ppermute | solution.py:262
  160.0 26.7 %collective-permute-start.24 = (bf16[512,384]{1,0:T(8,128)(2,1)}, bf16[512,384]{1,0:T(8,128)(2,1)S(1)}, u32[]{:S(2)}, u32[]{:S(2)}) collective-permute-start(bf16[512,384]{1,0:T(8,128)(2,1)} %get-tuple-element.42), channel_id=1, source_target_pairs={{0,8},{4,12},{8,0},{12,4},{1,9},{5,13},{9,1},{13,5},{2,10},{6,14},... | collective-permute-start | bytes 1179656 | tf_op jit(solution)/shard_map/ppermute | solution.py:262
  186.3 70.6 %collective-permute-start.35 = (bf16[512,512]{1,0:T(8,128)(2,1)}, bf16[512,512]{1,0:T(8,128)(2,1)S(1)}, u32[]{:S(2)}, u32[]{:S(2)}) collective-permute-start(bf16[512,512]{1,0:T(8,128)(2,1)} %get-tuple-element.63), channel_id=1, source_target_pairs={{0,8},{4,12},{8,0},{12,4},{1,9},{5,13},{9,1},{13,5},{2,10},{6,14},... | collective-permute-start | bytes 1572872 | tf_op jit(solution)/shard_map/ppermute | solution.py:262
  211.6 38.7 %collective-permute-start.29 = (bf16[128,512]{1,0:T(8,128)(2,1)S(1)}, bf16[128,512]{1,0:T(8,128)(2,1)S(1)}, u32[]{:S(2)}, u32[]{:S(2)}) collective-permute-start(bf16[128,512]{1,0:T(8,128)(2,1)S(1)} %get-tuple-element.68), channel_id=1, source_target_pairs={{0,1},{1,0},{2,3},{3,2},{4,5},{5,4},{6,7},{7,6},{8,9},{9,8},{10,11... | collective-permute-start | bytes 393224 | tf_op jit(solution)/shard_map/ppermute | solution.py:262
  256.4 21.2 %collective-permute-start.43 = (bf16[512,512]{1,0:T(8,128)(2,1)S(1)}, bf16[512,512]{1,0:T(8,128)(2,1)S(1)}, u32[]{:S(2)}, u32[]{:S(2)}) collective-permute-start(bf16[512,512]{1,0:T(8,128)(2,1)S(1)} %get-tuple-element.59), channel_id=1, source_target_pairs={{0,8},{4,12},{8,0},{12,4},{1,9},{5,13},{9,1},{13,5},{2,10},{6,14},... | collective-permute-start | bytes 1572872 | tf_op jit(solution)/shard_map/ppermute | solution.py:262
  256.9 20.7 %collective-permute-start.32 = (bf16[128,2048]{1,0:T(8,128)(2,1)S(1)}, bf16[128,2048]{1,0:T(8,128)(2,1)S(1)}, u32[]{:S(2)}, u32[]{:S(2)}) collective-permute-start(bf16[128,2048]{1,0:T(8,128)(2,1)S(1)} %pad_maximum_fusion.2.own_ref), channel_id=1, source_target_pairs={{0,16},{16,0},{1,17},{17,1},{2,18},{18,2},{3,19},{19,3},{4,20},{20... | collective-permute-start | bytes 1572872 | tf_op jit(solution)/shard_map/ppermute | solution.py:262
  (49 other events, 631.6 us)
